TPU v7x, 128 devices: a whole 4x4x4 slice. The times are simulated.
128 devices in a mesh: row: 16 (over z, x), vec: 8 (over y, core).
Axes of the slice: x: 4, y: 4, z: 4, core: 2. Of those that a mesh axis runs over, the one named last changes fastest.
Arguments:
- vectors: float32 [32768, 1024], P('row', 'vec'), may hold values from -8 to 8
- hamiltonian: float32 [256, 12, 128, 128], P('row'), may hold values from -0.15 to 0.15, as said below
- column_blocks: int32 [256, 12], P('row'), may hold values from 0 to 255, as said below
- live_counts: int32 [256], P('row'), may hold values from 3 to 12
- lower_bound: float32 [1], replicated, may hold values from -0.85 to -0.65
- upper_bound: float32 [1], replicated, may hold values from 1.05 to 1.3
Outputs:
- filtered: float32 [32768, 1024], P('row', 'vec')
Inputs may be any that keep to these rules, and one draw needn't show every extreme that they name: column_blocks[i, 0] = i, and every entry lies within 16 block rows of its row i, cyclically modulo 256; the distances 16 and -16 both occur. `hamiltonian`: H is symmetric: for every used slot of block row i that names column block j there is a used slot of block row j that names i and holds the transpose of its block, and slot 0 of every block row holds a symmetric block.
All inputs are finite; a program needn't handle non-finite values.
Results may differ from a plain program's by a relative error of at most 0.0003.
Values sent between devices are 32-bit elements; how exact they have to be, the bound alone decides.
No kernel may reach another device: no remote copies, remote signals or barrier semaphores. Data moves between devices by JAX's collectives and lax.ppermute only.
A program may use at most 128 MiB of HBM per device.

v0:
```python
import functools
import math

import jax
import jax.numpy as jnp
from jax import lax
from jax.experimental import pallas as pl
from jax.experimental.pallas import tpu as pltpu
from jax.sharding import PartitionSpec as P

NV = 1024
BF = jnp.bfloat16
F32 = jnp.float32
VMEM_LIMIT = 56 * 1024 * 1024


def split(x):
    high = x.astype(BF)
    return high, (x - high.astype(F32)).astype(BF)


def fold(full):
    rows, cols = full.shape[0] // 2, full.shape[1] // 2
    return (full[:rows, :cols] + full[rows:, :cols]) + (full[:rows, cols:] + full[rows:, cols:])


def mm(a, b):
    return jnp.dot(a, b, preferred_element_type=F32)


def cost(flops, moved):
    return pl.CostEstimate(flops=flops, bytes_accessed=moved, transcendentals=0)


def split_kernel(h_ref, o_ref):
    high, low = split(h_ref[0])
    o_ref[0, :, :128, :] = high
    o_ref[0, :, 128:, :] = low


def split_blocks(hamiltonian):
    block_rows, slots, size, _ = hamiltonian.shape
    return pl.pallas_call(
        split_kernel,
        out_shape=jax.ShapeDtypeStruct((block_rows, slots, 2 * size, size), BF),
        grid=(block_rows,),
        in_specs=[pl.BlockSpec((1, slots, size, size), lambda i: (i, 0, 0, 0))],
        out_specs=pl.BlockSpec((1, slots, 2 * size, size), lambda i: (i, 0, 0, 0)),
        compiler_params=pltpu.CompilerParams(vmem_limit_bytes=VMEM_LIMIT),
        cost_estimate=cost(0, 8 * block_rows * slots * size * size),
        name="split_blocks",
    )(hamiltonian)


def field_kernel(slots, second, cols_ref, coef_ref, h_ref, left_ref, own_ref, right_ref, *rest):
    if second:
        prev_ref, o_ref, wide = rest
    else:
        o_ref, wide = rest
    i = pl.program_id(0)
    count = own_ref.shape[0]

    @pl.when(i == 0)
    def _():
        for part, ref in enumerate((left_ref, own_ref, right_ref)):

            @pl.loop(0, count)
            def _(j):
                high, low = split(ref[j])
                wide[part * count + j, :, :128] = high
                wide[part * count + j, :, 128:] = low

        wide[3 * count] = jnp.zeros(wide.shape[1:], BF)

    lhs = jnp.concatenate([h_ref[0, k] for k in range(slots)], axis=1)
    rhs = jnp.concatenate([wide[cols_ref[i * slots + k]] for k in range(slots)], axis=0)
    summed = fold(mm(lhs, rhs))
    centre, inverse = coef_ref[0], coef_ref[1]
    result = (summed - centre * own_ref[i]) * inverse
    if second:
        result = 2.0 * result - prev_ref[i]
    o_ref[0] = result


def apply_field(second, cols, coef, split_h, left, own, right, prev=None):
    block_rows, slots, double, size = split_h.shape
    whole = pl.BlockSpec((block_rows, size, size), lambda i, *_: (0, 0, 0))
    operands = [split_h, left, own, right] + ([prev] if second else [])
    return pl.pallas_call(
        functools.partial(field_kernel, slots, second),
        out_shape=jax.ShapeDtypeStruct((block_rows, size, size), F32),
        grid_spec=pltpu.PrefetchScalarGridSpec(
            num_scalar_prefetch=2,
            grid=(block_rows,),
            in_specs=[pl.BlockSpec((1, slots, double, size), lambda i, *_: (i, 0, 0, 0))]
            + [whole] * (len(operands) - 1),
            out_specs=pl.BlockSpec((1, size, size), lambda i, *_: (i, 0, 0)),
            scratch_shapes=[pltpu.VMEM((3 * block_rows + 1, size, 2 * size), BF)],
        ),
        compiler_params=pltpu.CompilerParams(vmem_limit_bytes=VMEM_LIMIT),
        cost_estimate=cost(8 * block_rows * slots * size**3, 2 * split_h.size),
        name="field",
    )(cols, coef, *operands)


GRAM_BLOCKS = 5


def gram_kernel(y_ref, own_ref, s_ref, u_ref, us_ref, o_ref, os_ref, out_ref, acc):
    step = pl.program_id(0)

    @pl.when(step == 0)
    def _():
        acc[...] = jnp.zeros_like(acc)

    lhs = jnp.concatenate(split(own_ref[...].T), axis=0)

    def add(block, ref):
        acc[block] += mm(lhs, jnp.concatenate(split(ref[...]), axis=1))

    for block, ref in enumerate((own_ref, s_ref, u_ref, us_ref)):
        add(block, ref)

    @pl.when(y_ref[0] < 2)
    def _():
        add(4, o_ref)

    @pl.when(y_ref[0] >= 2)
    def _():
        add(4, os_ref)

    @pl.when(step == pl.num_programs(0) - 1)
    def _():
        for block in range(GRAM_BLOCKS):
            out_ref[:, block * 128 : (block + 1) * 128] = fold(acc[block])


def gram_share(y, pieces):
    rows, cols = pieces[0].shape
    chunk = 512
    return pl.pallas_call(
        gram_kernel,
        out_shape=jax.ShapeDtypeStruct((cols, GRAM_BLOCKS * cols), F32),
        grid_spec=pltpu.PrefetchScalarGridSpec(
            num_scalar_prefetch=1,
            grid=(rows // chunk,),
            in_specs=[pl.BlockSpec((chunk, cols), lambda i, *_: (i, 0))] * len(pieces),
            out_specs=pl.BlockSpec((cols, GRAM_BLOCKS * cols), lambda i, *_: (0, 0)),
            scratch_shapes=[pltpu.VMEM((GRAM_BLOCKS, 2 * cols, 2 * cols), F32)],
        ),
        compiler_params=pltpu.CompilerParams(vmem_limit_bytes=VMEM_LIMIT),
        cost_estimate=cost(8 * rows * cols * cols * GRAM_BLOCKS, 4 * rows * cols * len(pieces)),
        name="gram_share",
    )(y, *pieces)


KEEP = {0: 1, 3: 2, 4: 1, 8: 1}
BASE = {2: 1, 6: 1, 10: 1, 11: 2}
PIECES = ((0, 0), (1, 0), (0, 1), (1, 1), (0, 3), (1, 3), (0, 2), (1, 2))


def finish_kernel(total_rows, y_ref, ga_ref, gb_ref, *rest):
    x_refs = rest[: len(PIECES)]
    out_ref, gram, gram_low, state, factor = rest[len(PIECES) :]
    grams = (ga_ref, gb_ref)
    y = y_ref[0]

    @pl.when(pl.program_id(0) == 0)
    def _():
        diagonal = lax.broadcasted_iota(jnp.int32, (128, 128), 0) == lax.broadcasted_iota(
            jnp.int32, (128, 128), 1
        )

        def block(k, row, b):
            return grams[k][:, row, :, b * 128 : (b + 1) * 128].reshape(128, 128)

        trace = jnp.zeros((128, 128), F32)
        for k in range(2):
            for row in range(4):
                trace += jnp.where(diagonal, block(k, row, 0), 0.0)
        energy = jnp.sum(jnp.sum(trace, axis=0, keepdims=True), axis=1, keepdims=True)
        square = NV / (4 * (energy + 1e-06))

        def put(at_row, at_col, value):
            high, low = split(value)
            rows, cols = slice(at_row * 128, at_row * 128 + 128), slice(at_col * 128, at_col * 128 + 128)
            gram[rows, cols] = high
            gram_low[rows, cols] = low

        for k in range(2):
            for row in range(4):
                here = 4 * k + row
                after, across = (row + 1) % 4, (row + 2) % 4
                side = k if row < 2 else 1 - k
                put(here, here, block(k, row, 0) * square)
                put(here, 4 * (1 - k) + row, block(k, row, 1) * square)
                for there, b in ((4 * k + after, 2), (4 * (1 - k) + after, 3), (4 * side + across, 4)):
                    value = block(k, row, b) * square
                    put(here, there, value)
                    put(there, here, value.T)

        mine = pl.ds(pl.multiple_of(y * 128, 128), 128)
        column = lax.broadcasted_iota(jnp.int32, (128, NV), 1) - y * 128
        unit = (column == lax.broadcasted_iota(jnp.int32, (128, NV), 0)).astype(F32)
        state[0] = 1.5 * unit - 0.5 * (gram[mine, :].astype(F32) + gram_low[mine, :].astype(F32))

        @pl.loop(0, 12)
        def _(step):
            current = state[0]
            for at, slot in KEEP.items():

                @pl.when(step == at)
                def _():
                    state[slot] = current

            slot = jnp.int32(0)
            for at, value in BASE.items():
                slot = jnp.where(step == at, value, slot)
            high, low = split(current)
            twice = mm(jnp.concatenate([high, low], axis=0), gram[...])
            product = (twice[:128] + twice[128:]) + mm(high, gram_low[...])
            state[0] = 1.5 * state[slot] - 0.5 * product

        scale = jnp.sqrt(square) * math.sqrt(total_rows)
        high, low = split(state[0].T * scale)
        factor[:, :128] = high
        factor[:, 128:] = low

    lhs = jnp.concatenate([ref[...] for ref in x_refs], axis=1)
    rhs = jnp.concatenate(
        [
            factor[pl.ds(pl.multiple_of((4 * k + lax.rem(y + dy, 4)) * 128, 128), 128), :]
            for k, dy in PIECES
        ],
        axis=0,
    )
    out_ref[...] = fold(mm(jnp.concatenate(split(lhs), axis=0), rhs))


def finish(total_rows, y, gram_a, gram_b, pieces):
    rows, cols = pieces[0].shape
    chunk = 256
    whole = pl.BlockSpec(gram_a.shape, lambda i, *_: (0, 0, 0, 0))
    part = pl.BlockSpec((chunk, cols), lambda i, *_: (i, 0))
    return pl.pallas_call(
        functools.partial(finish_kernel, total_rows),
        out_shape=jax.ShapeDtypeStruct((rows, cols), F32),
        grid_spec=pltpu.PrefetchScalarGridSpec(
            num_scalar_prefetch=1,
            grid=(rows // chunk,),
            in_specs=[whole, whole] + [part] * len(pieces),
            out_specs=part,
            scratch_shapes=[
                pltpu.VMEM((NV, NV), BF),
                pltpu.VMEM((NV, NV), BF),
                pltpu.VMEM((3, cols, NV), F32),
                pltpu.VMEM((NV, 2 * cols), BF),
            ],
        ),
        compiler_params=pltpu.CompilerParams(vmem_limit_bytes=VMEM_LIMIT),
        cost_estimate=cost(12 * 6 * cols * NV * NV, 4 * rows * cols * 9),
        name="finish",
    )(y, gram_a, gram_b, *pieces)


def on_device(vectors, hamiltonian, column_blocks, live_counts, lower_bound, upper_bound):
    rows_dev, panel_cols = vectors.shape
    block_rows, slot_count, block_size, unused_size = hamiltonian.shape
    row_count, vec_count = lax.axis_size("row"), lax.axis_size("vec")
    first_row = lax.axis_index("row") * block_rows
    local = (column_blocks - first_row + block_rows) % (block_rows * row_count)
    live = jnp.arange(slot_count, dtype=jnp.int32)[None, :] < live_counts[:, None]
    cols = jnp.where(live, jnp.minimum(local, 3 * block_rows - 1), 3 * block_rows).reshape(-1)
    centre = (upper_bound[0] + lower_bound[0]) / 2
    radius = (upper_bound[0] - lower_bound[0]) / 2
    coef = jnp.stack([centre, 1.0 / radius])
    y = (lax.axis_index("vec") // 2)[None].astype(jnp.int32)

    def from_row(value, step):
        return lax.ppermute(value, "row", [((i + step) % row_count, i) for i in range(row_count)])

    def from_y(value, step):
        return lax.ppermute(
            value, "vec", [((i + 2 * step) % vec_count, i) for i in range(vec_count)]
        )

    def swap(value):
        return lax.ppermute(value, "vec", [(i, i ^ 1) for i in range(vec_count)])

    split_h = split_blocks(hamiltonian)
    blocks = vectors.reshape(block_rows, block_size, panel_cols)
    first = apply_field(False, cols, coef, split_h, from_row(blocks, -1), blocks, from_row(blocks, 1))
    second = apply_field(
        True, cols, coef, split_h, from_row(first, -1), first, from_row(first, 1), blocks
    )
    own = second.reshape(rows_dev, panel_cols)

    half = rows_dev // 2
    up, down = from_y(own, 1), from_y(own, -1)
    across = jnp.concatenate([from_y(up[:half], 1), from_y(down[half:], -1)], axis=0)
    pieces = (own, swap(own), up, swap(up), down, swap(down), across, swap(across))

    share = gram_share(y, pieces[:4] + pieces[6:])
    strip = share.shape[0] // row_count
    parts = lax.all_to_all(
        share.reshape(row_count, strip, -1), "row", split_axis=0, concat_axis=0, tiled=True
    )
    part = jnp.sum(parts, axis=0)
    groups = [
        [r * vec_count + v for r in range(row_count) for v in range(core, vec_count, 2)]
        for core in range(2)
    ]
    members = row_count * vec_count // 2
    gram_a = lax.all_to_all(
        jnp.broadcast_to(part[None], (members,) + part.shape),
        ("row", "vec"),
        split_axis=0,
        concat_axis=0,
        tiled=True,
        axis_index_groups=groups,
    ).reshape(row_count, vec_count // 2, strip, -1)
    gram_b = swap(gram_a)
    return finish(rows_dev * row_count, y, gram_a, gram_b, pieces)


def solution(mesh):
    placed = (P("row", "vec"), P("row", None, None, None), P("row", None), P("row"), P(), P())
    return jax.shard_map(
        on_device, mesh=mesh, in_specs=placed, out_specs=P("row", "vec"), check_vma=False
    )
```

profile of v0, /device:TPU:1, one launch (start us, length us, event | category | flops | bytes accessed | tf_op | source)
XLA Modules:
  0.0 216.7 jit_solution(8825139255870497994)
XLA Ops:
  0.0 6.8 %collective-permute-start.1 = (f32[16,128,128]{2,1,0:T(8,128)}, f32[16,128,128]{2,1,0:T(8,128)S(1)}, u32[]{:S(2)}, u32[]{:S(2)}) collective-permute-start(f32[16,128,128]{2,1,0:T(8,128)} %bitcast.5), channel_id=1, source_target_pairs={{8,0},{16,8},{24,16},{32,24},{40,32},{48,40},{56,48},{64,56},{72,6... | collective-permute-start | bytes 3145736 | tf_op jit(solution)/shard_map/ppermute | solution.py:280
  6.8 0.0 collective-permute-start
  8.1 0.8 fusion.2
  8.8 0.7 reshape.27.cols_ref
  9.5 15.6 %split_blocks.1.h_ref = bf16[16,12,256,128]{3,2,1,0:T(8,128)(2,1)} custom-call(f32[16,12,128,128]{3,2,1,0:T(8,128)} %h_ref.1), custom_call_target="tpu_custom_call" | custom-call | bytes 25165824 | tf_op jit(solution)/shard_map/split_blocks/pallas_call | solution.py:43
  25.2 0.6 pad_maximum_fusion.coef_ref
  25.8 3.1 %collective-permute-done.1.right_ref = f32[16,128,128]{2,1,0:T(8,128)S(1)} collective-permute-done((f32[16,128,128]{2,1,0:T(8,128)}, f32[16,128,128]{2,1,0:T(8,128)S(1)}, u32[]{:S(2)}, u32[]{:S(2)}) %collective-permute-start.1) | collective-permute-done | bytes 1048608 | tf_op jit(solution)/shard_map/ppermute | solution.py:280
  28.9 5.1 %collective-permute-done.left_ref = f32[16,128,128]{2,1,0:T(8,128)S(1)} collective-permute-done((f32[16,128,128]{2,1,0:T(8,128)}, f32[16,128,128]{2,1,0:T(8,128)S(1)}, u32[]{:S(2)}, u32[]{:S(2)}) %collective-permute-start) | collective-permute-done | bytes 1048608 | tf_op jit(solution)/shard_map/ppermute | solution.py:280
  34.1 0.0 copy-done.4
  34.1 1.0 copy-done.5
  35.0 16.3 %field.2.own_ref = f32[16,128,128]{2,1,0:T(8,128)} custom-call(s32[192]{0:T(256)} %reshape.27.cols_ref, f32[2]{0:T(128)} %pad_maximum_fusion.coef_ref, bf16[16,12,256,128]{3,2,1,0:T(8,128)(2,1)} %split_blocks.1.h_ref, f32[16,128,128]{2,1,0:T(8,128)} %copy-done.5, f32[16,128,128]{2,1,0:T(8,128)} %bitcast.7, f32[16,128,128]{2,1,0:T(8,128)} %copy-done.4), custom_call_target="tpu_custom_call" | custom-call | flops 3221225472 | bytes 12582912 | tf_op jit(solution)/shard_map/field/pallas_call | solution.py:89
  51.4 1.3 collective-permute-start.3
  52.7 0.2 collective-permute-start.2
  52.9 21.7 %collective-permute-done.3.right_ref = f32[16,128,128]{2,1,0:T(8,128)S(1)} collective-permute-done((f32[16,128,128]{2,1,0:T(8,128)}, f32[16,128,128]{2,1,0:T(8,128)S(1)}, u32[]{:S(2)}, u32[]{:S(2)}) %collective-permute-start.3) | collective-permute-done | bytes 1048608 | tf_op jit(solution)/shard_map/ppermute | solution.py:280
  74.5 4.6 %collective-permute-done.2.left_ref = f32[16,128,128]{2,1,0:T(8,128)S(1)} collective-permute-done((f32[16,128,128]{2,1,0:T(8,128)}, f32[16,128,128]{2,1,0:T(8,128)S(1)}, u32[]{:S(2)}, u32[]{:S(2)}) %collective-permute-start.2) | collective-permute-done | bytes 1048608 | tf_op jit(solution)/shard_map/ppermute | solution.py:280
  79.1 0.0 copy-done.6
  79.1 1.0 copy-done.7
  80.1 16.7 %field.3 = f32[16,128,128]{2,1,0:T(8,128)} custom-call(s32[192]{0:T(256)} %reshape.27.cols_ref, f32[2]{0:T(128)} %pad_maximum_fusion.coef_ref, bf16[16,12,256,128]{3,2,1,0:T(8,128)(2,1)} %split_blocks.1.h_ref, f32[16,128,128]{2,1,0:T(8,128)} %copy-done.7, f32[16,128,128]{2,1,0:T(8,128)} %field.2.own_ref, f32[16,128,128]{2,1,0:T(8,128)} %copy-done.6, ...), custom_call_target="tpu_custom_call" | custom-call | flops 3221225472 | bytes 12582912 | tf_op jit(solution)/shard_map/field/pallas_call | solution.py:89
  96.8 2.7 %collective-permute-start.5 = (f32[2048,128]{1,0:T(8,128)}, f32[2048,128]{1,0:T(8,128)S(1)}, u32[]{:S(2)}, u32[]{:S(2)}) collective-permute-start(f32[2048,128]{1,0:T(8,128)} %bitcast.9), channel_id=1, source_target_pairs={{2,0},{3,1},{4,2},{5,3},{6,4},{7,5},{0,6},{1,7},{10,8},{11,9},{12,... | collective-permute-start | bytes 3145736 | tf_op jit(solution)/shard_map/ppermute | solution.py:283
  99.5 0.0 collective-permute-start.8
  99.5 20.1 %collective-permute-done.5.u_ref.rest_2_ = f32[2048,128]{1,0:T(8,128)S(1)} collective-permute-done((f32[2048,128]{1,0:T(8,128)}, f32[2048,128]{1,0:T(8,128)S(1)}, u32[]{:S(2)}, u32[]{:S(2)}) %collective-permute-start.5) | collective-permute-done | bytes 1048608 | tf_op jit(solution)/shard_map/ppermute | solution.py:283
  119.7 3.4 %collective-permute-start.7 = (f32[1024,128]{1,0:T(8,128)S(1)}, f32[1024,128]{1,0:T(8,128)S(1)}, u32[]{:S(2)}, u32[]{:S(2)}) collective-permute-start(f32[1024,128]{1,0:T(8,128)S(1)} %slice.8), channel_id=1, source_target_pairs={{2,0},{3,1},{4,2},{5,3},{6,4},{7,5},{0,6},{1,7},{10,8},{11,9},{12,... | collective-permute-start | bytes 1572872 | tf_op jit(solution)/shard_map/ppermute | solution.py:283
  123.1 0.0 collective-permute-done.8.rest_4_
  123.1 0.1 collective-permute-start.9
  123.2 3.9 %collective-permute-start.4 = (f32[2048,128]{1,0:T(8,128)S(1)}, f32[2048,128]{1,0:T(8,128)}, u32[]{:S(2)}, u32[]{:S(2)}) collective-permute-start(f32[2048,128]{1,0:T(8,128)S(1)} %bitcast.13), channel_id=1, source_target_pairs={{0,1},{1,0},{2,3},{3,2},{4,5},{5,4},{6,7},{7,6},{8,9},{9,8},{10,11... | collective-permute-start | bytes 3145736 | tf_op jit(solution)/shard_map/ppermute | solution.py:288
  127.1 0.1 collective-permute-start.6
  127.2 3.6 %collective-permute-done.7 = f32[1024,128]{1,0:T(8,128)S(1)} collective-permute-done((f32[1024,128]{1,0:T(8,128)S(1)}, f32[1024,128]{1,0:T(8,128)S(1)}, u32[]{:S(2)}, u32[]{:S(2)}) %collective-permute-start.7) | collective-permute-done | bytes 524320 | tf_op jit(solution)/shard_map/ppermute | solution.py:283
  130.9 0.0 copy-done.1
  130.9 3.2 %collective-permute-done.9 = f32[1024,128]{1,0:T(8,128)S(1)} collective-permute-done((f32[1024,128]{1,0:T(8,128)S(1)}, f32[1024,128]{1,0:T(8,128)S(1)}, u32[]{:S(2)}, u32[]{:S(2)}) %collective-permute-start.9) | collective-permute-done | bytes 524320 | tf_op jit(solution)/shard_map/ppermute | solution.py:283
  134.1 0.0 copy-done.8
  134.1 0.0 copy-start.2
  134.1 4.8 %collective-permute-start.10 = (f32[2048,128]{1,0:T(8,128)S(1)}, f32[2048,128]{1,0:T(8,128)}, u32[]{:S(2)}, u32[]{:S(2)}) collective-permute-start(f32[2048,128]{1,0:T(8,128)S(1)} %constant_dynamic-update-slice_fusion.o_ref.rest_6_), channel_id=1, source_target_pairs={{0,1},{1,0},{2,3},{3,2},{4,5},{5,4},{6,7},{7,6},{8,9},{9,8},{10,11... | collective-permute-start | bytes 3145736 | tf_op jit(solution)/shard_map/ppermute | solution.py:288
  138.9 0.0 collective-permute-done.4.s_ref.rest_1_
  138.9 0.0 collective-permute-done.6.us_ref.rest_3_
  138.9 2.4 %collective-permute-done.10.os_ref.rest_7_ = f32[2048,128]{1,0:T(8,128)} collective-permute-done((f32[2048,128]{1,0:T(8,128)S(1)}, f32[2048,128]{1,0:T(8,128)}, u32[]{:S(2)}, u32[]{:S(2)}) %collective-permute-start.10) | collective-permute-done | bytes 1048608 | tf_op jit(solution)/shard_map/ppermute | solution.py:288
  141.3 0.0 copy-done.2
  141.3 5.9 %gram_share.1 = f32[128,640]{1,0:T(8,128)} custom-call(s32[1]{0:T(128)} %bitcast.y_ref, f32[2048,128]{1,0:T(8,128)} %bitcast.11, f32[2048,128]{1,0:T(8,128)} %collective-permute-done.4.s_ref.rest_1_, f32[2048,128]{1,0:T(8,128)} %copy-done.1, f32[2048,128]{1,0:T(8,128)} %collective-permute-done.6.us_ref.rest_3_, f32[2048,128]{1,0:T(8,128)} %copy-done.2, ...), custom_call_target="tpu_custom_call" | custom-call | flops 1342177280 | bytes 6291456 | tf_op jit(solution)/shard_map/gram_share/pallas_call | solution.py:141
  147.2 12.5 %all_to_all.10 = f32[16,8,640]{2,1,0:T(8,128)S(1)} all-to-all(f32[16,8,640]{2,1,0:T(8,128)} %bitcast.16), channel_id=1, replica_groups=mesh['row'=16,'vec'=8] {'row'}, dimensions={0} | all-to-all | bytes 655360 | tf_op jit(solution)/shard_map/all_to_all | solution.py:305
  159.8 0.1 broadcast_in_dim.17
  159.9 23.6 %all_to_all.11 = f32[64,8,640]{2,1,0:T(8,128)S(1)} all-to-all(f32[64,8,640]{2,1,0:T(8,128)S(1)} %broadcast_in_dim.17), channel_id=1, replica_groups={{0,2,4,6,8,10,12,14,16,18,20,22,24,26,28,30,32,34,36,38,40,42,44,46,48,..., dimensions={0} | all-to-all | bytes 2621440 | tf_op jit(solution)/shard_map/all_to_all | solution.py:314
  183.4 2.8 %collective-permute-start.11 = (f32[16,4,8,640]{3,2,1,0:T(8,128)S(1)}, f32[16,4,8,640]{3,2,1,0:T(8,128)S(1)}, u32[]{:S(2)}, u32[]{:S(2)}) collective-permute-start(f32[16,4,8,640]{3,2,1,0:T(8,128)S(1)} %bitcast.14), channel_id=1, source_target_pairs={{0,1},{1,0},{2,3},{3,2},{4,5},{5,4},{6,7},{7,6},{8,9},{9,8},{10,11... | collective-permute-start | bytes 3932168 | tf_op jit(solution)/shard_map/ppermute | solution.py:288
  186.2 0.1 collective-permute-start.12
  186.3 4.1 %collective-permute-done.12.rest_5_ = f32[2048,128]{1,0:T(8,128)S(1)} collective-permute-done((f32[2048,128]{1,0:T(8,128)S(1)}, f32[2048,128]{1,0:T(8,128)S(1)}, u32[]{:S(2)}, u32[]{:S(2)}) %collective-permute-start.12) | collective-permute-done | bytes 1048608 | tf_op jit(solution)/shard_map/ppermute | solution.py:288
  190.4 0.0 collective-permute-done.11.gb_ref
  190.4 0.0 copy-done.3
  190.4 1.0 copy-done.11
  191.4 1.1 copy-done.10
  192.4 24.2 %finish.1 = f32[2048,128]{1,0:T(8,128)} custom-call(s32[1]{0:T(128)} %bitcast.y_ref, f32[16,4,8,640]{3,2,1,0:T(8,128)} %bitcast.15, f32[16,4,8,640]{3,2,1,0:T(8,128)} %copy-done.10, f32[2048,128]{1,0:T(8,128)} %bitcast.12, f32[2048,128]{1,0:T(8,128)} %collective-permute-done.4.s_ref.rest_1_, f32[2048,128]{1,0:T(8,128)} %copy-done.1, ...), custom_call_target="tpu_custom_call" | custom-call | flops 9663676416 | bytes 9437184 | tf_op jit(solution)/shard_map/finish/pallas_call | solution.py:245
  (18 shorter events, 0.2 us)
Async XLA Ops:
  0.0 28.9 %collective-permute-start.1 = (f32[16,128,128]{2,1,0:T(8,128)}, f32[16,128,128]{2,1,0:T(8,128)S(1)}, u32[]{:S(2)}, u32[]{:S(2)}) collective-permute-start(f32[16,128,128]{2,1,0:T(8,128)} %bitcast.5), channel_id=1, source_target_pairs={{8,0},{16,8},{24,16},{32,24},{40,32},{48,40},{56,48},{64,56},{72,6... | collective-permute-start | bytes 3145736 | tf_op jit(solution)/shard_map/ppermute | solution.py:280
  6.8 27.3 %collective-permute-start = (f32[16,128,128]{2,1,0:T(8,128)}, f32[16,128,128]{2,1,0:T(8,128)S(1)}, u32[]{:S(2)}, u32[]{:S(2)}) collective-permute-start(f32[16,128,128]{2,1,0:T(8,128)} %bitcast.6), channel_id=1, source_target_pairs={{120,0},{0,8},{8,16},{16,24},{24,32},{32,40},{40,48},{48,56},{56,6... | collective-permute-start | bytes 3145736 | tf_op jit(solution)/shard_map/ppermute | solution.py:280
  28.9 5.1 %copy-start.4 = (f32[16,128,128]{2,1,0:T(8,128)}, f32[16,128,128]{2,1,0:T(8,128)S(1)}, u32[]{:S(2)}) copy-start(f32[16,128,128]{2,1,0:T(8,128)S(1)} %collective-permute-done.1.right_ref) | copy-start | bytes 3145732
  34.1 1.0 copy-start.5
  51.4 23.1 %collective-permute-start.3 = (f32[16,128,128]{2,1,0:T(8,128)}, f32[16,128,128]{2,1,0:T(8,128)S(1)}, u32[]{:S(2)}, u32[]{:S(2)}) collective-permute-start(f32[16,128,128]{2,1,0:T(8,128)} %field.2.own_ref), channel_id=1, source_target_pairs={{8,0},{16,8},{24,16},{32,24},{40,32},{48,40},{56,48},{64,56},{72,6... | collective-permute-start | bytes 3145736 | tf_op jit(solution)/shard_map/ppermute | solution.py:280
  52.7 26.4 %collective-permute-start.2 = (f32[16,128,128]{2,1,0:T(8,128)}, f32[16,128,128]{2,1,0:T(8,128)S(1)}, u32[]{:S(2)}, u32[]{:S(2)}) collective-permute-start(f32[16,128,128]{2,1,0:T(8,128)} %field.2.own_ref), channel_id=1, source_target_pairs={{120,0},{0,8},{8,16},{16,24},{24,32},{32,40},{40,48},{48,56},{56,6... | collective-permute-start | bytes 3145736 | tf_op jit(solution)/shard_map/ppermute | solution.py:280
  74.5 4.6 %copy-start.6 = (f32[16,128,128]{2,1,0:T(8,128)}, f32[16,128,128]{2,1,0:T(8,128)S(1)}, u32[]{:S(2)}) copy-start(f32[16,128,128]{2,1,0:T(8,128)S(1)} %collective-permute-done.3.right_ref) | copy-start | bytes 3145732
  79.1 1.0 copy-start.7
  96.8 26.4 %copy-start = (f32[16,128,128]{2,1,0:T(8,128)S(1)}, f32[16,128,128]{2,1,0:T(8,128)}, u32[]{:S(2)}) copy-start(f32[16,128,128]{2,1,0:T(8,128)} %field.3) | copy-start | bytes 3145732
  96.8 22.9 %collective-permute-start.5 = (f32[2048,128]{1,0:T(8,128)}, f32[2048,128]{1,0:T(8,128)S(1)}, u32[]{:S(2)}, u32[]{:S(2)}) collective-permute-start(f32[2048,128]{1,0:T(8,128)} %bitcast.9), channel_id=1, source_target_pairs={{2,0},{3,1},{4,2},{5,3},{6,4},{7,5},{0,6},{1,7},{10,8},{11,9},{12,... | collective-permute-start | bytes 3145736 | tf_op jit(solution)/shard_map/ppermute | solution.py:283
  99.5 23.6 %collective-permute-start.8 = (f32[2048,128]{1,0:T(8,128)}, f32[2048,128]{1,0:T(8,128)S(1)}, u32[]{:S(2)}, u32[]{:S(2)}) collective-permute-start(f32[2048,128]{1,0:T(8,128)} %bitcast.10), channel_id=1, source_target_pairs={{6,0},{7,1},{0,2},{1,3},{2,4},{3,5},{4,6},{5,7},{14,8},{15,9},{8,1... | collective-permute-start | bytes 3145736 | tf_op jit(solution)/shard_map/ppermute | solution.py:283
  119.7 11.2 %copy-start.1 = (f32[2048,128]{1,0:T(8,128)}, f32[2048,128]{1,0:T(8,128)S(1)}, u32[]{:S(2)}) copy-start(f32[2048,128]{1,0:T(8,128)S(1)} %collective-permute-done.5.u_ref.rest_2_) | copy-start | bytes 3145732
  119.7 11.1 %collective-permute-start.7 = (f32[1024,128]{1,0:T(8,128)S(1)}, f32[1024,128]{1,0:T(8,128)S(1)}, u32[]{:S(2)}, u32[]{:S(2)}) collective-permute-start(f32[1024,128]{1,0:T(8,128)S(1)} %slice.8), channel_id=1, source_target_pairs={{2,0},{3,1},{4,2},{5,3},{6,4},{7,5},{0,6},{1,7},{10,8},{11,9},{12,... | collective-permute-start | bytes 1572872 | tf_op jit(solution)/shard_map/ppermute | solution.py:283
  123.1 11.0 %copy-start.8 = (f32[2048,128]{1,0:T(8,128)}, f32[2048,128]{1,0:T(8,128)S(1)}, u32[]{:S(2)}) copy-start(f32[2048,128]{1,0:T(8,128)S(1)} %collective-permute-done.8.rest_4_) | copy-start | bytes 3145732
  123.1 10.9 %collective-permute-start.9 = (f32[1024,128]{1,0:T(8,128)S(1)}, f32[1024,128]{1,0:T(8,128)S(1)}, u32[]{:S(2)}, u32[]{:S(2)}) collective-permute-start(f32[1024,128]{1,0:T(8,128)S(1)} %slice.9), channel_id=1, source_target_pairs={{6,0},{7,1},{0,2},{1,3},{2,4},{3,5},{4,6},{5,7},{14,8},{15,9},{8,1... | collective-permute-start | bytes 1572872 | tf_op jit(solution)/shard_map/ppermute | solution.py:283
  123.2 15.7 %collective-permute-start.4 = (f32[2048,128]{1,0:T(8,128)S(1)}, f32[2048,128]{1,0:T(8,128)}, u32[]{:S(2)}, u32[]{:S(2)}) collective-permute-start(f32[2048,128]{1,0:T(8,128)S(1)} %bitcast.13), channel_id=1, source_target_pairs={{0,1},{1,0},{2,3},{3,2},{4,5},{5,4},{6,7},{7,6},{8,9},{9,8},{10,11... | collective-permute-start | bytes 3145736 | tf_op jit(solution)/shard_map/ppermute | solution.py:288
  127.1 11.8 %collective-permute-start.6 = (f32[2048,128]{1,0:T(8,128)S(1)}, f32[2048,128]{1,0:T(8,128)}, u32[]{:S(2)}, u32[]{:S(2)}) collective-permute-start(f32[2048,128]{1,0:T(8,128)S(1)} %collective-permute-done.5.u_ref.rest_2_), channel_id=1, source_target_pairs={{0,1},{1,0},{2,3},{3,2},{4,5},{5,4},{6,7},{7,6},{8,9},{9,8},{10,11... | collective-permute-start | bytes 3145736 | tf_op jit(solution)/shard_map/ppermute | solution.py:288
  134.1 7.2 %copy-start.2 = (f32[2048,128]{1,0:T(8,128)}, f32[2048,128]{1,0:T(8,128)S(1)}, u32[]{:S(2)}) copy-start(f32[2048,128]{1,0:T(8,128)S(1)} %constant_dynamic-update-slice_fusion.o_ref.rest_6_) | copy-start | bytes 3145732
  134.1 7.2 %collective-permute-start.10 = (f32[2048,128]{1,0:T(8,128)S(1)}, f32[2048,128]{1,0:T(8,128)}, u32[]{:S(2)}, u32[]{:S(2)}) collective-permute-start(f32[2048,128]{1,0:T(8,128)S(1)} %constant_dynamic-update-slice_fusion.o_ref.rest_6_), channel_id=1, source_target_pairs={{0,1},{1,0},{2,3},{3,2},{4,5},{5,4},{6,7},{7,6},{8,9},{9,8},{10,11... | collective-permute-start | bytes 3145736 | tf_op jit(solution)/shard_map/ppermute | solution.py:288
  159.9 26.4 %copy-start.9 = (f32[2048,128]{1,0:T(8,128)S(1)}, f32[2048,128]{1,0:T(8,128)}, u32[]{:S(2)}) copy-start(f32[2048,128]{1,0:T(8,128)} %copy-done.8) | copy-start | bytes 3145732
  183.4 7.0 %copy-start.3 = (f32[64,8,640]{2,1,0:T(8,128)}, f32[64,8,640]{2,1,0:T(8,128)S(1)}, u32[]{:S(2)}) copy-start(f32[64,8,640]{2,1,0:T(8,128)S(1)} %all_to_all.11) | copy-start | bytes 3932164
  183.4 7.0 %collective-permute-start.11 = (f32[16,4,8,640]{3,2,1,0:T(8,128)S(1)}, f32[16,4,8,640]{3,2,1,0:T(8,128)S(1)}, u32[]{:S(2)}, u32[]{:S(2)}) collective-permute-start(f32[16,4,8,640]{3,2,1,0:T(8,128)S(1)} %bitcast.14), channel_id=1, source_target_pairs={{0,1},{1,0},{2,3},{3,2},{4,5},{5,4},{6,7},{7,6},{8,9},{9,8},{10,11... | collective-permute-start | bytes 3932168 | tf_op jit(solution)/shard_map/ppermute | solution.py:288
  186.2 4.2 %collective-permute-start.12 = (f32[2048,128]{1,0:T(8,128)S(1)}, f32[2048,128]{1,0:T(8,128)S(1)}, u32[]{:S(2)}, u32[]{:S(2)}) collective-permute-start(f32[2048,128]{1,0:T(8,128)S(1)} %copy-done.9), channel_id=1, source_target_pairs={{0,1},{1,0},{2,3},{3,2},{4,5},{5,4},{6,7},{7,6},{8,9},{9,8},{10,11... | collective-permute-start | bytes 3145736 | tf_op jit(solution)/shard_map/ppermute | solution.py:288
  190.4 1.0 copy-start.11
  191.4 1.1 copy-start.10
where the time goes:
time: 218 us; the launch traced here: 217 us
  Pallas kernels  78.8 us (36%)
  waiting for transfers between devices  68 us (31%)
  blocking collectives  36.1 us (17%)
  starting transfers between devices  26.1 us (12%)
  local copies, waits for them, and re-layouts  4.89 us (2%)
    ppermute x4, waiting for transfers between devices, from_row(): lax.ppermute(value, 'row', [((i + step) % row_count, i) for i in range(ro...  34.5 us
    pallas_call x2, Pallas kernels, apply_field(): pl.pallas_call(functools.partial(field_kernel, slots, second), out_shape=...  33 us
    ppermute x4, waiting for transfers between devices, from_y(): lax.ppermute(value, 'vec', [((i + 2 * step) % vec_count, i) for i in rang...  27 us
    pallas_call x1, Pallas kernels, finish(): pl.pallas_call(functools.partial(finish_kernel, total_rows), out_shape=ja...  24.2 us
    all_to_all x1, blocking collectives, on_device(): lax.all_to_all(jnp.broadcast_to(part[None], (members,) + part.shape), ('r...  23.6 us
    pallas_call x1, Pallas kernels, split_blocks(): pl.pallas_call(split_kernel, out_shape=jax.ShapeDtypeStruct((block_rows,...  15.6 us
    all_to_all x1, blocking collectives, on_device(): lax.all_to_all(share.reshape(row_count, strip, -1), 'row', split_axis=0,...  12.5 us
    ppermute x5, starting transfers between devices, swap(): return lax.ppermute(value, 'vec', [(i, i ^ 1) for i in range(vec_count)])  11.6 us
  transfers between devices with their start and end apart: 13, of which 9 were waited for; matrix products, arithmetic and copies ran while one was open for 1% of the time, Pallas kernels for 7%

commit v1 on v0

--- a/solution.py
+++ b/solution.py
@@ -52,52 +52,47 @@
     )(hamiltonian)
 
 
-def field_kernel(slots, second, cols_ref, coef_ref, h_ref, left_ref, own_ref, right_ref, *rest):
+SMEM_SPEC = pl.BlockSpec(memory_space=pltpu.SMEM)
+VMEM_SPEC = pl.BlockSpec(memory_space=pltpu.VMEM)
+
+
+def field_kernel(second, cols_ref, coef_ref, h_ref, left_ref, own_ref, right_ref, *rest):
     if second:
         prev_ref, o_ref, wide = rest
     else:
         o_ref, wide = rest
-    i = pl.program_id(0)
-    count = own_ref.shape[0]
-
-    @pl.when(i == 0)
-    def _():
-        for part, ref in enumerate((left_ref, own_ref, right_ref)):
-
-            @pl.loop(0, count)
-            def _(j):
-                high, low = split(ref[j])
-                wide[part * count + j, :, :128] = high
-                wide[part * count + j, :, 128:] = low
-
-        wide[3 * count] = jnp.zeros(wide.shape[1:], BF)
-
-    lhs = jnp.concatenate([h_ref[0, k] for k in range(slots)], axis=1)
-    rhs = jnp.concatenate([wide[cols_ref[i * slots + k]] for k in range(slots)], axis=0)
-    summed = fold(mm(lhs, rhs))
+    count, slots = h_ref.shape[:2]
+    for part, ref in enumerate((left_ref, own_ref, right_ref)):
+
+        @pl.loop(0, count)
+        def _(j):
+            high, low = split(ref[j])
+            wide[part * count + j, :, :128] = high
+            wide[part * count + j, :, 128:] = low
+
+    wide[3 * count] = jnp.zeros(wide.shape[1:], BF)
     centre, inverse = coef_ref[0], coef_ref[1]
-    result = (summed - centre * own_ref[i]) * inverse
-    if second:
-        result = 2.0 * result - prev_ref[i]
-    o_ref[0] = result
+
+    @pl.loop(0, count)
+    def _(i):
+        lhs = jnp.concatenate([h_ref[i, k] for k in range(slots)], axis=1)
+        rhs = jnp.concatenate([wide[cols_ref[i * slots + k]] for k in range(slots)], axis=0)
+        result = (fold(mm(lhs, rhs)) - centre * own_ref[i]) * inverse
+        if second:
+            result = 2.0 * result - prev_ref[i]
+        o_ref[i] = result
 
 
 def apply_field(second, cols, coef, split_h, left, own, right, prev=None):
     block_rows, slots, double, size = split_h.shape
-    whole = pl.BlockSpec((block_rows, size, size), lambda i, *_: (0, 0, 0))
     operands = [split_h, left, own, right] + ([prev] if second else [])
     return pl.pallas_call(
-        functools.partial(field_kernel, slots, second),
+        functools.partial(field_kernel, second),
         out_shape=jax.ShapeDtypeStruct((block_rows, size, size), F32),
-        grid_spec=pltpu.PrefetchScalarGridSpec(
-            num_scalar_prefetch=2,
-            grid=(block_rows,),
-            in_specs=[pl.BlockSpec((1, slots, double, size), lambda i, *_: (i, 0, 0, 0))]
-            + [whole] * (len(operands) - 1),
-            out_specs=pl.BlockSpec((1, size, size), lambda i, *_: (i, 0, 0)),
-            scratch_shapes=[pltpu.VMEM((3 * block_rows + 1, size, 2 * size), BF)],
-        ),
-        compiler_params=pltpu.CompilerParams(vmem_limit_bytes=VMEM_LIMIT),
+        in_specs=[SMEM_SPEC] * 2 + [VMEM_SPEC] * len(operands),
+        out_specs=VMEM_SPEC,
+        scratch_shapes=[pltpu.VMEM((3 * block_rows + 1, size, 2 * size), BF)],
+        compiler_params=pltpu.CompilerParams(vmem_limit_bytes=30 * 2**20),
         cost_estimate=cost(8 * block_rows * slots * size**3, 2 * split_h.size),
         name="field",
     )(cols, coef, *operands)
@@ -106,49 +101,46 @@
 GRAM_BLOCKS = 5
 
 
-def gram_kernel(y_ref, own_ref, s_ref, u_ref, us_ref, o_ref, os_ref, out_ref, acc):
-    step = pl.program_id(0)
-
-    @pl.when(step == 0)
-    def _():
-        acc[...] = jnp.zeros_like(acc)
-
-    lhs = jnp.concatenate(split(own_ref[...].T), axis=0)
-
-    def add(block, ref):
-        acc[block] += mm(lhs, jnp.concatenate(split(ref[...]), axis=1))
-
-    for block, ref in enumerate((own_ref, s_ref, u_ref, us_ref)):
-        add(block, ref)
-
-    @pl.when(y_ref[0] < 2)
-    def _():
-        add(4, o_ref)
-
-    @pl.when(y_ref[0] >= 2)
-    def _():
-        add(4, os_ref)
-
-    @pl.when(step == pl.num_programs(0) - 1)
-    def _():
-        for block in range(GRAM_BLOCKS):
-            out_ref[:, block * 128 : (block + 1) * 128] = fold(acc[block])
+def gram_kernel(y_ref, own_ref, s_ref, u_ref, us_ref, d_ref, out_ref, acc):
+    acc[...] = jnp.zeros_like(acc)
+    chunk = 512
+
+    @pl.loop(0, own_ref.shape[0] // chunk)
+    def _(step):
+        rows = pl.ds(pl.multiple_of(step * chunk, chunk), chunk)
+
+        def turned(ref):
+            return jnp.concatenate(split(ref[rows, :].T), axis=0)
+
+        def paired(ref):
+            return jnp.concatenate(split(ref[rows, :]), axis=1)
+
+        lhs = turned(own_ref)
+        for block, ref in enumerate((own_ref, s_ref, u_ref, us_ref)):
+            acc[block] += mm(lhs, paired(ref))
+        lhs = turned(d_ref)
+
+        @pl.when(y_ref[0] < 2)
+        def _():
+            acc[4] += mm(lhs, paired(u_ref))
+
+        @pl.when(y_ref[0] >= 2)
+        def _():
+            acc[4] += mm(lhs, paired(us_ref))
+
+    for block in range(GRAM_BLOCKS):
+        out_ref[:, block * 128 : (block + 1) * 128] = fold(acc[block])
 
 
 def gram_share(y, pieces):
     rows, cols = pieces[0].shape
-    chunk = 512
     return pl.pallas_call(
         gram_kernel,
         out_shape=jax.ShapeDtypeStruct((cols, GRAM_BLOCKS * cols), F32),
-        grid_spec=pltpu.PrefetchScalarGridSpec(
-            num_scalar_prefetch=1,
-            grid=(rows // chunk,),
-            in_specs=[pl.BlockSpec((chunk, cols), lambda i, *_: (i, 0))] * len(pieces),
-            out_specs=pl.BlockSpec((cols, GRAM_BLOCKS * cols), lambda i, *_: (0, 0)),
-            scratch_shapes=[pltpu.VMEM((GRAM_BLOCKS, 2 * cols, 2 * cols), F32)],
-        ),
-        compiler_params=pltpu.CompilerParams(vmem_limit_bytes=VMEM_LIMIT),
+        in_specs=[SMEM_SPEC] + [VMEM_SPEC] * len(pieces),
+        out_specs=VMEM_SPEC,
+        scratch_shapes=[pltpu.VMEM((GRAM_BLOCKS, 2 * cols, 2 * cols), F32)],
+        compiler_params=pltpu.CompilerParams(vmem_limit_bytes=30 * 2**20),
         cost_estimate=cost(8 * rows * cols * cols * GRAM_BLOCKS, 4 * rows * cols * len(pieces)),
         name="gram_share",
     )(y, *pieces)
@@ -161,12 +153,11 @@
 
 def finish_kernel(total_rows, y_ref, ga_ref, gb_ref, *rest):
     x_refs = rest[: len(PIECES)]
-    out_ref, gram, gram_low, state, factor = rest[len(PIECES) :]
+    out_ref, gram, gram_low, state, factor, ordered = rest[len(PIECES) :]
     grams = (ga_ref, gb_ref)
     y = y_ref[0]
 
-    @pl.when(pl.program_id(0) == 0)
-    def _():
+    if True:
         diagonal = lax.broadcasted_iota(jnp.int32, (128, 128), 0) == lax.broadcasted_iota(
             jnp.int32, (128, 128), 1
         )
@@ -190,14 +181,18 @@
         for k in range(2):
             for row in range(4):
                 here = 4 * k + row
-                after, across = (row + 1) % 4, (row + 2) % 4
+                after, before = (row + 1) % 4, (row + 3) % 4
                 side = k if row < 2 else 1 - k
                 put(here, here, block(k, row, 0) * square)
                 put(here, 4 * (1 - k) + row, block(k, row, 1) * square)
-                for there, b in ((4 * k + after, 2), (4 * (1 - k) + after, 3), (4 * side + across, 4)):
+                for one, two, b in (
+                    (here, 4 * k + after, 2),
+                    (here, 4 * (1 - k) + after, 3),
+                    (4 * k + before, 4 * side + after, 4),
+                ):
                     value = block(k, row, b) * square
-                    put(here, there, value)
-                    put(there, here, value.T)
+                    put(one, two, value)
+                    put(two, one, value.T)
 
         mine = pl.ds(pl.multiple_of(y * 128, 128), 128)
         column = lax.broadcasted_iota(jnp.int32, (128, NV), 1) - y * 128
@@ -226,7 +221,6 @@
         factor[:, :128] = high
         factor[:, 128:] = low
 
-    lhs = jnp.concatenate([ref[...] for ref in x_refs], axis=1)
     rhs = jnp.concatenate(
         [
             factor[pl.ds(pl.multiple_of((4 * k + lax.rem(y + dy, 4)) * 128, 128), 128), :]
@@ -234,30 +228,31 @@
         ],
         axis=0,
     )
-    out_ref[...] = fold(mm(jnp.concatenate(split(lhs), axis=0), rhs))
+    ordered[...] = rhs
+    chunk = 256
+
+    @pl.loop(0, out_ref.shape[0] // chunk)
+    def _(step):
+        rows = pl.ds(pl.multiple_of(step * chunk, chunk), chunk)
+        lhs = jnp.concatenate([ref[rows, :] for ref in x_refs], axis=1)
+        out_ref[rows, :] = fold(mm(jnp.concatenate(split(lhs), axis=0), ordered[...]))
 
 
 def finish(total_rows, y, gram_a, gram_b, pieces):
     rows, cols = pieces[0].shape
-    chunk = 256
-    whole = pl.BlockSpec(gram_a.shape, lambda i, *_: (0, 0, 0, 0))
-    part = pl.BlockSpec((chunk, cols), lambda i, *_: (i, 0))
     return pl.pallas_call(
         functools.partial(finish_kernel, total_rows),
         out_shape=jax.ShapeDtypeStruct((rows, cols), F32),
-        grid_spec=pltpu.PrefetchScalarGridSpec(
-            num_scalar_prefetch=1,
-            grid=(rows // chunk,),
-            in_specs=[whole, whole] + [part] * len(pieces),
-            out_specs=part,
-            scratch_shapes=[
-                pltpu.VMEM((NV, NV), BF),
-                pltpu.VMEM((NV, NV), BF),
-                pltpu.VMEM((3, cols, NV), F32),
-                pltpu.VMEM((NV, 2 * cols), BF),
-            ],
-        ),
-        compiler_params=pltpu.CompilerParams(vmem_limit_bytes=VMEM_LIMIT),
+        in_specs=[SMEM_SPEC] + [VMEM_SPEC] * (2 + len(pieces)),
+        out_specs=VMEM_SPEC,
+        scratch_shapes=[
+            pltpu.VMEM((NV, NV), BF),
+            pltpu.VMEM((NV, NV), BF),
+            pltpu.VMEM((3, cols, NV), F32),
+            pltpu.VMEM((NV, 2 * cols), BF),
+            pltpu.VMEM((NV, 2 * cols), BF),
+        ],
+        compiler_params=pltpu.CompilerParams(vmem_limit_bytes=40 * 2**20),
         cost_estimate=cost(12 * 6 * cols * NV * NV, 4 * rows * cols * 9),
         name="finish",
     )(y, gram_a, gram_b, *pieces)
@@ -300,7 +295,7 @@
     across = jnp.concatenate([from_y(up[:half], 1), from_y(down[half:], -1)], axis=0)
     pieces = (own, swap(own), up, swap(up), down, swap(down), across, swap(across))
 
-    share = gram_share(y, pieces[:4] + pieces[6:])
+    share = gram_share(y, pieces[:5])
     strip = share.shape[0] // row_count
     parts = lax.all_to_all(
         share.reshape(row_count, strip, -1), "row", split_axis=0, concat_axis=0, tiled=True

time: 218 us -> 188 us (0.86)
  blocking collectives: 36.1 us -> 11.1 us
  Pallas kernels: 78.8 us -> 56.5 us
  waiting for transfers between devices: 68 us -> 76.6 us
  starting transfers between devices: 26.1 us -> 31.1 us
  local copies, waits for them, and re-layouts: 4.89 us -> 9.66 us
    all_to_all x1 -> x0, blocking collectives: 23.6 us -> none  [on_device(): lax.all_to_all(jnp.broadcast_to(part[None], (members,) + part.shape), ('r...]
    pallas_call x2, Pallas kernels: 33 us -> 14.7 us  [apply_field(): pl.pallas_call(functools.partial(field_kernel, second), out_shape=jax.Sha...]
    all_to_all x0 -> x1, waiting for transfers between devices: none -> 15.6 us  [on_device(): lax.all_to_all(jnp.broadcast_to(part[None], (members,) + part.shape), ('r...]
    all_to_all x0 -> x1, starting transfers between devices: none -> 7.84 us  [on_device(): lax.all_to_all(jnp.broadcast_to(part[None], (members,) + part.shape), ('r...]
    ppermute x4, waiting for transfers between devices: 27 us -> 22 us  [from_y(): lax.ppermute(value, 'vec', [((i + 2 * step) % vec_count, i) for i in rang...]
    pallas_call x1, Pallas kernels: 24.2 us -> 21.5 us  [finish(): pl.pallas_call(functools.partial(finish_kernel, total_rows), out_shape=ja...]
    unnamed x25 -> x5, local copies, waits for them, and re-layouts: 4.01 us -> 5.66 us
  transfers between devices with their start and end apart: 13 -> 14, of which waited for: 9 -> 10; matrix products, arithmetic and copies ran while one was open for 1% -> 3% of each run, Pallas kernels for 7% -> 8%
where the time goes in v1:
time: 188 us; the launch traced here: 187 us
  waiting for transfers between devices  76.6 us (41%)
  Pallas kernels  56.5 us (30%)
  starting transfers between devices  31.1 us (17%)
  blocking collectives  11.1 us (6%)
  local copies, waits for them, and re-layouts  9.66 us (5%)
    ppermute x4, waiting for transfers between devices, from_row(): lax.ppermute(value, 'row', [((i + step) % row_count, i) for i in range(ro...  34.3 us
    ppermute x4, waiting for transfers between devices, from_y(): lax.ppermute(value, 'vec', [((i + 2 * step) % vec_count, i) for i in rang...  22 us
    pallas_call x1, Pallas kernels, finish(): pl.pallas_call(functools.partial(finish_kernel, total_rows), out_shape=ja...  21.5 us
    pallas_call x1, Pallas kernels, split_blocks(): pl.pallas_call(split_kernel, out_shape=jax.ShapeDtypeStruct((block_rows,...  15.7 us
    all_to_all x1, waiting for transfers between devices, on_device(): lax.all_to_all(jnp.broadcast_to(part[None], (members,) + part.shape), ('r...  15.6 us
    pallas_call x2, Pallas kernels, apply_field(): pl.pallas_call(functools.partial(field_kernel, second), out_shape=jax.Sha...  14.7 us
    all_to_all x1, blocking collectives, on_device(): lax.all_to_all(share.reshape(row_count, strip, -1), 'row', split_axis=0,...  11.1 us
    ppermute x5, starting transfers between devices, swap(): return lax.ppermute(value, 'vec', [(i, i ^ 1) for i in range(vec_count)])  10 us
  transfers between devices with their start and end apart: 14, of which 10 were waited for; matrix products, arithmetic and copies ran while one was open for 3% of the time, Pallas kernels for 8%

profile of v1, /device:TPU:1, one launch (start us, length us, event | category | flops | bytes accessed | tf_op | source)
XLA Modules:
  0.0 187.3 jit_solution(8702540319074492252)
XLA Ops:
  0.0 6.8 %collective-permute-start.1 = (f32[16,128,128]{2,1,0:T(8,128)}, f32[16,128,128]{2,1,0:T(8,128)S(1)}, u32[]{:S(2)}, u32[]{:S(2)}) collective-permute-start(f32[16,128,128]{2,1,0:T(8,128)} %bitcast.5), channel_id=1, source_target_pairs={{8,0},{16,8},{24,16},{32,24},{40,32},{48,40},{56,48},{64,56},{72,6... | collective-permute-start | bytes 3145736 | tf_op jit(solution)/shard_map/ppermute | solution.py:275
  6.8 0.0 collective-permute-start
  8.1 0.8 fusion.2
  8.8 0.1 reshape.27.cols_ref
  8.9 0.0 copy-start.1
  9.0 15.7 %split_blocks.1.h_ref = bf16[16,12,256,128]{3,2,1,0:T(8,128)(2,1)} custom-call(f32[16,12,128,128]{3,2,1,0:T(8,128)} %h_ref.1), custom_call_target="tpu_custom_call" | custom-call | bytes 25165824 | tf_op jit(solution)/shard_map/split_blocks/pallas_call | solution.py:43
  24.7 0.1 pad_maximum_fusion.coef_ref
  24.8 4.1 %collective-permute-done.1.right_ref = f32[16,128,128]{2,1,0:T(8,128)S(1)} collective-permute-done((f32[16,128,128]{2,1,0:T(8,128)}, f32[16,128,128]{2,1,0:T(8,128)S(1)}, u32[]{:S(2)}, u32[]{:S(2)}) %collective-permute-start.1) | collective-permute-done | bytes 1048608 | tf_op jit(solution)/shard_map/ppermute | solution.py:275
  28.9 5.1 %collective-permute-done.left_ref = f32[16,128,128]{2,1,0:T(8,128)S(1)} collective-permute-done((f32[16,128,128]{2,1,0:T(8,128)}, f32[16,128,128]{2,1,0:T(8,128)S(1)}, u32[]{:S(2)}, u32[]{:S(2)}) %collective-permute-start) | collective-permute-done | bytes 1048608 | tf_op jit(solution)/shard_map/ppermute | solution.py:275
  34.1 0.0 copy-done.1
  34.1 0.0 copy-start
  34.1 4.6 %copy-done = bf16[16,12,256,128]{3,2,1,0:T(8,128)(2,1)S(1)} copy-done((bf16[16,12,256,128]{3,2,1,0:T(8,128)(2,1)S(1)}, bf16[16,12,256,128]{3,2,1,0:T(8,128)(2,1)}, u32[]{:S(2)}) %copy-start) | copy-done | bytes 12582936
  38.6 7.3 %field.2.own_ref = f32[16,128,128]{2,1,0:T(8,128)S(1)} custom-call(s32[192]{0:T(256)S(1)} %reshape.27.cols_ref, f32[2]{0:T(128)S(1)} %pad_maximum_fusion.coef_ref, bf16[16,12,256,128]{3,2,1,0:T(8,128)(2,1)S(1)} %copy-done, f32[16,128,128]{2,1,0:T(8,128)S(1)} %collective-permute-done.left_ref, f32[16,128,128]{2,1,0:T(8,128)S(1)} %bitcast.7, ...), custom_call_target="tpu_custom_call" | custom-call | flops 3221225472 | bytes 12582912 | tf_op jit(solution)/shard_map/field/pallas_call | solution.py:89
  46.0 0.3 collective-permute-start.3
  46.3 1.2 collective-permute-start.2
  47.5 21.4 %collective-permute-done.3.right_ref = f32[16,128,128]{2,1,0:T(8,128)S(1)} collective-permute-done((f32[16,128,128]{2,1,0:T(8,128)S(1)}, f32[16,128,128]{2,1,0:T(8,128)S(1)}, u32[]{:S(2)}, u32[]{:S(2)}) %collective-permute-start.3) | collective-permute-done | bytes 1048608 | tf_op jit(solution)/shard_map/ppermute | solution.py:275
  69.0 3.6 %collective-permute-done.2.left_ref = f32[16,128,128]{2,1,0:T(8,128)S(1)} collective-permute-done((f32[16,128,128]{2,1,0:T(8,128)S(1)}, f32[16,128,128]{2,1,0:T(8,128)S(1)}, u32[]{:S(2)}, u32[]{:S(2)}) %collective-permute-start.2) | collective-permute-done | bytes 1048608 | tf_op jit(solution)/shard_map/ppermute | solution.py:275
  72.6 7.4 %field.3 = f32[16,128,128]{2,1,0:T(8,128)S(1)} custom-call(s32[192]{0:T(256)S(1)} %reshape.27.cols_ref, f32[2]{0:T(128)S(1)} %pad_maximum_fusion.coef_ref, bf16[16,12,256,128]{3,2,1,0:T(8,128)(2,1)S(1)} %copy-done, f32[16,128,128]{2,1,0:T(8,128)S(1)} %collective-permute-done.2.left_ref, f32[16,128,128]{2,1,0:T(8,128)S(1)} %field.2.own_ref, ...), custom_call_target="tpu_custom_call" | custom-call | flops 3221225472 | bytes 12582912 | tf_op jit(solution)/shard_map/field/pallas_call | solution.py:89
  79.9 2.8 %collective-permute-start.5 = (f32[2048,128]{1,0:T(8,128)S(1)}, f32[2048,128]{1,0:T(8,128)S(1)}, u32[]{:S(2)}, u32[]{:S(2)}) collective-permute-start(f32[2048,128]{1,0:T(8,128)S(1)} %bitcast.9), channel_id=1, source_target_pairs={{2,0},{3,1},{4,2},{5,3},{6,4},{7,5},{0,6},{1,7},{10,8},{11,9},{12,... | collective-permute-start | bytes 3145736 | tf_op jit(solution)/shard_map/ppermute | solution.py:278
  82.7 0.0 collective-permute-start.7
  82.8 2.9 %collective-permute-start.4 = (f32[2048,128]{1,0:T(8,128)S(1)}, f32[2048,128]{1,0:T(8,128)}, u32[]{:S(2)}, u32[]{:S(2)}) collective-permute-start(f32[2048,128]{1,0:T(8,128)S(1)} %bitcast.11), channel_id=1, source_target_pairs={{0,1},{1,0},{2,3},{3,2},{4,5},{5,4},{6,7},{7,6},{8,9},{9,8},{10,11... | collective-permute-start | bytes 3145736 | tf_op jit(solution)/shard_map/ppermute | solution.py:283
  85.7 16.9 %collective-permute-done.5.u_ref.rest_2_ = f32[2048,128]{1,0:T(8,128)S(1)} collective-permute-done((f32[2048,128]{1,0:T(8,128)S(1)}, f32[2048,128]{1,0:T(8,128)S(1)}, u32[]{:S(2)}, u32[]{:S(2)}) %collective-permute-start.5) | collective-permute-done | bytes 1048608 | tf_op jit(solution)/shard_map/ppermute | solution.py:278
  102.6 3.5 %collective-permute-start.6 = (f32[2048,128]{1,0:T(8,128)S(1)}, f32[2048,128]{1,0:T(8,128)}, u32[]{:S(2)}, u32[]{:S(2)}) collective-permute-start(f32[2048,128]{1,0:T(8,128)S(1)} %collective-permute-done.5.u_ref.rest_2_), channel_id=1, source_target_pairs={{0,1},{1,0},{2,3},{3,2},{4,5},{5,4},{6,7},{7,6},{8,9},{9,8},{10,11... | collective-permute-start | bytes 3145736 | tf_op jit(solution)/shard_map/ppermute | solution.py:283
  106.1 0.0 collective-permute-done.7.d_ref.rest_4_
  106.1 0.0 collective-permute-done.4.s_ref.rest_1_
  106.1 2.4 %collective-permute-done.6.us_ref.rest_3_ = f32[2048,128]{1,0:T(8,128)} collective-permute-done((f32[2048,128]{1,0:T(8,128)S(1)}, f32[2048,128]{1,0:T(8,128)}, u32[]{:S(2)}, u32[]{:S(2)}) %collective-permute-start.6) | collective-permute-done | bytes 1048608 | tf_op jit(solution)/shard_map/ppermute | solution.py:283
  108.5 4.6 %gram_share.1 = f32[128,640]{1,0:T(8,128)S(1)} custom-call(s32[1]{0:T(128)} %bitcast.y_ref, f32[2048,128]{1,0:T(8,128)S(1)} %bitcast.12, f32[2048,128]{1,0:T(8,128)} %collective-permute-done.4.s_ref.rest_1_, f32[2048,128]{1,0:T(8,128)S(1)} %collective-permute-done.5.u_ref.rest_2_, f32[2048,128]{1,0:T(8,128)} %collective-permute-done.6.us_ref.rest_3_, ...), custom_call_target="tpu_custom_call" | custom-call | flops 1342177280 | bytes 5242880 | tf_op jit(solution)/shard_map/gram_share/pallas_call | solution.py:137
  113.2 11.1 %all_to_all.10 = f32[16,8,640]{2,1,0:T(8,128)S(1)} all-to-all(f32[16,8,640]{2,1,0:T(8,128)S(1)} %bitcast.14), channel_id=1, replica_groups=mesh['row'=16,'vec'=8] {'row'}, dimensions={0} | all-to-all | bytes 655360 | tf_op jit(solution)/shard_map/all_to_all | solution.py:300
  124.3 1.1 broadcast_in_dim.17
  125.4 7.8 %all-to-all-start.1 = ((f32[64,8,640]{2,1,0:T(8,128)}), f32[64,8,640]{2,1,0:T(8,128)}, u32[]{:S(2)}, u32[]{:S(2)}) async-start(f32[64,8,640]{2,1,0:T(8,128)} %broadcast_in_dim.17), calls=%async_computation.1 | async-start | bytes 2621440 | tf_op jit(solution)/shard_map/all_to_all | solution.py:309
  133.3 0.8 slice.8
  134.1 2.2 %collective-permute-start.10 = (f32[1024,128]{1,0:T(8,128)}, f32[1024,128]{1,0:T(8,128)}, u32[]{:S(2)}, u32[]{:S(2)}) collective-permute-start(f32[1024,128]{1,0:T(8,128)} %slice.8), channel_id=1, source_target_pairs={{2,0},{3,1},{4,2},{5,3},{6,4},{7,5},{0,6},{1,7},{10,8},{11,9},{12,... | collective-permute-start | bytes 1572872 | tf_op jit(solution)/shard_map/ppermute | solution.py:278
  136.2 0.9 slice.9
  137.1 0.0 collective-permute-start.11
  137.1 15.6 %all-to-all-done.1 = f32[64,8,640]{2,1,0:T(8,128)} async-done(((f32[64,8,640]{2,1,0:T(8,128)}), f32[64,8,640]{2,1,0:T(8,128)}, u32[]{:S(2)}, u32[]{:S(2)}) %all-to-all-start.1) | async-done | bytes 1310752 | tf_op jit(solution)/shard_map/all_to_all | solution.py:309
  152.7 2.9 %collective-permute-start.8 = (f32[16,4,8,640]{3,2,1,0:T(8,128)}, f32[16,4,8,640]{3,2,1,0:T(8,128)S(1)}, u32[]{:S(2)}, u32[]{:S(2)}) collective-permute-start(f32[16,4,8,640]{3,2,1,0:T(8,128)} %bitcast.4.ga_ref), channel_id=1, source_target_pairs={{0,1},{1,0},{2,3},{3,2},{4,5},{5,4},{6,7},{7,6},{8,9},{9,8},{10,11... | collective-permute-start | bytes 3932168 | tf_op jit(solution)/shard_map/ppermute | solution.py:283
  155.6 0.0 collective-permute-start.9
  155.6 3.2 %collective-permute-done.10 = f32[1024,128]{1,0:T(8,128)} collective-permute-done((f32[1024,128]{1,0:T(8,128)}, f32[1024,128]{1,0:T(8,128)}, u32[]{:S(2)}, u32[]{:S(2)}) %collective-permute-start.10) | collective-permute-done | bytes 524320 | tf_op jit(solution)/shard_map/ppermute | solution.py:278
  158.9 1.1 constant_dynamic-update-slice_fusion.1
  159.9 1.9 %collective-permute-done.11 = f32[1024,128]{1,0:T(8,128)} collective-permute-done((f32[1024,128]{1,0:T(8,128)}, f32[1024,128]{1,0:T(8,128)}, u32[]{:S(2)}, u32[]{:S(2)}) %collective-permute-start.11) | collective-permute-done | bytes 524320 | tf_op jit(solution)/shard_map/ppermute | solution.py:278
  161.9 1.1 constant_dynamic-update-slice_fusion.rest_6_
  162.9 0.6 collective-permute-start.12
  163.6 0.0 collective-permute-done.9.rest_5_
  163.6 2.3 %collective-permute-done.12.rest_7_ = f32[2048,128]{1,0:T(8,128)S(1)} collective-permute-done((f32[2048,128]{1,0:T(8,128)S(1)}, f32[2048,128]{1,0:T(8,128)S(1)}, u32[]{:S(2)}, u32[]{:S(2)}) %collective-permute-start.12) | collective-permute-done | bytes 1048608 | tf_op jit(solution)/shard_map/ppermute | solution.py:283
  165.9 0.0 collective-permute-done.8.gb_ref
  165.9 21.5 %finish.1 = f32[2048,128]{1,0:T(8,128)} custom-call(s32[1]{0:T(128)} %bitcast.y_ref, f32[16,4,8,640]{3,2,1,0:T(8,128)} %bitcast.4.ga_ref, f32[16,4,8,640]{3,2,1,0:T(8,128)S(1)} %collective-permute-done.8.gb_ref, f32[2048,128]{1,0:T(8,128)S(1)} %bitcast.13, f32[2048,128]{1,0:T(8,128)} %collective-permute-done.4.s_ref.rest_1_, ...), custom_call_target="tpu_custom_call" | custom-call | flops 9663676416 | bytes 9437184 | tf_op jit(solution)/shard_map/finish/pallas_call | solution.py:243
  (1 shorter events, 0.0 us)
Async XLA Ops:
  0.0 28.9 %collective-permute-start.1 = (f32[16,128,128]{2,1,0:T(8,128)}, f32[16,128,128]{2,1,0:T(8,128)S(1)}, u32[]{:S(2)}, u32[]{:S(2)}) collective-permute-start(f32[16,128,128]{2,1,0:T(8,128)} %bitcast.5), channel_id=1, source_target_pairs={{8,0},{16,8},{24,16},{32,24},{40,32},{48,40},{56,48},{64,56},{72,6... | collective-permute-start | bytes 3145736 | tf_op jit(solution)/shard_map/ppermute | solution.py:275
  6.8 27.3 %collective-permute-start = (f32[16,128,128]{2,1,0:T(8,128)}, f32[16,128,128]{2,1,0:T(8,128)S(1)}, u32[]{:S(2)}, u32[]{:S(2)}) collective-permute-start(f32[16,128,128]{2,1,0:T(8,128)} %bitcast.6), channel_id=1, source_target_pairs={{120,0},{0,8},{8,16},{16,24},{24,32},{32,40},{40,48},{48,56},{56,6... | collective-permute-start | bytes 3145736 | tf_op jit(solution)/shard_map/ppermute | solution.py:275
  8.9 25.1 %copy-start.1 = (f32[2048,128]{1,0:T(8,128)S(1)}, f32[2048,128]{1,0:T(8,128)}, u32[]{:S(2)}) copy-start(f32[2048,128]{1,0:T(8,128)} %param.6) | copy-start | bytes 3145732
  34.1 4.6 %copy-start = (bf16[16,12,256,128]{3,2,1,0:T(8,128)(2,1)S(1)}, bf16[16,12,256,128]{3,2,1,0:T(8,128)(2,1)}, u32[]{:S(2)}) copy-start(bf16[16,12,256,128]{3,2,1,0:T(8,128)(2,1)} %split_blocks.1.h_ref) | copy-start | bytes 37748740
  46.0 23.0 %collective-permute-start.3 = (f32[16,128,128]{2,1,0:T(8,128)S(1)}, f32[16,128,128]{2,1,0:T(8,128)S(1)}, u32[]{:S(2)}, u32[]{:S(2)}) collective-permute-start(f32[16,128,128]{2,1,0:T(8,128)S(1)} %field.2.own_ref), channel_id=1, source_target_pairs={{8,0},{16,8},{24,16},{32,24},{40,32},{48,40},{56,48},{64,56},{72,6... | collective-permute-start | bytes 3145736 | tf_op jit(solution)/shard_map/ppermute | solution.py:275
  46.3 26.2 %collective-permute-start.2 = (f32[16,128,128]{2,1,0:T(8,128)S(1)}, f32[16,128,128]{2,1,0:T(8,128)S(1)}, u32[]{:S(2)}, u32[]{:S(2)}) collective-permute-start(f32[16,128,128]{2,1,0:T(8,128)S(1)} %field.2.own_ref), channel_id=1, source_target_pairs={{120,0},{0,8},{8,16},{16,24},{24,32},{32,40},{40,48},{48,56},{56,6... | collective-permute-start | bytes 3145736 | tf_op jit(solution)/shard_map/ppermute | solution.py:275
  79.9 22.7 %collective-permute-start.5 = (f32[2048,128]{1,0:T(8,128)S(1)}, f32[2048,128]{1,0:T(8,128)S(1)}, u32[]{:S(2)}, u32[]{:S(2)}) collective-permute-start(f32[2048,128]{1,0:T(8,128)S(1)} %bitcast.9), channel_id=1, source_target_pairs={{2,0},{3,1},{4,2},{5,3},{6,4},{7,5},{0,6},{1,7},{10,8},{11,9},{12,... | collective-permute-start | bytes 3145736 | tf_op jit(solution)/shard_map/ppermute | solution.py:278
  82.7 23.4 %collective-permute-start.7 = (f32[2048,128]{1,0:T(8,128)S(1)}, f32[2048,128]{1,0:T(8,128)S(1)}, u32[]{:S(2)}, u32[]{:S(2)}) collective-permute-start(f32[2048,128]{1,0:T(8,128)S(1)} %bitcast.10), channel_id=1, source_target_pairs={{6,0},{7,1},{0,2},{1,3},{2,4},{3,5},{4,6},{5,7},{14,8},{15,9},{8,1... | collective-permute-start | bytes 3145736 | tf_op jit(solution)/shard_map/ppermute | solution.py:278
  82.8 23.4 %collective-permute-start.4 = (f32[2048,128]{1,0:T(8,128)S(1)}, f32[2048,128]{1,0:T(8,128)}, u32[]{:S(2)}, u32[]{:S(2)}) collective-permute-start(f32[2048,128]{1,0:T(8,128)S(1)} %bitcast.11), channel_id=1, source_target_pairs={{0,1},{1,0},{2,3},{3,2},{4,5},{5,4},{6,7},{7,6},{8,9},{9,8},{10,11... | collective-permute-start | bytes 3145736 | tf_op jit(solution)/shard_map/ppermute | solution.py:283
  102.6 5.9 %collective-permute-start.6 = (f32[2048,128]{1,0:T(8,128)S(1)}, f32[2048,128]{1,0:T(8,128)}, u32[]{:S(2)}, u32[]{:S(2)}) collective-permute-start(f32[2048,128]{1,0:T(8,128)S(1)} %collective-permute-done.5.u_ref.rest_2_), channel_id=1, source_target_pairs={{0,1},{1,0},{2,3},{3,2},{4,5},{5,4},{6,7},{7,6},{8,9},{9,8},{10,11... | collective-permute-start | bytes 3145736 | tf_op jit(solution)/shard_map/ppermute | solution.py:283
  125.4 27.3 %all-to-all-start.1 = ((f32[64,8,640]{2,1,0:T(8,128)}), f32[64,8,640]{2,1,0:T(8,128)}, u32[]{:S(2)}, u32[]{:S(2)}) async-start(f32[64,8,640]{2,1,0:T(8,128)} %broadcast_in_dim.17), calls=%async_computation.1 | async-start | bytes 2621440 | tf_op jit(solution)/shard_map/all_to_all | solution.py:309
  134.1 24.8 %collective-permute-start.10 = (f32[1024,128]{1,0:T(8,128)}, f32[1024,128]{1,0:T(8,128)}, u32[]{:S(2)}, u32[]{:S(2)}) collective-permute-start(f32[1024,128]{1,0:T(8,128)} %slice.8), channel_id=1, source_target_pairs={{2,0},{3,1},{4,2},{5,3},{6,4},{7,5},{0,6},{1,7},{10,8},{11,9},{12,... | collective-permute-start | bytes 1572872 | tf_op jit(solution)/shard_map/ppermute | solution.py:278
  137.1 24.7 %collective-permute-start.11 = (f32[1024,128]{1,0:T(8,128)}, f32[1024,128]{1,0:T(8,128)}, u32[]{:S(2)}, u32[]{:S(2)}) collective-permute-start(f32[1024,128]{1,0:T(8,128)} %slice.9), channel_id=1, source_target_pairs={{6,0},{7,1},{0,2},{1,3},{2,4},{3,5},{4,6},{5,7},{14,8},{15,9},{8,1... | collective-permute-start | bytes 1572872 | tf_op jit(solution)/shard_map/ppermute | solution.py:278
  152.7 13.1 %collective-permute-start.8 = (f32[16,4,8,640]{3,2,1,0:T(8,128)}, f32[16,4,8,640]{3,2,1,0:T(8,128)S(1)}, u32[]{:S(2)}, u32[]{:S(2)}) collective-permute-start(f32[16,4,8,640]{3,2,1,0:T(8,128)} %bitcast.4.ga_ref), channel_id=1, source_target_pairs={{0,1},{1,0},{2,3},{3,2},{4,5},{5,4},{6,7},{7,6},{8,9},{9,8},{10,11... | collective-permute-start | bytes 3932168 | tf_op jit(solution)/shard_map/ppermute | solution.py:283
  155.6 7.9 %collective-permute-start.9 = (f32[2048,128]{1,0:T(8,128)S(1)}, f32[2048,128]{1,0:T(8,128)S(1)}, u32[]{:S(2)}, u32[]{:S(2)}) collective-permute-start(f32[2048,128]{1,0:T(8,128)S(1)} %collective-permute-done.7.d_ref.rest_4_), channel_id=1, source_target_pairs={{0,1},{1,0},{2,3},{3,2},{4,5},{5,4},{6,7},{7,6},{8,9},{9,8},{10,11... | collective-permute-start | bytes 3145736 | tf_op jit(solution)/shard_map/ppermute | solution.py:283
  162.9 2.9 %collective-permute-start.12 = (f32[2048,128]{1,0:T(8,128)S(1)}, f32[2048,128]{1,0:T(8,128)S(1)}, u32[]{:S(2)}, u32[]{:S(2)}) collective-permute-start(f32[2048,128]{1,0:T(8,128)S(1)} %constant_dynamic-update-slice_fusion.rest_6_), channel_id=1, source_target_pairs={{0,1},{1,0},{2,3},{3,2},{4,5},{5,4},{6,7},{7,6},{8,9},{9,8},{10,11... | collective-permute-start | bytes 3145736 | tf_op jit(solution)/shard_map/ppermute | solution.py:283

commit v2 on v1

--- a/solution.py
+++ b/solution.py
@@ -8,10 +8,10 @@
 from jax.experimental.pallas import tpu as pltpu
 from jax.sharding import PartitionSpec as P
 
+
 NV = 1024
 BF = jnp.bfloat16
 F32 = jnp.float32
-VMEM_LIMIT = 56 * 1024 * 1024
 
 
 def split(x):
@@ -32,10 +32,32 @@
     return pl.CostEstimate(flops=flops, bytes_accessed=moved, transcendentals=0)
 
 
-def split_kernel(h_ref, o_ref):
-    high, low = split(h_ref[0])
-    o_ref[0, :, :128, :] = high
-    o_ref[0, :, 128:, :] = low
+DEPTH = 4
+
+
+def split_kernel(h_ref, o_ref, buffer, arrived):
+    count, size = o_ref.shape[0], h_ref.shape[-1]
+
+    def fetch(row, slot):
+        return pltpu.make_async_copy(h_ref.at[row], buffer.at[slot], arrived.at[slot])
+
+    for slot in range(DEPTH):
+        fetch(slot, slot).start()
+
+    @pl.loop(0, count)
+    def _(row):
+        slot = lax.rem(row, DEPTH)
+        fetch(row, slot).wait()
+
+        @pl.loop(0, o_ref.shape[1])
+        def _(k):
+            high, low = split(buffer[slot, k])
+            o_ref[row, k, :size, :] = high
+            o_ref[row, k, size:, :] = low
+
+        @pl.when(row + DEPTH < count)
+        def _():
+            fetch(row + DEPTH, slot).start()
 
 
 def split_blocks(hamiltonian):
@@ -43,10 +65,13 @@
     return pl.pallas_call(
         split_kernel,
         out_shape=jax.ShapeDtypeStruct((block_rows, slots, 2 * size, size), BF),
-        grid=(block_rows,),
-        in_specs=[pl.BlockSpec((1, slots, size, size), lambda i: (i, 0, 0, 0))],
-        out_specs=pl.BlockSpec((1, slots, 2 * size, size), lambda i: (i, 0, 0, 0)),
-        compiler_params=pltpu.CompilerParams(vmem_limit_bytes=VMEM_LIMIT),
+        in_specs=[pl.BlockSpec(memory_space=pl.ANY)],
+        out_specs=pl.BlockSpec(memory_space=pltpu.VMEM),
+        scratch_shapes=[
+            pltpu.VMEM((DEPTH, slots, size, size), F32),
+            pltpu.SemaphoreType.DMA((DEPTH,)),
+        ],
+        compiler_params=pltpu.CompilerParams(vmem_limit_bytes=30 * 2**20),
         cost_estimate=cost(0, 8 * block_rows * slots * size * size),
         name="split_blocks",
     )(hamiltonian)
@@ -84,7 +109,7 @@
 
 
 def apply_field(second, cols, coef, split_h, left, own, right, prev=None):
-    block_rows, slots, double, size = split_h.shape
+    block_rows, slots, _, size = split_h.shape
     operands = [split_h, left, own, right] + ([prev] if second else [])
     return pl.pallas_call(
         functools.partial(field_kernel, second),
@@ -149,77 +174,78 @@
 KEEP = {0: 1, 3: 2, 4: 1, 8: 1}
 BASE = {2: 1, 6: 1, 10: 1, 11: 2}
 PIECES = ((0, 0), (1, 0), (0, 1), (1, 1), (0, 3), (1, 3), (0, 2), (1, 2))
+WHOLE = 6
 
 
 def finish_kernel(total_rows, y_ref, ga_ref, gb_ref, *rest):
-    x_refs = rest[: len(PIECES)]
-    out_ref, gram, gram_low, state, factor, ordered = rest[len(PIECES) :]
+    x_refs = rest[:WHOLE]
+    halves = (rest[WHOLE : WHOLE + 2], rest[WHOLE + 2 : WHOLE + 4])
+    out_ref, gram, gram_low, state, factor, ordered = rest[WHOLE + 4 :]
     grams = (ga_ref, gb_ref)
     y = y_ref[0]
 
-    if True:
-        diagonal = lax.broadcasted_iota(jnp.int32, (128, 128), 0) == lax.broadcasted_iota(
-            jnp.int32, (128, 128), 1
-        )
-
-        def block(k, row, b):
-            return grams[k][:, row, :, b * 128 : (b + 1) * 128].reshape(128, 128)
-
-        trace = jnp.zeros((128, 128), F32)
-        for k in range(2):
-            for row in range(4):
-                trace += jnp.where(diagonal, block(k, row, 0), 0.0)
-        energy = jnp.sum(jnp.sum(trace, axis=0, keepdims=True), axis=1, keepdims=True)
-        square = NV / (4 * (energy + 1e-06))
-
-        def put(at_row, at_col, value):
-            high, low = split(value)
-            rows, cols = slice(at_row * 128, at_row * 128 + 128), slice(at_col * 128, at_col * 128 + 128)
-            gram[rows, cols] = high
-            gram_low[rows, cols] = low
-
-        for k in range(2):
-            for row in range(4):
-                here = 4 * k + row
-                after, before = (row + 1) % 4, (row + 3) % 4
-                side = k if row < 2 else 1 - k
-                put(here, here, block(k, row, 0) * square)
-                put(here, 4 * (1 - k) + row, block(k, row, 1) * square)
-                for one, two, b in (
-                    (here, 4 * k + after, 2),
-                    (here, 4 * (1 - k) + after, 3),
-                    (4 * k + before, 4 * side + after, 4),
-                ):
-                    value = block(k, row, b) * square
-                    put(one, two, value)
-                    put(two, one, value.T)
-
-        mine = pl.ds(pl.multiple_of(y * 128, 128), 128)
-        column = lax.broadcasted_iota(jnp.int32, (128, NV), 1) - y * 128
-        unit = (column == lax.broadcasted_iota(jnp.int32, (128, NV), 0)).astype(F32)
-        state[0] = 1.5 * unit - 0.5 * (gram[mine, :].astype(F32) + gram_low[mine, :].astype(F32))
-
-        @pl.loop(0, 12)
-        def _(step):
-            current = state[0]
-            for at, slot in KEEP.items():
-
-                @pl.when(step == at)
-                def _():
-                    state[slot] = current
-
-            slot = jnp.int32(0)
-            for at, value in BASE.items():
-                slot = jnp.where(step == at, value, slot)
-            high, low = split(current)
-            twice = mm(jnp.concatenate([high, low], axis=0), gram[...])
-            product = (twice[:128] + twice[128:]) + mm(high, gram_low[...])
-            state[0] = 1.5 * state[slot] - 0.5 * product
-
-        scale = jnp.sqrt(square) * math.sqrt(total_rows)
-        high, low = split(state[0].T * scale)
-        factor[:, :128] = high
-        factor[:, 128:] = low
+    diagonal = lax.broadcasted_iota(jnp.int32, (128, 128), 0) == lax.broadcasted_iota(
+        jnp.int32, (128, 128), 1
+    )
+
+    def block(k, row, b):
+        return grams[k][:, row, :, b * 128 : (b + 1) * 128].reshape(128, 128)
+
+    trace = jnp.zeros((128, 128), F32)
+    for k in range(2):
+        for row in range(4):
+            trace += jnp.where(diagonal, block(k, row, 0), 0.0)
+    energy = jnp.sum(jnp.sum(trace, axis=0, keepdims=True), axis=1, keepdims=True)
+    square = NV / (4 * (energy + 1e-06))
+
+    def put(at_row, at_col, value):
+        high, low = split(value)
+        rows, cols = slice(at_row * 128, at_row * 128 + 128), slice(at_col * 128, at_col * 128 + 128)
+        gram[rows, cols] = high
+        gram_low[rows, cols] = low
+
+    for k in range(2):
+        for row in range(4):
+            here = 4 * k + row
+            after, before = (row + 1) % 4, (row + 3) % 4
+            side = k if row < 2 else 1 - k
+            put(here, here, block(k, row, 0) * square)
+            put(here, 4 * (1 - k) + row, block(k, row, 1) * square)
+            for one, two, b in (
+                (here, 4 * k + after, 2),
+                (here, 4 * (1 - k) + after, 3),
+                (4 * k + before, 4 * side + after, 4),
+            ):
+                value = block(k, row, b) * square
+                put(one, two, value)
+                put(two, one, value.T)
+
+    mine = pl.ds(pl.multiple_of(y * 128, 128), 128)
+    column = lax.broadcasted_iota(jnp.int32, (128, NV), 1) - y * 128
+    unit = (column == lax.broadcasted_iota(jnp.int32, (128, NV), 0)).astype(F32)
+    state[0] = 1.5 * unit - 0.5 * (gram[mine, :].astype(F32) + gram_low[mine, :].astype(F32))
+
+    @pl.loop(0, 12)
+    def _(step):
+        current = state[0]
+        for at, slot in KEEP.items():
+
+            @pl.when(step == at)
+            def _():
+                state[slot] = current
+
+        slot = jnp.int32(0)
+        for at, value in BASE.items():
+            slot = jnp.where(step == at, value, slot)
+        high, low = split(current)
+        twice = mm(jnp.concatenate([high, low], axis=0), gram[...])
+        product = (twice[:128] + twice[128:]) + mm(high, gram_low[...])
+        state[0] = 1.5 * state[slot] - 0.5 * product
+
+    scale = jnp.sqrt(square) * math.sqrt(total_rows)
+    high, low = split(state[0].T * scale)
+    factor[:, :128] = high
+    factor[:, 128:] = low
 
     rhs = jnp.concatenate(
         [
@@ -230,12 +256,16 @@
     )
     ordered[...] = rhs
     chunk = 256
-
-    @pl.loop(0, out_ref.shape[0] // chunk)
-    def _(step):
-        rows = pl.ds(pl.multiple_of(step * chunk, chunk), chunk)
-        lhs = jnp.concatenate([ref[rows, :] for ref in x_refs], axis=1)
-        out_ref[rows, :] = fold(mm(jnp.concatenate(split(lhs), axis=0), ordered[...]))
+    half = out_ref.shape[0] // 2
+    for part in range(2):
+
+        @pl.loop(0, half // chunk)
+        def _(step):
+            within = pl.ds(pl.multiple_of(step * chunk, chunk), chunk)
+            rows = pl.ds(pl.multiple_of(part * half + step * chunk, chunk), chunk)
+            parts = [ref[rows, :] for ref in x_refs] + [ref[part][within, :] for ref in halves]
+            lhs = jnp.concatenate(split(jnp.concatenate(parts, axis=1)), axis=0)
+            out_ref[rows, :] = fold(mm(lhs, ordered[...]))
 
 
 def finish(total_rows, y, gram_a, gram_b, pieces):
@@ -260,7 +290,7 @@
 
 def on_device(vectors, hamiltonian, column_blocks, live_counts, lower_bound, upper_bound):
     rows_dev, panel_cols = vectors.shape
-    block_rows, slot_count, block_size, unused_size = hamiltonian.shape
+    block_rows, slot_count, block_size, _ = hamiltonian.shape
     row_count, vec_count = lax.axis_size("row"), lax.axis_size("vec")
     first_row = lax.axis_index("row") * block_rows
     local = (column_blocks - first_row + block_rows) % (block_rows * row_count)
@@ -291,11 +321,16 @@
     own = second.reshape(rows_dev, panel_cols)
 
     half = rows_dev // 2
-    up, down = from_y(own, 1), from_y(own, -1)
-    across = jnp.concatenate([from_y(up[:half], 1), from_y(down[half:], -1)], axis=0)
-    pieces = (own, swap(own), up, swap(up), down, swap(down), across, swap(across))
-
-    share = gram_share(y, pieces[:5])
+    up = from_y(own, 1)
+    down = from_y(own, -1)
+    own_s = swap(own)
+    up_s = swap(up)
+    down_s = swap(down)
+    across, across_s = [], []
+    for part, source, step in ((0, up[:half], 1), (1, down[half:], -1)):
+        across.append(from_y(source, step))
+        across_s.append(swap(across[-1]))
+    share = gram_share(y, (own, own_s, up, up_s, down))
     strip = share.shape[0] // row_count
     parts = lax.all_to_all(
         share.reshape(row_count, strip, -1), "row", split_axis=0, concat_axis=0, tiled=True
@@ -315,11 +350,13 @@
         axis_index_groups=groups,
     ).reshape(row_count, vec_count // 2, strip, -1)
     gram_b = swap(gram_a)
+    pieces = (own, own_s, up, up_s, down, down_s, *across, *across_s)
     return finish(rows_dev * row_count, y, gram_a, gram_b, pieces)
 
 
 def solution(mesh):
     placed = (P("row", "vec"), P("row", None, None, None), P("row", None), P("row"), P(), P())
+
     return jax.shard_map(
         on_device, mesh=mesh, in_specs=placed, out_specs=P("row", "vec"), check_vma=False
     )

time: 188 us -> 189 us (level)
  blocking collectives: 11.1 us -> 38.1 us
  local copies, waits for them, and re-layouts: 9.66 us -> 0.25 us
  Pallas kernels: 56.5 us -> 47.2 us
  starting transfers between devices: 31.1 us -> 24.6 us
    all_to_all x0 -> x1, blocking collectives: none -> 27 us  [on_device(): lax.all_to_all(jnp.broadcast_to(part[None], (members,) + part.shape), ('r...]
    all_to_all x1 -> x0, waiting for transfers between devices: 15.6 us -> none  [on_device(): lax.all_to_all(jnp.broadcast_to(part[None], (members,) + part.shape), ('r...]
    ppermute x4, waiting for transfers between devices: 34.3 us -> 43.7 us  [from_row(): lax.ppermute(value, 'row', [((i + step) % row_count, i) for i in range(ro...]
    pallas_call x1, Pallas kernels: 15.7 us -> 6.37 us  [split_blocks(): pl.pallas_call(split_kernel, out_shape=jax.ShapeDtypeStruct((block_rows,...]
    all_to_all x1 -> x0, starting transfers between devices: 7.84 us -> none  [on_device(): lax.all_to_all(jnp.broadcast_to(part[None], (members,) + part.shape), ('r...]
    ppermute x4, waiting for transfers between devices: 22 us -> 28.2 us  [from_y(): lax.ppermute(value, 'vec', [((i + 2 * step) % vec_count, i) for i in rang...]
    unnamed x5 -> x2, local copies, waits for them, and re-layouts: 5.66 us -> 0.01 us
    ppermute x5 -> x6, starting transfers between devices: 10 us -> 10.7 us  [swap(): return lax.ppermute(value, 'vec', [(i, i ^ 1) for i in range(vec_count)])]
  transfers between devices with their start and end apart: 14 -> 14, of which waited for: 10 -> 9; matrix products, arithmetic and copies ran while one was open for 3% -> 1% of each run, Pallas kernels for 8% -> 3%
where the time goes in v2:
time: 189 us
  waiting for transfers between devices  76.6 us (41%)
  Pallas kernels  47.2 us (25%)
  blocking collectives  38.1 us (20%)
  starting transfers between devices  24.6 us (13%)
    ppermute x4, waiting for transfers between devices, from_row(): lax.ppermute(value, 'row', [((i + step) % row_count, i) for i in range(ro...  43.7 us
    ppermute x4, waiting for transfers between devices, from_y(): lax.ppermute(value, 'vec', [((i + 2 * step) % vec_count, i) for i in rang...  28.2 us
    all_to_all x1, blocking collectives, on_device(): lax.all_to_all(jnp.broadcast_to(part[None], (members,) + part.shape), ('r...  27 us
    pallas_call x1, Pallas kernels, finish(): pl.pallas_call(functools.partial(finish_kernel, total_rows), out_shape=ja...  21.2 us
    pallas_call x2, Pallas kernels, apply_field(): pl.pallas_call(functools.partial(field_kernel, second), out_shape=jax.Sha...  15 us
    all_to_all x1, blocking collectives, on_device(): lax.all_to_all(share.reshape(row_count, strip, -1), 'row', split_axis=0,...  11.1 us
    ppermute x6, starting transfers between devices, swap(): return lax.ppermute(value, 'vec', [(i, i ^ 1) for i in range(vec_count)])  10.7 us
    ppermute x4, starting transfers between devices, from_row(): lax.ppermute(value, 'row', [((i + step) % row_count, i) for i in range(ro...  8.31 us
  transfers between devices with their start and end apart: 14, of which 9 were waited for; matrix products, arithmetic and copies ran while one was open for 1% of the time, Pallas kernels for 3%

profile of v2, /device:TPU:1, one launch (start us, length us, event | category | flops | bytes accessed | tf_op | source)
XLA Modules:
  0.0 189.0 jit_solution(15159126686132472264)
XLA Ops:
  0.0 6.8 %collective-permute-start.1 = (f32[16,128,128]{2,1,0:T(8,128)}, f32[16,128,128]{2,1,0:T(8,128)S(1)}, u32[]{:S(2)}, u32[]{:S(2)}) collective-permute-start(f32[16,128,128]{2,1,0:T(8,128)} %bitcast.5), channel_id=1, source_target_pairs={{8,0},{16,8},{24,16},{32,24},{40,32},{48,40},{56,48},{64,56},{72,6... | collective-permute-start | bytes 3145736 | tf_op jit(solution)/shard_map/ppermute | solution.py:305
  6.8 0.0 collective-permute-start
  8.1 0.8 fusion.2
  8.8 0.1 reshape.27.cols_ref
  8.9 0.0 copy-start
  9.0 6.4 %split_blocks.1.h_ref = bf16[16,12,256,128]{3,2,1,0:T(8,128)(2,1)S(1)} custom-call(f32[16,12,128,128]{3,2,1,0:T(8,128)} %h_ref.1), custom_call_target="tpu_custom_call" | custom-call | bytes 25165824 | tf_op jit(solution)/shard_map/split_blocks/pallas_call | solution.py:65
  15.4 0.1 pad_maximum_fusion.coef_ref
  15.4 13.5 %collective-permute-done.1.right_ref = f32[16,128,128]{2,1,0:T(8,128)S(1)} collective-permute-done((f32[16,128,128]{2,1,0:T(8,128)}, f32[16,128,128]{2,1,0:T(8,128)S(1)}, u32[]{:S(2)}, u32[]{:S(2)}) %collective-permute-start.1) | collective-permute-done | bytes 1048608 | tf_op jit(solution)/shard_map/ppermute | solution.py:305
  28.9 5.1 %collective-permute-done.left_ref = f32[16,128,128]{2,1,0:T(8,128)S(1)} collective-permute-done((f32[16,128,128]{2,1,0:T(8,128)}, f32[16,128,128]{2,1,0:T(8,128)S(1)}, u32[]{:S(2)}, u32[]{:S(2)}) %collective-permute-start) | collective-permute-done | bytes 1048608 | tf_op jit(solution)/shard_map/ppermute | solution.py:305
  34.1 0.0 copy-done
  34.1 7.5 %field.2.own_ref = f32[16,128,128]{2,1,0:T(8,128)S(1)} custom-call(s32[192]{0:T(256)S(1)} %reshape.27.cols_ref, f32[2]{0:T(128)S(1)} %pad_maximum_fusion.coef_ref, bf16[16,12,256,128]{3,2,1,0:T(8,128)(2,1)S(1)} %split_blocks.1.h_ref, f32[16,128,128]{2,1,0:T(8,128)S(1)} %collective-permute-done.left_ref, f32[16,128,128]{2,1,0:T(8,128)S(1)} %bitcast.7, ...), custom_call_target="tpu_custom_call" | custom-call | flops 3221225472 | bytes 12582912 | tf_op jit(solution)/shard_map/field/pallas_call | solution.py:114
  41.6 0.3 collective-permute-start.3
  41.9 1.2 collective-permute-start.2
  43.1 21.4 %collective-permute-done.3.right_ref = f32[16,128,128]{2,1,0:T(8,128)S(1)} collective-permute-done((f32[16,128,128]{2,1,0:T(8,128)S(1)}, f32[16,128,128]{2,1,0:T(8,128)S(1)}, u32[]{:S(2)}, u32[]{:S(2)}) %collective-permute-start.3) | collective-permute-done | bytes 1048608 | tf_op jit(solution)/shard_map/ppermute | solution.py:305
  64.5 3.6 %collective-permute-done.2.left_ref = f32[16,128,128]{2,1,0:T(8,128)S(1)} collective-permute-done((f32[16,128,128]{2,1,0:T(8,128)S(1)}, f32[16,128,128]{2,1,0:T(8,128)S(1)}, u32[]{:S(2)}, u32[]{:S(2)}) %collective-permute-start.2) | collective-permute-done | bytes 1048608 | tf_op jit(solution)/shard_map/ppermute | solution.py:305
  68.1 7.5 %field.3 = f32[16,128,128]{2,1,0:T(8,128)S(1)} custom-call(s32[192]{0:T(256)S(1)} %reshape.27.cols_ref, f32[2]{0:T(128)S(1)} %pad_maximum_fusion.coef_ref, bf16[16,12,256,128]{3,2,1,0:T(8,128)(2,1)S(1)} %split_blocks.1.h_ref, f32[16,128,128]{2,1,0:T(8,128)S(1)} %collective-permute-done.2.left_ref, f32[16,128,128]{2,1,0:T(8,128)S(1)} %field.2.own_ref, ...), custom_call_target="tpu_custom_call" | custom-call | flops 3221225472 | bytes 12582912 | tf_op jit(solution)/shard_map/field/pallas_call | solution.py:114
  75.7 2.8 %collective-permute-start.5 = (f32[2048,128]{1,0:T(8,128)S(1)}, f32[2048,128]{1,0:T(8,128)S(1)}, u32[]{:S(2)}, u32[]{:S(2)}) collective-permute-start(f32[2048,128]{1,0:T(8,128)S(1)} %bitcast.9), channel_id=1, source_target_pairs={{2,0},{3,1},{4,2},{5,3},{6,4},{7,5},{0,6},{1,7},{10,8},{11,9},{12,... | collective-permute-start | bytes 3145736 | tf_op jit(solution)/shard_map/ppermute | solution.py:308
  78.5 0.0 collective-permute-start.7
  78.5 2.9 %collective-permute-start.4 = (f32[2048,128]{1,0:T(8,128)S(1)}, f32[2048,128]{1,0:T(8,128)}, u32[]{:S(2)}, u32[]{:S(2)}) collective-permute-start(f32[2048,128]{1,0:T(8,128)S(1)} %bitcast.11), channel_id=1, source_target_pairs={{0,1},{1,0},{2,3},{3,2},{4,5},{5,4},{6,7},{7,6},{8,9},{9,8},{10,11... | collective-permute-start | bytes 3145736 | tf_op jit(solution)/shard_map/ppermute | solution.py:313
  81.4 16.9 %collective-permute-done.5.u_ref.rest_2_ = f32[2048,128]{1,0:T(8,128)S(1)} collective-permute-done((f32[2048,128]{1,0:T(8,128)S(1)}, f32[2048,128]{1,0:T(8,128)S(1)}, u32[]{:S(2)}, u32[]{:S(2)}) %collective-permute-start.5) | collective-permute-done | bytes 1048608 | tf_op jit(solution)/shard_map/ppermute | solution.py:308
  98.3 3.5 %collective-permute-start.6 = (f32[2048,128]{1,0:T(8,128)S(1)}, f32[2048,128]{1,0:T(8,128)}, u32[]{:S(2)}, u32[]{:S(2)}) collective-permute-start(f32[2048,128]{1,0:T(8,128)S(1)} %collective-permute-done.5.u_ref.rest_2_), channel_id=1, source_target_pairs={{0,1},{1,0},{2,3},{3,2},{4,5},{5,4},{6,7},{7,6},{8,9},{9,8},{10,11... | collective-permute-start | bytes 3145736 | tf_op jit(solution)/shard_map/ppermute | solution.py:313
  101.8 0.0 collective-permute-done.7.d_ref.rest_4_
  101.8 0.0 collective-permute-done.4.s_ref.rest_1_
  101.8 2.4 %collective-permute-done.6.us_ref.rest_3_ = f32[2048,128]{1,0:T(8,128)} collective-permute-done((f32[2048,128]{1,0:T(8,128)S(1)}, f32[2048,128]{1,0:T(8,128)}, u32[]{:S(2)}, u32[]{:S(2)}) %collective-permute-start.6) | collective-permute-done | bytes 1048608 | tf_op jit(solution)/shard_map/ppermute | solution.py:313
  104.2 4.6 %gram_share.1 = f32[128,640]{1,0:T(8,128)S(1)} custom-call(s32[1]{0:T(128)} %bitcast.y_ref, f32[2048,128]{1,0:T(8,128)S(1)} %bitcast.12, f32[2048,128]{1,0:T(8,128)} %collective-permute-done.4.s_ref.rest_1_, f32[2048,128]{1,0:T(8,128)S(1)} %collective-permute-done.5.u_ref.rest_2_, f32[2048,128]{1,0:T(8,128)} %collective-permute-done.6.us_ref.rest_3_, ...), custom_call_target="tpu_custom_call" | custom-call | flops 1342177280 | bytes 5242880 | tf_op jit(solution)/shard_map/gram_share/pallas_call | solution.py:162
  108.9 11.1 %all_to_all.10 = f32[16,8,640]{2,1,0:T(8,128)S(1)} all-to-all(f32[16,8,640]{2,1,0:T(8,128)S(1)} %bitcast.14), channel_id=1, replica_groups=mesh['row'=16,'vec'=8] {'row'}, dimensions={0} | all-to-all | bytes 655360 | tf_op jit(solution)/shard_map/all_to_all | solution.py:335
  120.0 0.1 broadcast_in_dim.17
  120.1 27.0 %all_to_all.11 = f32[64,8,640]{2,1,0:T(8,128)S(1)} all-to-all(f32[64,8,640]{2,1,0:T(8,128)S(1)} %broadcast_in_dim.17), channel_id=1, replica_groups={{0,2,4,6,8,10,12,14,16,18,20,22,24,26,28,30,32,34,36,38,40,42,44,46,48,..., dimensions={0} | all-to-all | bytes 2621440 | tf_op jit(solution)/shard_map/all_to_all | solution.py:344
  147.1 2.8 %collective-permute-start.8 = (f32[16,4,8,640]{3,2,1,0:T(8,128)S(1)}, f32[16,4,8,640]{3,2,1,0:T(8,128)S(1)}, u32[]{:S(2)}, u32[]{:S(2)}) collective-permute-start(f32[16,4,8,640]{3,2,1,0:T(8,128)S(1)} %bitcast.15), channel_id=1, source_target_pairs={{0,1},{1,0},{2,3},{3,2},{4,5},{5,4},{6,7},{7,6},{8,9},{9,8},{10,11... | collective-permute-start | bytes 3932168 | tf_op jit(solution)/shard_map/ppermute | solution.py:313
  149.9 0.6 collective-permute-start.11
  150.5 2.2 %collective-permute-start.10 = (f32[1024,128]{1,0:T(8,128)S(1)}, f32[1024,128]{1,0:T(8,128)S(1)}, u32[]{:S(2)}, u32[]{:S(2)}) collective-permute-start(f32[1024,128]{1,0:T(8,128)S(1)} %slice.8), channel_id=1, source_target_pairs={{2,0},{3,1},{4,2},{5,3},{6,4},{7,5},{0,6},{1,7},{10,8},{11,9},{12,... | collective-permute-start | bytes 1572872 | tf_op jit(solution)/shard_map/ppermute | solution.py:308
  152.8 0.6 collective-permute-start.9
  153.3 11.3 %collective-permute-done.11.rest_7_ = f32[1024,128]{1,0:T(8,128)S(1)} collective-permute-done((f32[1024,128]{1,0:T(8,128)S(1)}, f32[1024,128]{1,0:T(8,128)S(1)}, u32[]{:S(2)}, u32[]{:S(2)}) %collective-permute-start.11) | collective-permute-done | bytes 524320 | tf_op jit(solution)/shard_map/ppermute | solution.py:308
  164.7 0.9 collective-permute-start.13
  165.5 0.0 collective-permute-done.10.rest_6_
  165.5 0.0 collective-permute-start.12
  165.5 1.5 collective-permute-done.13.rest_9_
  167.1 0.7 collective-permute-done.12.rest_8_
  167.8 0.0 collective-permute-done.9.rest_5_
  167.8 0.0 collective-permute-done.8.gb_ref
  167.8 21.2 %finish.1 = f32[2048,128]{1,0:T(8,128)} custom-call(s32[1]{0:T(128)} %bitcast.y_ref, f32[16,4,8,640]{3,2,1,0:T(8,128)S(1)} %bitcast.16, f32[16,4,8,640]{3,2,1,0:T(8,128)S(1)} %collective-permute-done.8.gb_ref, f32[2048,128]{1,0:T(8,128)S(1)} %bitcast.13, f32[2048,128]{1,0:T(8,128)} %collective-permute-done.4.s_ref.rest_1_, ...), custom_call_target="tpu_custom_call" | custom-call | flops 9663676416 | bytes 9437184 | tf_op jit(solution)/shard_map/finish/pallas_call | solution.py:273
  (3 shorter events, 0.1 us)
Async XLA Ops:
  0.0 28.9 %collective-permute-start.1 = (f32[16,128,128]{2,1,0:T(8,128)}, f32[16,128,128]{2,1,0:T(8,128)S(1)}, u32[]{:S(2)}, u32[]{:S(2)}) collective-permute-start(f32[16,128,128]{2,1,0:T(8,128)} %bitcast.5), channel_id=1, source_target_pairs={{8,0},{16,8},{24,16},{32,24},{40,32},{48,40},{56,48},{64,56},{72,6... | collective-permute-start | bytes 3145736 | tf_op jit(solution)/shard_map/ppermute | solution.py:305
  6.8 27.3 %collective-permute-start = (f32[16,128,128]{2,1,0:T(8,128)}, f32[16,128,128]{2,1,0:T(8,128)S(1)}, u32[]{:S(2)}, u32[]{:S(2)}) collective-permute-start(f32[16,128,128]{2,1,0:T(8,128)} %bitcast.6), channel_id=1, source_target_pairs={{120,0},{0,8},{8,16},{16,24},{24,32},{32,40},{40,48},{48,56},{56,6... | collective-permute-start | bytes 3145736 | tf_op jit(solution)/shard_map/ppermute | solution.py:305
  8.9 25.1 %copy-start = (f32[2048,128]{1,0:T(8,128)S(1)}, f32[2048,128]{1,0:T(8,128)}, u32[]{:S(2)}) copy-start(f32[2048,128]{1,0:T(8,128)} %param.6) | copy-start | bytes 3145732
  41.6 23.0 %collective-permute-start.3 = (f32[16,128,128]{2,1,0:T(8,128)S(1)}, f32[16,128,128]{2,1,0:T(8,128)S(1)}, u32[]{:S(2)}, u32[]{:S(2)}) collective-permute-start(f32[16,128,128]{2,1,0:T(8,128)S(1)} %field.2.own_ref), channel_id=1, source_target_pairs={{8,0},{16,8},{24,16},{32,24},{40,32},{48,40},{56,48},{64,56},{72,6... | collective-permute-start | bytes 3145736 | tf_op jit(solution)/shard_map/ppermute | solution.py:305
  41.9 26.2 %collective-permute-start.2 = (f32[16,128,128]{2,1,0:T(8,128)S(1)}, f32[16,128,128]{2,1,0:T(8,128)S(1)}, u32[]{:S(2)}, u32[]{:S(2)}) collective-permute-start(f32[16,128,128]{2,1,0:T(8,128)S(1)} %field.2.own_ref), channel_id=1, source_target_pairs={{120,0},{0,8},{8,16},{16,24},{24,32},{32,40},{40,48},{48,56},{56,6... | collective-permute-start | bytes 3145736 | tf_op jit(solution)/shard_map/ppermute | solution.py:305
  75.7 22.6 %collective-permute-start.5 = (f32[2048,128]{1,0:T(8,128)S(1)}, f32[2048,128]{1,0:T(8,128)S(1)}, u32[]{:S(2)}, u32[]{:S(2)}) collective-permute-start(f32[2048,128]{1,0:T(8,128)S(1)} %bitcast.9), channel_id=1, source_target_pairs={{2,0},{3,1},{4,2},{5,3},{6,4},{7,5},{0,6},{1,7},{10,8},{11,9},{12,... | collective-permute-start | bytes 3145736 | tf_op jit(solution)/shard_map/ppermute | solution.py:308
  78.5 23.4 %collective-permute-start.7 = (f32[2048,128]{1,0:T(8,128)S(1)}, f32[2048,128]{1,0:T(8,128)S(1)}, u32[]{:S(2)}, u32[]{:S(2)}) collective-permute-start(f32[2048,128]{1,0:T(8,128)S(1)} %bitcast.10), channel_id=1, source_target_pairs={{6,0},{7,1},{0,2},{1,3},{2,4},{3,5},{4,6},{5,7},{14,8},{15,9},{8,1... | collective-permute-start | bytes 3145736 | tf_op jit(solution)/shard_map/ppermute | solution.py:308
  78.5 23.4 %collective-permute-start.4 = (f32[2048,128]{1,0:T(8,128)S(1)}, f32[2048,128]{1,0:T(8,128)}, u32[]{:S(2)}, u32[]{:S(2)}) collective-permute-start(f32[2048,128]{1,0:T(8,128)S(1)} %bitcast.11), channel_id=1, source_target_pairs={{0,1},{1,0},{2,3},{3,2},{4,5},{5,4},{6,7},{7,6},{8,9},{9,8},{10,11... | collective-permute-start | bytes 3145736 | tf_op jit(solution)/shard_map/ppermute | solution.py:313
  98.3 5.9 %collective-permute-start.6 = (f32[2048,128]{1,0:T(8,128)S(1)}, f32[2048,128]{1,0:T(8,128)}, u32[]{:S(2)}, u32[]{:S(2)}) collective-permute-start(f32[2048,128]{1,0:T(8,128)S(1)} %collective-permute-done.5.u_ref.rest_2_), channel_id=1, source_target_pairs={{0,1},{1,0},{2,3},{3,2},{4,5},{5,4},{6,7},{7,6},{8,9},{9,8},{10,11... | collective-permute-start | bytes 3145736 | tf_op jit(solution)/shard_map/ppermute | solution.py:313
  147.1 20.8 %collective-permute-start.8 = (f32[16,4,8,640]{3,2,1,0:T(8,128)S(1)}, f32[16,4,8,640]{3,2,1,0:T(8,128)S(1)}, u32[]{:S(2)}, u32[]{:S(2)}) collective-permute-start(f32[16,4,8,640]{3,2,1,0:T(8,128)S(1)} %bitcast.15), channel_id=1, source_target_pairs={{0,1},{1,0},{2,3},{3,2},{4,5},{5,4},{6,7},{7,6},{8,9},{9,8},{10,11... | collective-permute-start | bytes 3932168 | tf_op jit(solution)/shard_map/ppermute | solution.py:313
  149.9 14.8 %collective-permute-start.11 = (f32[1024,128]{1,0:T(8,128)S(1)}, f32[1024,128]{1,0:T(8,128)S(1)}, u32[]{:S(2)}, u32[]{:S(2)}) collective-permute-start(f32[1024,128]{1,0:T(8,128)S(1)} %slice.9), channel_id=1, source_target_pairs={{6,0},{7,1},{0,2},{1,3},{2,4},{3,5},{4,6},{5,7},{14,8},{15,9},{8,1... | collective-permute-start | bytes 1572872 | tf_op jit(solution)/shard_map/ppermute | solution.py:308
  150.5 15.0 %collective-permute-start.10 = (f32[1024,128]{1,0:T(8,128)S(1)}, f32[1024,128]{1,0:T(8,128)S(1)}, u32[]{:S(2)}, u32[]{:S(2)}) collective-permute-start(f32[1024,128]{1,0:T(8,128)S(1)} %slice.8), channel_id=1, source_target_pairs={{2,0},{3,1},{4,2},{5,3},{6,4},{7,5},{0,6},{1,7},{10,8},{11,9},{12,... | collective-permute-start | bytes 1572872 | tf_op jit(solution)/shard_map/ppermute | solution.py:308
  152.8 15.1 %collective-permute-start.9 = (f32[2048,128]{1,0:T(8,128)S(1)}, f32[2048,128]{1,0:T(8,128)S(1)}, u32[]{:S(2)}, u32[]{:S(2)}) collective-permute-start(f32[2048,128]{1,0:T(8,128)S(1)} %collective-permute-done.7.d_ref.rest_4_), channel_id=1, source_target_pairs={{0,1},{1,0},{2,3},{3,2},{4,5},{5,4},{6,7},{7,6},{8,9},{9,8},{10,11... | collective-permute-start | bytes 3145736 | tf_op jit(solution)/shard_map/ppermute | solution.py:313
  164.7 2.4 %collective-permute-start.13 = (f32[1024,128]{1,0:T(8,128)S(1)}, f32[1024,128]{1,0:T(8,128)S(1)}, u32[]{:S(2)}, u32[]{:S(2)}) collective-permute-start(f32[1024,128]{1,0:T(8,128)S(1)} %collective-permute-done.11.rest_7_), channel_id=1, source_target_pairs={{0,1},{1,0},{2,3},{3,2},{4,5},{5,4},{6,7},{7,6},{8,9},{9,8},{10,11... | collective-permute-start | bytes 1572872 | tf_op jit(solution)/shard_map/ppermute | solution.py:313
  165.5 2.3 %collective-permute-start.12 = (f32[1024,128]{1,0:T(8,128)S(1)}, f32[1024,128]{1,0:T(8,128)S(1)}, u32[]{:S(2)}, u32[]{:S(2)}) collective-permute-start(f32[1024,128]{1,0:T(8,128)S(1)} %collective-permute-done.10.rest_6_), channel_id=1, source_target_pairs={{0,1},{1,0},{2,3},{3,2},{4,5},{5,4},{6,7},{7,6},{8,9},{9,8},{10,11... | collective-permute-start | bytes 1572872 | tf_op jit(solution)/shard_map/ppermute | solution.py:313

commit v3 on v2

--- a/solution.py
+++ b/solution.py
@@ -81,28 +81,74 @@
 VMEM_SPEC = pl.BlockSpec(memory_space=pltpu.VMEM)
 
 
+CHUNKS = 2
+
+
+def lanes_low(shape):
+    return lax.broadcasted_iota(jnp.int32, shape, 1) < shape[1] // 2
+
+
+def turn(x):
+    return pltpu.roll(x, x.shape[1] // 2, 1)
+
+
+def pack_kernel(v_ref, a_ref, b_ref):
+    low = lanes_low(v_ref.shape[1:])
+    half = a_ref.shape[0]
+
+    @pl.loop(0, half)
+    def _(j):
+        one, two = v_ref[j], v_ref[j + half]
+        a_ref[j] = jnp.where(low, one, turn(two))
+        b_ref[j] = jnp.where(low, turn(one), two)
+
+
+def pack(blocks):
+    count, size, cols = blocks.shape
+    shape = jax.ShapeDtypeStruct((count // 2, size, cols), F32)
+    return pl.pallas_call(
+        pack_kernel,
+        out_shape=(shape, shape),
+        in_specs=[VMEM_SPEC],
+        out_specs=(VMEM_SPEC, VMEM_SPEC),
+        compiler_params=pltpu.CompilerParams(vmem_limit_bytes=30 * 2**20),
+        cost_estimate=cost(0, 8 * blocks.size),
+        name="pack",
+    )(blocks)
+
+
 def field_kernel(second, cols_ref, coef_ref, h_ref, left_ref, own_ref, right_ref, *rest):
     if second:
         prev_ref, o_ref, wide = rest
     else:
         o_ref, wide = rest
     count, slots = h_ref.shape[:2]
+    half = count // 2
+    low = lanes_low(own_ref.shape[1:])
     for part, ref in enumerate((left_ref, own_ref, right_ref)):
 
-        @pl.loop(0, count)
+        @pl.loop(0, half)
         def _(j):
-            high, low = split(ref[j])
-            wide[part * count + j, :, :128] = high
-            wide[part * count + j, :, 128:] = low
+            value = ref[j]
+            high = value.astype(BF).astype(F32)
+            rest_of = value - high
+            wide[part * count + j] = jnp.where(low, high, turn(rest_of)).astype(BF)
+            wide[part * count + half + j] = jnp.where(low, turn(high), rest_of).astype(BF)
 
     wide[3 * count] = jnp.zeros(wide.shape[1:], BF)
     centre, inverse = coef_ref[0], coef_ref[1]
 
-    @pl.loop(0, count)
-    def _(i):
+    def row(i):
         lhs = jnp.concatenate([h_ref[i, k] for k in range(slots)], axis=1)
         rhs = jnp.concatenate([wide[cols_ref[i * slots + k]] for k in range(slots)], axis=0)
-        result = (fold(mm(lhs, rhs)) - centre * own_ref[i]) * inverse
+        full = mm(lhs, rhs)
+        full = full[: full.shape[0] // 2] + full[full.shape[0] // 2 :]
+        return full + turn(full)
+
+    @pl.loop(0, half)
+    def _(i):
+        summed = jnp.where(low, row(i), row(i + half))
+        result = (summed - centre * own_ref[i]) * inverse
         if second:
             result = 2.0 * result - prev_ref[i]
         o_ref[i] = result
@@ -113,74 +159,82 @@
     operands = [split_h, left, own, right] + ([prev] if second else [])
     return pl.pallas_call(
         functools.partial(field_kernel, second),
-        out_shape=jax.ShapeDtypeStruct((block_rows, size, size), F32),
+        out_shape=jax.ShapeDtypeStruct(own.shape, F32),
         in_specs=[SMEM_SPEC] * 2 + [VMEM_SPEC] * len(operands),
         out_specs=VMEM_SPEC,
-        scratch_shapes=[pltpu.VMEM((3 * block_rows + 1, size, 2 * size), BF)],
+        scratch_shapes=[pltpu.VMEM((3 * block_rows + 1, size, size), BF)],
         compiler_params=pltpu.CompilerParams(vmem_limit_bytes=30 * 2**20),
         cost_estimate=cost(8 * block_rows * slots * size**3, 2 * split_h.size),
         name="field",
     )(cols, coef, *operands)
 
 
+def natural(refs, rows, part):
+    a, b = (ref[rows, :] for ref in refs)
+    low = lanes_low(a.shape)
+    return jnp.where(low, turn(a), b) if part else jnp.where(low, a, turn(b))
+
+
 GRAM_BLOCKS = 5
 
 
-def gram_kernel(y_ref, own_ref, s_ref, u_ref, us_ref, d_ref, out_ref, acc):
+def gram_kernel(y_ref, *rest):
+    own, beside, up, up_s, down = (rest[2 * n : 2 * n + 2] for n in range(5))
+    out_ref, acc = rest[10:]
     acc[...] = jnp.zeros_like(acc)
     chunk = 512
-
-    @pl.loop(0, own_ref.shape[0] // chunk)
-    def _(step):
-        rows = pl.ds(pl.multiple_of(step * chunk, chunk), chunk)
-
-        def turned(ref):
-            return jnp.concatenate(split(ref[rows, :].T), axis=0)
-
-        def paired(ref):
-            return jnp.concatenate(split(ref[rows, :]), axis=1)
-
-        lhs = turned(own_ref)
-        for block, ref in enumerate((own_ref, s_ref, u_ref, us_ref)):
-            acc[block] += mm(lhs, paired(ref))
-        lhs = turned(d_ref)
-
-        @pl.when(y_ref[0] < 2)
-        def _():
-            acc[4] += mm(lhs, paired(u_ref))
-
-        @pl.when(y_ref[0] >= 2)
-        def _():
-            acc[4] += mm(lhs, paired(us_ref))
+    for part in range(2):
+
+        @pl.loop(0, own[0].shape[0] // chunk)
+        def _(step):
+            rows = pl.ds(pl.multiple_of(step * chunk, chunk), chunk)
+
+            def turned(refs):
+                return jnp.concatenate(split(natural(refs, rows, part).T), axis=0)
+
+            def paired(refs):
+                return jnp.concatenate(split(natural(refs, rows, part)), axis=1)
+
+            lhs = turned(own)
+            for block, refs in enumerate((own, beside, up, up_s)):
+                acc[block] += mm(lhs, paired(refs))
+            lhs = turned(down)
+
+            @pl.when(y_ref[0] < 2)
+            def _():
+                acc[4] += mm(lhs, paired(up))
+
+            @pl.when(y_ref[0] >= 2)
+            def _():
+                acc[4] += mm(lhs, paired(up_s))
 
     for block in range(GRAM_BLOCKS):
         out_ref[:, block * 128 : (block + 1) * 128] = fold(acc[block])
 
 
 def gram_share(y, pieces):
-    rows, cols = pieces[0].shape
+    operands = [chunk for piece in pieces for chunk in piece]
+    rows, cols = operands[0].shape
     return pl.pallas_call(
         gram_kernel,
         out_shape=jax.ShapeDtypeStruct((cols, GRAM_BLOCKS * cols), F32),
-        in_specs=[SMEM_SPEC] + [VMEM_SPEC] * len(pieces),
+        in_specs=[SMEM_SPEC] + [VMEM_SPEC] * len(operands),
         out_specs=VMEM_SPEC,
         scratch_shapes=[pltpu.VMEM((GRAM_BLOCKS, 2 * cols, 2 * cols), F32)],
         compiler_params=pltpu.CompilerParams(vmem_limit_bytes=30 * 2**20),
-        cost_estimate=cost(8 * rows * cols * cols * GRAM_BLOCKS, 4 * rows * cols * len(pieces)),
+        cost_estimate=cost(16 * rows * cols * cols * GRAM_BLOCKS, 4 * rows * cols * len(operands)),
         name="gram_share",
-    )(y, *pieces)
+    )(y, *operands)
 
 
 KEEP = {0: 1, 3: 2, 4: 1, 8: 1}
 BASE = {2: 1, 6: 1, 10: 1, 11: 2}
 PIECES = ((0, 0), (1, 0), (0, 1), (1, 1), (0, 3), (1, 3), (0, 2), (1, 2))
-WHOLE = 6
 
 
 def finish_kernel(total_rows, y_ref, ga_ref, gb_ref, *rest):
-    x_refs = rest[:WHOLE]
-    halves = (rest[WHOLE : WHOLE + 2], rest[WHOLE + 2 : WHOLE + 4])
-    out_ref, gram, gram_low, state, factor, ordered = rest[WHOLE + 4 :]
+    x_refs = [rest[2 * n : 2 * n + 2] for n in range(len(PIECES))]
+    out_ref, gram, gram_low, state, factor, ordered = rest[2 * len(PIECES) :]
     grams = (ga_ref, gb_ref)
     y = y_ref[0]
 
@@ -263,17 +317,18 @@
         def _(step):
             within = pl.ds(pl.multiple_of(step * chunk, chunk), chunk)
             rows = pl.ds(pl.multiple_of(part * half + step * chunk, chunk), chunk)
-            parts = [ref[rows, :] for ref in x_refs] + [ref[part][within, :] for ref in halves]
+            parts = [natural(refs, within, part) for refs in x_refs]
             lhs = jnp.concatenate(split(jnp.concatenate(parts, axis=1)), axis=0)
             out_ref[rows, :] = fold(mm(lhs, ordered[...]))
 
 
 def finish(total_rows, y, gram_a, gram_b, pieces):
-    rows, cols = pieces[0].shape
+    operands = [chunk for piece in pieces for chunk in piece]
+    rows, cols = 2 * operands[0].shape[0], operands[0].shape[1]
     return pl.pallas_call(
         functools.partial(finish_kernel, total_rows),
         out_shape=jax.ShapeDtypeStruct((rows, cols), F32),
-        in_specs=[SMEM_SPEC] + [VMEM_SPEC] * (2 + len(pieces)),
+        in_specs=[SMEM_SPEC] + [VMEM_SPEC] * (2 + len(operands)),
         out_specs=VMEM_SPEC,
         scratch_shapes=[
             pltpu.VMEM((NV, NV), BF),
@@ -285,7 +340,7 @@
         compiler_params=pltpu.CompilerParams(vmem_limit_bytes=40 * 2**20),
         cost_estimate=cost(12 * 6 * cols * NV * NV, 4 * rows * cols * 9),
         name="finish",
-    )(y, gram_a, gram_b, *pieces)
+    )(y, gram_a, gram_b, *operands)
 
 
 def on_device(vectors, hamiltonian, column_blocks, live_counts, lower_bound, upper_bound):
@@ -312,23 +367,25 @@
     def swap(value):
         return lax.ppermute(value, "vec", [(i, i ^ 1) for i in range(vec_count)])
 
+    blocks = pack(vectors.reshape(block_rows, block_size, panel_cols))
     split_h = split_blocks(hamiltonian)
-    blocks = vectors.reshape(block_rows, block_size, panel_cols)
-    first = apply_field(False, cols, coef, split_h, from_row(blocks, -1), blocks, from_row(blocks, 1))
-    second = apply_field(
-        True, cols, coef, split_h, from_row(first, -1), first, from_row(first, 1), blocks
-    )
-    own = second.reshape(rows_dev, panel_cols)
-
-    half = rows_dev // 2
-    up = from_y(own, 1)
-    down = from_y(own, -1)
-    own_s = swap(own)
-    up_s = swap(up)
-    down_s = swap(down)
-    across, across_s = [], []
-    for part, source, step in ((0, up[:half], 1), (1, down[half:], -1)):
-        across.append(from_y(source, step))
+
+    def applied(second, operand, prev=None):
+        right = from_row(operand, 1)
+        left = from_row(operand, -1)
+        return apply_field(second, cols, coef, split_h, left, operand, right, prev)
+
+    own, own_s, up, up_s, down, down_s, across, across_s = ([] for _ in range(8))
+    for chunk in range(CHUNKS):
+        first = applied(False, blocks[chunk])
+        second = applied(True, first, blocks[chunk])
+        own.append(second.reshape(rows_dev // 2, panel_cols))
+        up.append(from_y(own[-1], 1))
+        down.append(from_y(own[-1], -1))
+        own_s.append(swap(own[-1]))
+        up_s.append(swap(up[-1]))
+        down_s.append(swap(down[-1]))
+        across.append(from_y((up, down)[chunk][-1], (1, -1)[chunk]))
         across_s.append(swap(across[-1]))
     share = gram_share(y, (own, own_s, up, up_s, down))
     strip = share.shape[0] // row_count
@@ -350,7 +407,7 @@
         axis_index_groups=groups,
     ).reshape(row_count, vec_count // 2, strip, -1)
     gram_b = swap(gram_a)
-    pieces = (own, own_s, up, up_s, down, down_s, *across, *across_s)
+    pieces = (own, own_s, up, up_s, down, down_s, across, across_s)
     return finish(rows_dev * row_count, y, gram_a, gram_b, pieces)
 
 

time: 189 us -> 184 us (0.974)
  waiting for transfers between devices: 76.6 us -> 37.3 us
  Pallas kernels: 47.2 us -> 66.1 us
  starting transfers between devices: 24.6 us -> 39.4 us
    ppermute x4 -> x8, waiting for transfers between devices: 43.7 us -> 0.02 us  [from_row(): lax.ppermute(value, 'row', [((i + step) % row_count, i) for i in range(ro...]
    pallas_call x2 -> x4, Pallas kernels: 15 us -> 31.4 us  [apply_field(): pl.pallas_call(functools.partial(field_kernel, second), out_shape=jax.Sha...]
    ppermute x4 -> x8, starting transfers between devices: 8.31 us -> 21.4 us  [from_row(): lax.ppermute(value, 'row', [((i + step) % row_count, i) for i in range(ro...]
    ppermute x4 -> x6, waiting for transfers between devices: 28.2 us -> 35.7 us  [from_y(): lax.ppermute(value, 'vec', [((i + 2 * step) % vec_count, i) for i in rang...]
    all_to_all x1, blocking collectives: 27 us -> 23 us  [on_device(): lax.all_to_all(jnp.broadcast_to(part[None], (members,) + part.shape), ('r...]
    all_to_all x1, blocking collectives: 11.1 us -> 14.3 us  [on_device(): lax.all_to_all(share.reshape(row_count, strip, -1), 'row', split_axis=0,...]
    ppermute x6 -> x9, waiting for transfers between devices: 4.7 us -> 1.55 us  [swap(): return lax.ppermute(value, 'vec', [(i, i ^ 1) for i in range(vec_count)])]
    ppermute x6 -> x9, starting transfers between devices: 10.7 us -> 13.2 us  [swap(): return lax.ppermute(value, 'vec', [(i, i ^ 1) for i in range(vec_count)])]
  transfers between devices with their start and end apart: 14 -> 23, of which waited for: 9 -> 7; matrix products, arithmetic and copies ran while one was open for 1% -> 1% of each run, Pallas kernels for 3% -> 21%
where the time goes in v3:
time: 184 us
  Pallas kernels  66.1 us (36%)
  starting transfers between devices  39.4 us (21%)
  waiting for transfers between devices  37.3 us (20%)
  blocking collectives  37.3 us (20%)
    ppermute x6, waiting for transfers between devices, from_y(): lax.ppermute(value, 'vec', [((i + 2 * step) % vec_count, i) for i in rang...  35.7 us
    pallas_call x4, Pallas kernels, apply_field(): pl.pallas_call(functools.partial(field_kernel, second), out_shape=jax.Sha...  31.4 us
    all_to_all x1, blocking collectives, on_device(): lax.all_to_all(jnp.broadcast_to(part[None], (members,) + part.shape), ('r...  23 us
    pallas_call x1, Pallas kernels, finish(): pl.pallas_call(functools.partial(finish_kernel, total_rows), out_shape=ja...  22 us
    ppermute x8, starting transfers between devices, from_row(): lax.ppermute(value, 'row', [((i + step) % row_count, i) for i in range(ro...  21.4 us
    all_to_all x1, blocking collectives, on_device(): lax.all_to_all(share.reshape(row_count, strip, -1), 'row', split_axis=0,...  14.3 us
    ppermute x9, starting transfers between devices, swap(): return lax.ppermute(value, 'vec', [(i, i ^ 1) for i in range(vec_count)])  13.2 us
    pallas_call x1, Pallas kernels, split_blocks(): pl.pallas_call(split_kernel, out_shape=jax.ShapeDtypeStruct((block_rows,...  6.28 us
  transfers between devices with their start and end apart: 23, of which 7 were waited for; matrix products, arithmetic and copies ran while one was open for 1% of the time, Pallas kernels for 21%

profile of v3, /device:TPU:1, one launch (start us, length us, event | category | flops | bytes accessed | tf_op | source)
XLA Modules:
  0.0 183.8 jit_solution(405013047762327457)
XLA Ops:
  0.0 1.2 copy-done
  1.2 0.8 pack.1
  2.0 2.1 %collective-permute-start = (f32[8,128,128]{2,1,0:T(8,128)S(1)}, f32[8,128,128]{2,1,0:T(8,128)S(1)}, u32[]{:S(2)}, u32[]{:S(2)}) collective-permute-start(f32[8,128,128]{2,1,0:T(8,128)S(1)} %get-tuple-element.7.own_ref.rest_0_), channel_id=1, source_target_pairs={{120,0},{0,8},{8,16},{16,24},{24,32},{32,40},{40,48},{48,56},{56,6... | collective-permute-start | bytes 1572872 | tf_op jit(solution)/shard_map/ppermute | solution.py:360
  4.1 4.8 %collective-permute-start.1 = (f32[8,128,128]{2,1,0:T(8,128)S(1)}, f32[8,128,128]{2,1,0:T(8,128)S(1)}, u32[]{:S(2)}, u32[]{:S(2)}) collective-permute-start(f32[8,128,128]{2,1,0:T(8,128)S(1)} %get-tuple-element.7.own_ref.rest_0_), channel_id=1, source_target_pairs={{8,0},{16,8},{24,16},{32,24},{40,32},{48,40},{56,48},{64,56},{72,6... | collective-permute-start | bytes 1572872 | tf_op jit(solution)/shard_map/ppermute | solution.py:360
  9.0 4.8 %collective-permute-start.5 = (f32[8,128,128]{2,1,0:T(8,128)S(1)}, f32[8,128,128]{2,1,0:T(8,128)S(1)}, u32[]{:S(2)}, u32[]{:S(2)}) collective-permute-start(f32[8,128,128]{2,1,0:T(8,128)S(1)} %get-tuple-element.8.own_ref.rest_0_), channel_id=1, source_target_pairs={{8,0},{16,8},{24,16},{32,24},{40,32},{48,40},{56,48},{64,56},{72,6... | collective-permute-start | bytes 1572872 | tf_op jit(solution)/shard_map/ppermute | solution.py:360
  13.7 0.8 fusion.2
  15.8 0.1 reshape.30.cols_ref
  15.9 6.3 %split_blocks.1.h_ref = bf16[16,12,256,128]{3,2,1,0:T(8,128)(2,1)S(1)} custom-call(f32[16,12,128,128]{3,2,1,0:T(8,128)} %h_ref.1), custom_call_target="tpu_custom_call" | custom-call | bytes 25165824 | tf_op jit(solution)/shard_map/split_blocks/pallas_call | solution.py:65
  22.2 0.1 pad_maximum_fusion.coef_ref
  22.3 0.0 collective-permute-done.left_ref
  22.3 0.0 collective-permute-done.1.right_ref
  22.3 7.8 %field.4.own_ref = f32[8,128,128]{2,1,0:T(8,128)S(1)} custom-call(s32[192]{0:T(256)S(1)} %reshape.30.cols_ref, f32[2]{0:T(128)S(1)} %pad_maximum_fusion.coef_ref, bf16[16,12,256,128]{3,2,1,0:T(8,128)(2,1)S(1)} %split_blocks.1.h_ref, f32[8,128,128]{2,1,0:T(8,128)S(1)} %collective-permute-done.left_ref, f32[8,128,128]{2,1,0:T(8,128)S(1)} %get-tuple-element.7.own_ref.rest_0_, ...), custom_call_target="tpu_custom_call" | custom-call | flops 3221225472 | bytes 12582912 | tf_op jit(solution)/shard_map/field/pallas_call | solution.py:160
  30.2 0.1 collective-permute-start.2
  30.3 4.8 %collective-permute-start.3 = (f32[8,128,128]{2,1,0:T(8,128)S(1)}, f32[8,128,128]{2,1,0:T(8,128)S(1)}, u32[]{:S(2)}, u32[]{:S(2)}) collective-permute-start(f32[8,128,128]{2,1,0:T(8,128)S(1)} %field.4.own_ref), channel_id=1, source_target_pairs={{8,0},{16,8},{24,16},{32,24},{40,32},{48,40},{56,48},{64,56},{72,6... | collective-permute-start | bytes 1572872 | tf_op jit(solution)/shard_map/ppermute | solution.py:360
  35.0 7.8 %field.6.own_ref = f32[8,128,128]{2,1,0:T(8,128)S(1)} custom-call(s32[192]{0:T(256)S(1)} %reshape.30.cols_ref, f32[2]{0:T(128)S(1)} %pad_maximum_fusion.coef_ref, bf16[16,12,256,128]{3,2,1,0:T(8,128)(2,1)S(1)} %split_blocks.1.h_ref, f32[8,128,128]{2,1,0:T(8,128)S(1)} %collective-permute-done.4.left_ref, f32[8,128,128]{2,1,0:T(8,128)S(1)} %get-tuple-element.8.own_ref.rest_0_, ...), custom_call_target="tpu_custom_call" | custom-call | flops 3221225472 | bytes 12582912 | tf_op jit(solution)/shard_map/field/pallas_call | solution.py:160
  42.9 0.1 collective-permute-start.6
  43.0 4.8 %collective-permute-start.7 = (f32[8,128,128]{2,1,0:T(8,128)S(1)}, f32[8,128,128]{2,1,0:T(8,128)S(1)}, u32[]{:S(2)}, u32[]{:S(2)}) collective-permute-start(f32[8,128,128]{2,1,0:T(8,128)S(1)} %field.6.own_ref), channel_id=1, source_target_pairs={{8,0},{16,8},{24,16},{32,24},{40,32},{48,40},{56,48},{64,56},{72,6... | collective-permute-start | bytes 1572872 | tf_op jit(solution)/shard_map/ppermute | solution.py:360
  47.8 0.0 collective-permute-done.2.left_ref
  47.8 0.0 collective-permute-done.3.right_ref
  47.8 7.9 %field.5 = f32[8,128,128]{2,1,0:T(8,128)S(1)} custom-call(s32[192]{0:T(256)S(1)} %reshape.30.cols_ref, f32[2]{0:T(128)S(1)} %pad_maximum_fusion.coef_ref, bf16[16,12,256,128]{3,2,1,0:T(8,128)(2,1)S(1)} %split_blocks.1.h_ref, f32[8,128,128]{2,1,0:T(8,128)S(1)} %collective-permute-done.2.left_ref, f32[8,128,128]{2,1,0:T(8,128)S(1)} %field.4.own_ref, ...), custom_call_target="tpu_custom_call" | custom-call | flops 3221225472 | bytes 12582912 | tf_op jit(solution)/shard_map/field/pallas_call | solution.py:160
  55.6 2.7 %collective-permute-start.8 = (f32[1024,128]{1,0:T(8,128)S(1)}, f32[1024,128]{1,0:T(8,128)S(1)}, u32[]{:S(2)}, u32[]{:S(2)}) collective-permute-start(f32[1024,128]{1,0:T(8,128)S(1)} %bitcast.6), channel_id=1, source_target_pairs={{0,1},{1,0},{2,3},{3,2},{4,5},{5,4},{6,7},{7,6},{8,9},{9,8},{10,11... | collective-permute-start | bytes 1572872 | tf_op jit(solution)/shard_map/ppermute | solution.py:368
  58.4 2.7 %collective-permute-start.10 = (f32[1024,128]{1,0:T(8,128)S(1)}, f32[1024,128]{1,0:T(8,128)S(1)}, u32[]{:S(2)}, u32[]{:S(2)}) collective-permute-start(f32[1024,128]{1,0:T(8,128)S(1)} %bitcast.7), channel_id=1, source_target_pairs={{2,0},{3,1},{4,2},{5,3},{6,4},{7,5},{0,6},{1,7},{10,8},{11,9},{12,... | collective-permute-start | bytes 1572872 | tf_op jit(solution)/shard_map/ppermute | solution.py:363
  61.1 7.9 %field.7 = f32[8,128,128]{2,1,0:T(8,128)S(1)} custom-call(s32[192]{0:T(256)S(1)} %reshape.30.cols_ref, f32[2]{0:T(128)S(1)} %pad_maximum_fusion.coef_ref, bf16[16,12,256,128]{3,2,1,0:T(8,128)(2,1)S(1)} %split_blocks.1.h_ref, f32[8,128,128]{2,1,0:T(8,128)S(1)} %collective-permute-done.6.left_ref, f32[8,128,128]{2,1,0:T(8,128)S(1)} %field.6.own_ref, ...), custom_call_target="tpu_custom_call" | custom-call | flops 3221225472 | bytes 12582912 | tf_op jit(solution)/shard_map/field/pallas_call | solution.py:160
  69.0 0.5 collective-permute-start.11
  69.5 2.1 %collective-permute-start.9 = (f32[1024,128]{1,0:T(8,128)S(1)}, f32[1024,128]{1,0:T(8,128)S(1)}, u32[]{:S(2)}, u32[]{:S(2)}) collective-permute-start(f32[1024,128]{1,0:T(8,128)S(1)} %bitcast.12), channel_id=1, source_target_pairs={{0,1},{1,0},{2,3},{3,2},{4,5},{5,4},{6,7},{7,6},{8,9},{9,8},{10,11... | collective-permute-start | bytes 1572872 | tf_op jit(solution)/shard_map/ppermute | solution.py:368
  71.6 0.0 collective-permute-start.14
  71.6 0.0 collective-permute-done.8.rest_2_
  71.6 0.0 collective-permute-start.15
  71.6 0.7 collective-permute-done.10.rest_4_
  72.3 1.5 collective-permute-start.12
  73.8 9.8 %collective-permute-done.11.rest_5_ = f32[1024,128]{1,0:T(8,128)S(1)} collective-permute-done((f32[1024,128]{1,0:T(8,128)S(1)}, f32[1024,128]{1,0:T(8,128)S(1)}, u32[]{:S(2)}, u32[]{:S(2)}) %collective-permute-start.11) | collective-permute-done | bytes 524320 | tf_op jit(solution)/shard_map/ppermute | solution.py:363
  83.5 0.9 collective-permute-start.13
  84.5 1.9 %collective-permute-done.14.rest_8_ = f32[1024,128]{1,0:T(8,128)} collective-permute-done((f32[1024,128]{1,0:T(8,128)S(1)}, f32[1024,128]{1,0:T(8,128)}, u32[]{:S(2)}, u32[]{:S(2)}) %collective-permute-start.14) | collective-permute-done | bytes 524320 | tf_op jit(solution)/shard_map/ppermute | solution.py:363
  86.4 11.2 %collective-permute-done.15.rest_9_ = f32[1024,128]{1,0:T(8,128)} collective-permute-done((f32[1024,128]{1,0:T(8,128)S(1)}, f32[1024,128]{1,0:T(8,128)}, u32[]{:S(2)}, u32[]{:S(2)}) %collective-permute-start.15) | collective-permute-done | bytes 524320 | tf_op jit(solution)/shard_map/ppermute | solution.py:363
  97.6 5.6 %gram_share.1 = f32[128,640]{1,0:T(8,128)S(1)} custom-call(s32[1]{0:T(128)} %bitcast.y_ref, f32[1024,128]{1,0:T(8,128)S(1)} %bitcast.9, f32[1024,128]{1,0:T(8,128)S(1)} %bitcast.14, f32[1024,128]{1,0:T(8,128)S(1)} %collective-permute-done.8.rest_2_, f32[1024,128]{1,0:T(8,128)S(1)} %collective-permute-done.9.rest_3_, ...), custom_call_target="tpu_custom_call" | custom-call | flops 1342177280 | bytes 5242880 | tf_op jit(solution)/shard_map/gram_share/pallas_call | solution.py:218
  103.3 14.3 %all_to_all.10 = f32[16,8,640]{2,1,0:T(8,128)S(1)} all-to-all(f32[16,8,640]{2,1,0:T(8,128)S(1)} %bitcast.16), channel_id=1, replica_groups=mesh['row'=16,'vec'=8] {'row'}, dimensions={0} | all-to-all | bytes 655360 | tf_op jit(solution)/shard_map/all_to_all | solution.py:392
  117.6 0.1 broadcast_in_dim.17
  117.7 23.0 %all_to_all.11 = f32[64,8,640]{2,1,0:T(8,128)S(1)} all-to-all(f32[64,8,640]{2,1,0:T(8,128)S(1)} %broadcast_in_dim.17), channel_id=1, replica_groups={{0,2,4,6,8,10,12,14,16,18,20,22,24,26,28,30,32,34,36,38,40,42,44,46,48,..., dimensions={0} | all-to-all | bytes 2621440 | tf_op jit(solution)/shard_map/all_to_all | solution.py:401
  140.7 3.4 %collective-permute-start.16 = (f32[16,4,8,640]{3,2,1,0:T(8,128)S(1)}, f32[16,4,8,640]{3,2,1,0:T(8,128)S(1)}, u32[]{:S(2)}, u32[]{:S(2)}) collective-permute-start(f32[16,4,8,640]{3,2,1,0:T(8,128)S(1)} %bitcast.17), channel_id=1, source_target_pairs={{0,1},{1,0},{2,3},{3,2},{4,5},{5,4},{6,7},{7,6},{8,9},{9,8},{10,11... | collective-permute-start | bytes 3932168 | tf_op jit(solution)/shard_map/ppermute | solution.py:368
  144.1 0.4 collective-permute-start.19
  144.5 1.1 collective-permute-start.20
  145.6 0.6 collective-permute-start.17
  146.1 11.4 %collective-permute-done.19.rest_12_ = f32[1024,128]{1,0:T(8,128)S(1)} collective-permute-done((f32[1024,128]{1,0:T(8,128)S(1)}, f32[1024,128]{1,0:T(8,128)S(1)}, u32[]{:S(2)}, u32[]{:S(2)}) %collective-permute-start.19) | collective-permute-done | bytes 524320 | tf_op jit(solution)/shard_map/ppermute | solution.py:363
  157.6 0.9 collective-permute-start.21
  158.4 0.7 collective-permute-done.20.rest_13_
  159.1 1.1 collective-permute-start.22
  160.3 1.5 collective-permute-done.22.rest_15_
  161.8 22.0 %finish.1 = f32[2048,128]{1,0:T(8,128)} custom-call(s32[1]{0:T(128)} %bitcast.y_ref, f32[16,4,8,640]{3,2,1,0:T(8,128)S(1)} %bitcast.18, f32[16,4,8,640]{3,2,1,0:T(8,128)S(1)} %collective-permute-done.16.gb_ref, f32[1024,128]{1,0:T(8,128)S(1)} %bitcast.10, f32[1024,128]{1,0:T(8,128)S(1)} %bitcast.15, f32[1024,128]{1,0:T(8,128)S(1)} %collective-permute-done.8.rest_2_, ...), custom_call_target="tpu_custom_call" | custom-call | flops 9663676416 | bytes 9437184 | tf_op jit(solution)/shard_map/finish/pallas_call | solution.py:328
  (15 shorter events, 0.1 us)
Async XLA Ops:
  0.0 1.2 copy-start
  2.0 20.3 %collective-permute-start = (f32[8,128,128]{2,1,0:T(8,128)S(1)}, f32[8,128,128]{2,1,0:T(8,128)S(1)}, u32[]{:S(2)}, u32[]{:S(2)}) collective-permute-start(f32[8,128,128]{2,1,0:T(8,128)S(1)} %get-tuple-element.7.own_ref.rest_0_), channel_id=1, source_target_pairs={{120,0},{0,8},{8,16},{16,24},{24,32},{32,40},{40,48},{48,56},{56,6... | collective-permute-start | bytes 1572872 | tf_op jit(solution)/shard_map/ppermute | solution.py:360
  4.1 18.2 %collective-permute-start.1 = (f32[8,128,128]{2,1,0:T(8,128)S(1)}, f32[8,128,128]{2,1,0:T(8,128)S(1)}, u32[]{:S(2)}, u32[]{:S(2)}) collective-permute-start(f32[8,128,128]{2,1,0:T(8,128)S(1)} %get-tuple-element.7.own_ref.rest_0_), channel_id=1, source_target_pairs={{8,0},{16,8},{24,16},{32,24},{40,32},{48,40},{56,48},{64,56},{72,6... | collective-permute-start | bytes 1572872 | tf_op jit(solution)/shard_map/ppermute | solution.py:360
  9.0 26.1 %collective-permute-start.4 = (f32[8,128,128]{2,1,0:T(8,128)S(1)}, f32[8,128,128]{2,1,0:T(8,128)S(1)}, u32[]{:S(2)}, u32[]{:S(2)}) collective-permute-start(f32[8,128,128]{2,1,0:T(8,128)S(1)} %get-tuple-element.8.own_ref.rest_0_), channel_id=1, source_target_pairs={{120,0},{0,8},{8,16},{16,24},{24,32},{32,40},{40,48},{48,56},{56,6... | collective-permute-start | bytes 1572872 | tf_op jit(solution)/shard_map/ppermute | solution.py:360
  9.0 26.1 %collective-permute-start.5 = (f32[8,128,128]{2,1,0:T(8,128)S(1)}, f32[8,128,128]{2,1,0:T(8,128)S(1)}, u32[]{:S(2)}, u32[]{:S(2)}) collective-permute-start(f32[8,128,128]{2,1,0:T(8,128)S(1)} %get-tuple-element.8.own_ref.rest_0_), channel_id=1, source_target_pairs={{8,0},{16,8},{24,16},{32,24},{40,32},{48,40},{56,48},{64,56},{72,6... | collective-permute-start | bytes 1572872 | tf_op jit(solution)/shard_map/ppermute | solution.py:360
  30.2 17.6 %collective-permute-start.2 = (f32[8,128,128]{2,1,0:T(8,128)S(1)}, f32[8,128,128]{2,1,0:T(8,128)S(1)}, u32[]{:S(2)}, u32[]{:S(2)}) collective-permute-start(f32[8,128,128]{2,1,0:T(8,128)S(1)} %field.4.own_ref), channel_id=1, source_target_pairs={{120,0},{0,8},{8,16},{16,24},{24,32},{32,40},{40,48},{48,56},{56,6... | collective-permute-start | bytes 1572872 | tf_op jit(solution)/shard_map/ppermute | solution.py:360
  30.3 17.5 %collective-permute-start.3 = (f32[8,128,128]{2,1,0:T(8,128)S(1)}, f32[8,128,128]{2,1,0:T(8,128)S(1)}, u32[]{:S(2)}, u32[]{:S(2)}) collective-permute-start(f32[8,128,128]{2,1,0:T(8,128)S(1)} %field.4.own_ref), channel_id=1, source_target_pairs={{8,0},{16,8},{24,16},{32,24},{40,32},{48,40},{56,48},{64,56},{72,6... | collective-permute-start | bytes 1572872 | tf_op jit(solution)/shard_map/ppermute | solution.py:360
  42.9 18.2 %collective-permute-start.6 = (f32[8,128,128]{2,1,0:T(8,128)S(1)}, f32[8,128,128]{2,1,0:T(8,128)S(1)}, u32[]{:S(2)}, u32[]{:S(2)}) collective-permute-start(f32[8,128,128]{2,1,0:T(8,128)S(1)} %field.6.own_ref), channel_id=1, source_target_pairs={{120,0},{0,8},{8,16},{16,24},{24,32},{32,40},{40,48},{48,56},{56,6... | collective-permute-start | bytes 1572872 | tf_op jit(solution)/shard_map/ppermute | solution.py:360
  43.0 18.1 %collective-permute-start.7 = (f32[8,128,128]{2,1,0:T(8,128)S(1)}, f32[8,128,128]{2,1,0:T(8,128)S(1)}, u32[]{:S(2)}, u32[]{:S(2)}) collective-permute-start(f32[8,128,128]{2,1,0:T(8,128)S(1)} %field.6.own_ref), channel_id=1, source_target_pairs={{8,0},{16,8},{24,16},{32,24},{40,32},{48,40},{56,48},{64,56},{72,6... | collective-permute-start | bytes 1572872 | tf_op jit(solution)/shard_map/ppermute | solution.py:360
  55.6 16.0 %collective-permute-start.8 = (f32[1024,128]{1,0:T(8,128)S(1)}, f32[1024,128]{1,0:T(8,128)S(1)}, u32[]{:S(2)}, u32[]{:S(2)}) collective-permute-start(f32[1024,128]{1,0:T(8,128)S(1)} %bitcast.6), channel_id=1, source_target_pairs={{0,1},{1,0},{2,3},{3,2},{4,5},{5,4},{6,7},{7,6},{8,9},{9,8},{10,11... | collective-permute-start | bytes 1572872 | tf_op jit(solution)/shard_map/ppermute | solution.py:368
  58.4 13.9 %collective-permute-start.10 = (f32[1024,128]{1,0:T(8,128)S(1)}, f32[1024,128]{1,0:T(8,128)S(1)}, u32[]{:S(2)}, u32[]{:S(2)}) collective-permute-start(f32[1024,128]{1,0:T(8,128)S(1)} %bitcast.7), channel_id=1, source_target_pairs={{2,0},{3,1},{4,2},{5,3},{6,4},{7,5},{0,6},{1,7},{10,8},{11,9},{12,... | collective-permute-start | bytes 1572872 | tf_op jit(solution)/shard_map/ppermute | solution.py:363
  69.0 14.6 %collective-permute-start.11 = (f32[1024,128]{1,0:T(8,128)S(1)}, f32[1024,128]{1,0:T(8,128)S(1)}, u32[]{:S(2)}, u32[]{:S(2)}) collective-permute-start(f32[1024,128]{1,0:T(8,128)S(1)} %bitcast.11), channel_id=1, source_target_pairs={{2,0},{3,1},{4,2},{5,3},{6,4},{7,5},{0,6},{1,7},{10,8},{11,9},{12,... | collective-permute-start | bytes 1572872 | tf_op jit(solution)/shard_map/ppermute | solution.py:363
  69.5 15.0 %collective-permute-start.9 = (f32[1024,128]{1,0:T(8,128)S(1)}, f32[1024,128]{1,0:T(8,128)S(1)}, u32[]{:S(2)}, u32[]{:S(2)}) collective-permute-start(f32[1024,128]{1,0:T(8,128)S(1)} %bitcast.12), channel_id=1, source_target_pairs={{0,1},{1,0},{2,3},{3,2},{4,5},{5,4},{6,7},{7,6},{8,9},{9,8},{10,11... | collective-permute-start | bytes 1572872 | tf_op jit(solution)/shard_map/ppermute | solution.py:368
  71.6 14.8 %collective-permute-start.14 = (f32[1024,128]{1,0:T(8,128)S(1)}, f32[1024,128]{1,0:T(8,128)}, u32[]{:S(2)}, u32[]{:S(2)}) collective-permute-start(f32[1024,128]{1,0:T(8,128)S(1)} %bitcast.8), channel_id=1, source_target_pairs={{6,0},{7,1},{0,2},{1,3},{2,4},{3,5},{4,6},{5,7},{14,8},{15,9},{8,1... | collective-permute-start | bytes 1572872 | tf_op jit(solution)/shard_map/ppermute | solution.py:363
  71.6 26.0 %collective-permute-start.15 = (f32[1024,128]{1,0:T(8,128)S(1)}, f32[1024,128]{1,0:T(8,128)}, u32[]{:S(2)}, u32[]{:S(2)}) collective-permute-start(f32[1024,128]{1,0:T(8,128)S(1)} %bitcast.13), channel_id=1, source_target_pairs={{6,0},{7,1},{0,2},{1,3},{2,4},{3,5},{4,6},{5,7},{14,8},{15,9},{8,1... | collective-permute-start | bytes 1572872 | tf_op jit(solution)/shard_map/ppermute | solution.py:363
  72.3 25.3 %collective-permute-start.12 = (f32[1024,128]{1,0:T(8,128)S(1)}, f32[1024,128]{1,0:T(8,128)}, u32[]{:S(2)}, u32[]{:S(2)}) collective-permute-start(f32[1024,128]{1,0:T(8,128)S(1)} %collective-permute-done.10.rest_4_), channel_id=1, source_target_pairs={{0,1},{1,0},{2,3},{3,2},{4,5},{5,4},{6,7},{7,6},{8,9},{9,8},{10,11... | collective-permute-start | bytes 1572872 | tf_op jit(solution)/shard_map/ppermute | solution.py:368
  83.5 14.1 %collective-permute-start.13 = (f32[1024,128]{1,0:T(8,128)S(1)}, f32[1024,128]{1,0:T(8,128)}, u32[]{:S(2)}, u32[]{:S(2)}) collective-permute-start(f32[1024,128]{1,0:T(8,128)S(1)} %collective-permute-done.11.rest_5_), channel_id=1, source_target_pairs={{0,1},{1,0},{2,3},{3,2},{4,5},{5,4},{6,7},{7,6},{8,9},{9,8},{10,11... | collective-permute-start | bytes 1572872 | tf_op jit(solution)/shard_map/ppermute | solution.py:368
  140.7 21.1 %collective-permute-start.16 = (f32[16,4,8,640]{3,2,1,0:T(8,128)S(1)}, f32[16,4,8,640]{3,2,1,0:T(8,128)S(1)}, u32[]{:S(2)}, u32[]{:S(2)}) collective-permute-start(f32[16,4,8,640]{3,2,1,0:T(8,128)S(1)} %bitcast.17), channel_id=1, source_target_pairs={{0,1},{1,0},{2,3},{3,2},{4,5},{5,4},{6,7},{7,6},{8,9},{9,8},{10,11... | collective-permute-start | bytes 3932168 | tf_op jit(solution)/shard_map/ppermute | solution.py:368
  144.1 13.5 %collective-permute-start.19 = (f32[1024,128]{1,0:T(8,128)S(1)}, f32[1024,128]{1,0:T(8,128)S(1)}, u32[]{:S(2)}, u32[]{:S(2)}) collective-permute-start(f32[1024,128]{1,0:T(8,128)S(1)} %collective-permute-done.10.rest_4_), channel_id=1, source_target_pairs={{2,0},{3,1},{4,2},{5,3},{6,4},{7,5},{0,6},{1,7},{10,8},{11,9},{12,... | collective-permute-start | bytes 1572872 | tf_op jit(solution)/shard_map/ppermute | solution.py:363
  144.5 14.6 %collective-permute-start.20 = (f32[1024,128]{1,0:T(8,128)}, f32[1024,128]{1,0:T(8,128)S(1)}, u32[]{:S(2)}, u32[]{:S(2)}) collective-permute-start(f32[1024,128]{1,0:T(8,128)} %collective-permute-done.15.rest_9_), channel_id=1, source_target_pairs={{6,0},{7,1},{0,2},{1,3},{2,4},{3,5},{4,6},{5,7},{14,8},{15,9},{8,1... | collective-permute-start | bytes 1572872 | tf_op jit(solution)/shard_map/ppermute | solution.py:363
  145.6 14.7 %collective-permute-start.17 = (f32[1024,128]{1,0:T(8,128)}, f32[1024,128]{1,0:T(8,128)S(1)}, u32[]{:S(2)}, u32[]{:S(2)}) collective-permute-start(f32[1024,128]{1,0:T(8,128)} %collective-permute-done.14.rest_8_), channel_id=1, source_target_pairs={{0,1},{1,0},{2,3},{3,2},{4,5},{5,4},{6,7},{7,6},{8,9},{9,8},{10,11... | collective-permute-start | bytes 1572872 | tf_op jit(solution)/shard_map/ppermute | solution.py:368
  146.1 14.1 %collective-permute-start.18 = (f32[1024,128]{1,0:T(8,128)}, f32[1024,128]{1,0:T(8,128)S(1)}, u32[]{:S(2)}, u32[]{:S(2)}) collective-permute-start(f32[1024,128]{1,0:T(8,128)} %collective-permute-done.15.rest_9_), channel_id=1, source_target_pairs={{0,1},{1,0},{2,3},{3,2},{4,5},{5,4},{6,7},{7,6},{8,9},{9,8},{10,11... | collective-permute-start | bytes 1572872 | tf_op jit(solution)/shard_map/ppermute | solution.py:368
  157.6 2.7 %collective-permute-start.21 = (f32[1024,128]{1,0:T(8,128)S(1)}, f32[1024,128]{1,0:T(8,128)S(1)}, u32[]{:S(2)}, u32[]{:S(2)}) collective-permute-start(f32[1024,128]{1,0:T(8,128)S(1)} %collective-permute-done.19.rest_12_), channel_id=1, source_target_pairs={{0,1},{1,0},{2,3},{3,2},{4,5},{5,4},{6,7},{7,6},{8,9},{9,8},{10,11... | collective-permute-start | bytes 1572872 | tf_op jit(solution)/shard_map/ppermute | solution.py:368
  159.1 2.7 %collective-permute-start.22 = (f32[1024,128]{1,0:T(8,128)S(1)}, f32[1024,128]{1,0:T(8,128)S(1)}, u32[]{:S(2)}, u32[]{:S(2)}) collective-permute-start(f32[1024,128]{1,0:T(8,128)S(1)} %collective-permute-done.20.rest_13_), channel_id=1, source_target_pairs={{0,1},{1,0},{2,3},{3,2},{4,5},{5,4},{6,7},{7,6},{8,9},{9,8},{10,11... | collective-permute-start | bytes 1572872 | tf_op jit(solution)/shard_map/ppermute | solution.py:368

commit v4 on v3

--- a/solution.py
+++ b/solution.py
@@ -117,6 +117,9 @@
     )(blocks)
 
 
+UNROLL = 4
+
+
 def field_kernel(second, cols_ref, coef_ref, h_ref, left_ref, own_ref, right_ref, *rest):
     if second:
         prev_ref, o_ref, wide = rest
@@ -127,7 +130,7 @@
     low = lanes_low(own_ref.shape[1:])
     for part, ref in enumerate((left_ref, own_ref, right_ref)):
 
-        @pl.loop(0, half)
+        @pl.loop(0, half, unroll=2)
         def _(j):
             value = ref[j]
             high = value.astype(BF).astype(F32)
@@ -145,13 +148,15 @@
         full = full[: full.shape[0] // 2] + full[full.shape[0] // 2 :]
         return full + turn(full)
 
-    @pl.loop(0, half)
-    def _(i):
-        summed = jnp.where(low, row(i), row(i + half))
-        result = (summed - centre * own_ref[i]) * inverse
-        if second:
-            result = 2.0 * result - prev_ref[i]
-        o_ref[i] = result
+    @pl.loop(0, half // UNROLL)
+    def _(step):
+        for within in range(UNROLL):
+            i = step * UNROLL + within
+            summed = jnp.where(low, row(i), row(i + half))
+            result = (summed - centre * own_ref[i]) * inverse
+            if second:
+                result = 2.0 * result - prev_ref[i]
+            o_ref[i] = result
 
 
 def apply_field(second, cols, coef, split_h, left, own, right, prev=None):
@@ -176,55 +181,57 @@
 
 
 GRAM_BLOCKS = 5
-
-
-def gram_kernel(y_ref, *rest):
-    own, beside, up, up_s, down = (rest[2 * n : 2 * n + 2] for n in range(5))
-    out_ref, acc = rest[10:]
-    acc[...] = jnp.zeros_like(acc)
-    chunk = 512
+NEAR_BLOCKS = 2
+
+
+def gram_product(left, right):
+    total = None
     for part in range(2):
-
-        @pl.loop(0, own[0].shape[0] // chunk)
-        def _(step):
-            rows = pl.ds(pl.multiple_of(step * chunk, chunk), chunk)
-
-            def turned(refs):
-                return jnp.concatenate(split(natural(refs, rows, part).T), axis=0)
-
-            def paired(refs):
-                return jnp.concatenate(split(natural(refs, rows, part)), axis=1)
-
-            lhs = turned(own)
-            for block, refs in enumerate((own, beside, up, up_s)):
-                acc[block] += mm(lhs, paired(refs))
-            lhs = turned(down)
-
-            @pl.when(y_ref[0] < 2)
-            def _():
-                acc[4] += mm(lhs, paired(up))
-
-            @pl.when(y_ref[0] >= 2)
-            def _():
-                acc[4] += mm(lhs, paired(up_s))
-
-    for block in range(GRAM_BLOCKS):
-        out_ref[:, block * 128 : (block + 1) * 128] = fold(acc[block])
-
-
-def gram_share(y, pieces):
+        lhs = jnp.concatenate(split(natural(left, slice(None), part).T), axis=0)
+        rhs = jnp.concatenate(split(natural(right, slice(None), part)), axis=1)
+        term = mm(lhs, rhs)
+        total = term if total is None else total + term
+    return fold(total)
+
+
+def columns_of(ref, block):
+    return ref.at[:, block * 128 : (block + 1) * 128]
+
+
+def near_kernel(*rest):
+    own, beside = (rest[2 * n : 2 * n + 2] for n in range(2))
+    out_ref = rest[4]
+    for block, refs in enumerate((own, beside)):
+        columns_of(out_ref, block)[...] = gram_product(own, refs)
+
+
+def far_kernel(y_ref, near_ref, *rest):
+    own, up, up_s, down = (rest[2 * n : 2 * n + 2] for n in range(4))
+    out_ref = rest[8]
+    out_ref[:, : NEAR_BLOCKS * 128] = near_ref[...]
+    columns_of(out_ref, 2)[...] = gram_product(own, up)
+    columns_of(out_ref, 3)[...] = gram_product(own, up_s)
+
+    @pl.when(y_ref[0] < 2)
+    def _():
+        columns_of(out_ref, 4)[...] = gram_product(down, up)
+
+    @pl.when(y_ref[0] >= 2)
+    def _():
+        columns_of(out_ref, 4)[...] = gram_product(down, up_s)
+
+
+def gram_call(kernel, blocks, products, before, pieces):
     operands = [chunk for piece in pieces for chunk in piece]
     rows, cols = operands[0].shape
     return pl.pallas_call(
-        gram_kernel,
-        out_shape=jax.ShapeDtypeStruct((cols, GRAM_BLOCKS * cols), F32),
-        in_specs=[SMEM_SPEC] + [VMEM_SPEC] * len(operands),
+        kernel,
+        out_shape=jax.ShapeDtypeStruct((cols, blocks * cols), F32),
+        in_specs=([SMEM_SPEC, VMEM_SPEC] if before else []) + [VMEM_SPEC] * len(operands),
         out_specs=VMEM_SPEC,
-        scratch_shapes=[pltpu.VMEM((GRAM_BLOCKS, 2 * cols, 2 * cols), F32)],
         compiler_params=pltpu.CompilerParams(vmem_limit_bytes=30 * 2**20),
-        cost_estimate=cost(16 * rows * cols * cols * GRAM_BLOCKS, 4 * rows * cols * len(operands)),
-        name="gram_share",
-    )(y, *operands)
+        cost_estimate=cost(16 * rows * cols * cols * products, 4 * rows * cols * len(operands)),
+    )(*before, *operands)
 
 
 KEEP = {0: 1, 3: 2, 4: 1, 8: 1}
@@ -313,7 +320,7 @@
     half = out_ref.shape[0] // 2
     for part in range(2):
 
-        @pl.loop(0, half // chunk)
+        @pl.loop(0, half // chunk, unroll=2)
         def _(step):
             within = pl.ds(pl.multiple_of(step * chunk, chunk), chunk)
             rows = pl.ds(pl.multiple_of(part * half + step * chunk, chunk), chunk)
@@ -387,7 +394,8 @@
         down_s.append(swap(down[-1]))
         across.append(from_y((up, down)[chunk][-1], (1, -1)[chunk]))
         across_s.append(swap(across[-1]))
-    share = gram_share(y, (own, own_s, up, up_s, down))
+    near = gram_call(near_kernel, NEAR_BLOCKS, 2, (), (own, own_s))
+    share = gram_call(far_kernel, GRAM_BLOCKS, 3, (y, near), (own, up, up_s, down))
     strip = share.shape[0] // row_count
     parts = lax.all_to_all(
         share.reshape(row_count, strip, -1), "row", split_axis=0, concat_axis=0, tiled=True

time: 184 us -> 176 us (0.957)
  Pallas kernels: 66.1 us -> 56.9 us
  starting transfers between devices: 39.4 us -> 42.8 us
  waiting for transfers between devices: 37.3 us -> 35 us
    pallas_call x4, Pallas kernels: 31.4 us -> 22.7 us  [apply_field(): pl.pallas_call(functools.partial(field_kernel, second), out_shape=jax.Sha...]
    ppermute x6, waiting for transfers between devices: 35.7 us -> 33.4 us  [from_y(): lax.ppermute(value, 'vec', [((i + 2 * step) % vec_count, i) for i in rang...]
    ppermute x6, starting transfers between devices: 4.76 us -> 6.84 us  [from_y(): lax.ppermute(value, 'vec', [((i + 2 * step) % vec_count, i) for i in rang...]
    pallas_call x1 -> x2, Pallas kernels: 5.64 us -> 6.31 us  [gram_call(): pl.pallas_call(kernel, out_shape=jax.ShapeDtypeStruct((cols, blocks * col...]
  transfers between devices with their start and end apart: 23 -> 23, of which waited for: 7 -> 7; matrix products, arithmetic and copies ran while one was open for 1% -> 1% of each run, Pallas kernels for 21% -> 17%
where the time goes in v4:
time: 176 us
  Pallas kernels  56.9 us (32%)
  starting transfers between devices  42.8 us (24%)
  blocking collectives  37.1 us (21%)
  waiting for transfers between devices  35 us (20%)
    ppermute x6, waiting for transfers between devices, from_y(): lax.ppermute(value, 'vec', [((i + 2 * step) % vec_count, i) for i in rang...  33.4 us
    all_to_all x1, blocking collectives, on_device(): lax.all_to_all(jnp.broadcast_to(part[None], (members,) + part.shape), ('r...  22.8 us
    pallas_call x4, Pallas kernels, apply_field(): pl.pallas_call(functools.partial(field_kernel, second), out_shape=jax.Sha...  22.7 us
    ppermute x8, starting transfers between devices, from_row(): lax.ppermute(value, 'row', [((i + step) % row_count, i) for i in range(ro...  21.4 us
    pallas_call x1, Pallas kernels, finish(): pl.pallas_call(functools.partial(finish_kernel, total_rows), out_shape=ja...  20.9 us
    ppermute x9, starting transfers between devices, swap(): return lax.ppermute(value, 'vec', [(i, i ^ 1) for i in range(vec_count)])  14.6 us
    all_to_all x1, blocking collectives, on_device(): lax.all_to_all(share.reshape(row_count, strip, -1), 'row', split_axis=0,...  14.3 us
    ppermute x6, starting transfers between devices, from_y(): lax.ppermute(value, 'vec', [((i + 2 * step) % vec_count, i) for i in rang...  6.84 us
  transfers between devices with their start and end apart: 23, of which 7 were waited for; matrix products, arithmetic and copies ran while one was open for 1% of the time, Pallas kernels for 17%

profile of v4, /device:TPU:1, one launch (start us, length us, event | category | flops | bytes accessed | tf_op | source)
XLA Modules:
  0.0 175.6 jit_solution(3492778447657729821)
XLA Ops:
  0.0 1.2 copy-done
  1.2 0.8 pack.1
  2.0 2.1 %collective-permute-start = (f32[8,128,128]{2,1,0:T(8,128)S(1)}, f32[8,128,128]{2,1,0:T(8,128)S(1)}, u32[]{:S(2)}, u32[]{:S(2)}) collective-permute-start(f32[8,128,128]{2,1,0:T(8,128)S(1)} %get-tuple-element.7.own_ref.rest_0_), channel_id=1, source_target_pairs={{120,0},{0,8},{8,16},{16,24},{24,32},{32,40},{40,48},{48,56},{56,6... | collective-permute-start | bytes 1572872 | tf_op jit(solution)/shard_map/ppermute | solution.py:367
  4.1 4.8 %collective-permute-start.1 = (f32[8,128,128]{2,1,0:T(8,128)S(1)}, f32[8,128,128]{2,1,0:T(8,128)S(1)}, u32[]{:S(2)}, u32[]{:S(2)}) collective-permute-start(f32[8,128,128]{2,1,0:T(8,128)S(1)} %get-tuple-element.7.own_ref.rest_0_), channel_id=1, source_target_pairs={{8,0},{16,8},{24,16},{32,24},{40,32},{48,40},{56,48},{64,56},{72,6... | collective-permute-start | bytes 1572872 | tf_op jit(solution)/shard_map/ppermute | solution.py:367
  9.0 4.8 %collective-permute-start.5 = (f32[8,128,128]{2,1,0:T(8,128)S(1)}, f32[8,128,128]{2,1,0:T(8,128)S(1)}, u32[]{:S(2)}, u32[]{:S(2)}) collective-permute-start(f32[8,128,128]{2,1,0:T(8,128)S(1)} %get-tuple-element.8.own_ref.rest_0_), channel_id=1, source_target_pairs={{8,0},{16,8},{24,16},{32,24},{40,32},{48,40},{56,48},{64,56},{72,6... | collective-permute-start | bytes 1572872 | tf_op jit(solution)/shard_map/ppermute | solution.py:367
  13.7 0.8 fusion.2
  15.8 0.1 reshape.30.cols_ref
  15.9 6.3 %split_blocks.1.h_ref = bf16[16,12,256,128]{3,2,1,0:T(8,128)(2,1)S(1)} custom-call(f32[16,12,128,128]{3,2,1,0:T(8,128)} %h_ref.1), custom_call_target="tpu_custom_call" | custom-call | bytes 25165824 | tf_op jit(solution)/shard_map/split_blocks/pallas_call | solution.py:65
  22.2 0.1 pad_maximum_fusion.coef_ref
  22.3 0.0 collective-permute-done.left_ref
  22.3 0.0 collective-permute-done.1.right_ref
  22.3 5.7 %field.4.own_ref = f32[8,128,128]{2,1,0:T(8,128)S(1)} custom-call(s32[192]{0:T(256)S(1)} %reshape.30.cols_ref, f32[2]{0:T(128)S(1)} %pad_maximum_fusion.coef_ref, bf16[16,12,256,128]{3,2,1,0:T(8,128)(2,1)S(1)} %split_blocks.1.h_ref, f32[8,128,128]{2,1,0:T(8,128)S(1)} %collective-permute-done.left_ref, f32[8,128,128]{2,1,0:T(8,128)S(1)} %get-tuple-element.7.own_ref.rest_0_, ...), custom_call_target="tpu_custom_call" | custom-call | flops 3221225472 | bytes 12582912 | tf_op jit(solution)/shard_map/field/pallas_call | solution.py:165
  28.0 0.1 collective-permute-start.2
  28.1 4.8 %collective-permute-start.3 = (f32[8,128,128]{2,1,0:T(8,128)S(1)}, f32[8,128,128]{2,1,0:T(8,128)S(1)}, u32[]{:S(2)}, u32[]{:S(2)}) collective-permute-start(f32[8,128,128]{2,1,0:T(8,128)S(1)} %field.4.own_ref), channel_id=1, source_target_pairs={{8,0},{16,8},{24,16},{32,24},{40,32},{48,40},{56,48},{64,56},{72,6... | collective-permute-start | bytes 1572872 | tf_op jit(solution)/shard_map/ppermute | solution.py:367
  32.8 0.0 collective-permute-done.5.right_ref
  32.8 5.7 %field.6.own_ref = f32[8,128,128]{2,1,0:T(8,128)S(1)} custom-call(s32[192]{0:T(256)S(1)} %reshape.30.cols_ref, f32[2]{0:T(128)S(1)} %pad_maximum_fusion.coef_ref, bf16[16,12,256,128]{3,2,1,0:T(8,128)(2,1)S(1)} %split_blocks.1.h_ref, f32[8,128,128]{2,1,0:T(8,128)S(1)} %collective-permute-done.4.left_ref, f32[8,128,128]{2,1,0:T(8,128)S(1)} %get-tuple-element.8.own_ref.rest_0_, ...), custom_call_target="tpu_custom_call" | custom-call | flops 3221225472 | bytes 12582912 | tf_op jit(solution)/shard_map/field/pallas_call | solution.py:165
  38.5 0.1 collective-permute-start.6
  38.6 4.8 %collective-permute-start.7 = (f32[8,128,128]{2,1,0:T(8,128)S(1)}, f32[8,128,128]{2,1,0:T(8,128)S(1)}, u32[]{:S(2)}, u32[]{:S(2)}) collective-permute-start(f32[8,128,128]{2,1,0:T(8,128)S(1)} %field.6.own_ref), channel_id=1, source_target_pairs={{8,0},{16,8},{24,16},{32,24},{40,32},{48,40},{56,48},{64,56},{72,6... | collective-permute-start | bytes 1572872 | tf_op jit(solution)/shard_map/ppermute | solution.py:367
  43.4 0.0 collective-permute-done.2.left_ref
  43.4 0.0 collective-permute-done.3.right_ref
  43.4 5.7 %field.5 = f32[8,128,128]{2,1,0:T(8,128)S(1)} custom-call(s32[192]{0:T(256)S(1)} %reshape.30.cols_ref, f32[2]{0:T(128)S(1)} %pad_maximum_fusion.coef_ref, bf16[16,12,256,128]{3,2,1,0:T(8,128)(2,1)S(1)} %split_blocks.1.h_ref, f32[8,128,128]{2,1,0:T(8,128)S(1)} %collective-permute-done.2.left_ref, f32[8,128,128]{2,1,0:T(8,128)S(1)} %field.4.own_ref, ...), custom_call_target="tpu_custom_call" | custom-call | flops 3221225472 | bytes 12582912 | tf_op jit(solution)/shard_map/field/pallas_call | solution.py:165
  49.0 3.1 %collective-permute-start.8 = (f32[1024,128]{1,0:T(8,128)S(1)}, f32[1024,128]{1,0:T(8,128)S(1)}, u32[]{:S(2)}, u32[]{:S(2)}) collective-permute-start(f32[1024,128]{1,0:T(8,128)S(1)} %bitcast.6), channel_id=1, source_target_pairs={{0,1},{1,0},{2,3},{3,2},{4,5},{5,4},{6,7},{7,6},{8,9},{9,8},{10,11... | collective-permute-start | bytes 1572872 | tf_op jit(solution)/shard_map/ppermute | solution.py:375
  52.2 2.7 %collective-permute-start.10 = (f32[1024,128]{1,0:T(8,128)S(1)}, f32[1024,128]{1,0:T(8,128)S(1)}, u32[]{:S(2)}, u32[]{:S(2)}) collective-permute-start(f32[1024,128]{1,0:T(8,128)S(1)} %bitcast.7), channel_id=1, source_target_pairs={{2,0},{3,1},{4,2},{5,3},{6,4},{7,5},{0,6},{1,7},{10,8},{11,9},{12,... | collective-permute-start | bytes 1572872 | tf_op jit(solution)/shard_map/ppermute | solution.py:370
  54.9 5.7 %field.7 = f32[8,128,128]{2,1,0:T(8,128)S(1)} custom-call(s32[192]{0:T(256)S(1)} %reshape.30.cols_ref, f32[2]{0:T(128)S(1)} %pad_maximum_fusion.coef_ref, bf16[16,12,256,128]{3,2,1,0:T(8,128)(2,1)S(1)} %split_blocks.1.h_ref, f32[8,128,128]{2,1,0:T(8,128)S(1)} %collective-permute-done.6.left_ref, f32[8,128,128]{2,1,0:T(8,128)S(1)} %field.6.own_ref, ...), custom_call_target="tpu_custom_call" | custom-call | flops 3221225472 | bytes 12582912 | tf_op jit(solution)/shard_map/field/pallas_call | solution.py:165
  60.6 2.6 %collective-permute-start.11 = (f32[1024,128]{1,0:T(8,128)S(1)}, f32[1024,128]{1,0:T(8,128)S(1)}, u32[]{:S(2)}, u32[]{:S(2)}) collective-permute-start(f32[1024,128]{1,0:T(8,128)S(1)} %bitcast.12), channel_id=1, source_target_pairs={{2,0},{3,1},{4,2},{5,3},{6,4},{7,5},{0,6},{1,7},{10,8},{11,9},{12,... | collective-permute-start | bytes 1572872 | tf_op jit(solution)/shard_map/ppermute | solution.py:370
  63.2 2.5 %collective-permute-start.9 = (f32[1024,128]{1,0:T(8,128)S(1)}, f32[1024,128]{1,0:T(8,128)S(1)}, u32[]{:S(2)}, u32[]{:S(2)}) collective-permute-start(f32[1024,128]{1,0:T(8,128)S(1)} %bitcast.13), channel_id=1, source_target_pairs={{0,1},{1,0},{2,3},{3,2},{4,5},{5,4},{6,7},{7,6},{8,9},{9,8},{10,11... | collective-permute-start | bytes 1572872 | tf_op jit(solution)/shard_map/ppermute | solution.py:375
  65.7 0.0 collective-permute-start.15
  65.7 0.2 collective-permute-done.10.rest_2_.rest_4_
  65.9 1.8 %collective-permute-start.12 = (f32[1024,128]{1,0:T(8,128)S(1)}, f32[1024,128]{1,0:T(8,128)}, u32[]{:S(2)}, u32[]{:S(2)}) collective-permute-start(f32[1024,128]{1,0:T(8,128)S(1)} %collective-permute-done.10.rest_2_.rest_4_), channel_id=1, source_target_pairs={{0,1},{1,0},{2,3},{3,2},{4,5},{5,4},{6,7},{7,6},{8,9},{9,8},{10,11... | collective-permute-start | bytes 1572872 | tf_op jit(solution)/shard_map/ppermute | solution.py:375
  67.8 9.4 %collective-permute-done.11.rest_3_.rest_5_ = f32[1024,128]{1,0:T(8,128)S(1)} collective-permute-done((f32[1024,128]{1,0:T(8,128)S(1)}, f32[1024,128]{1,0:T(8,128)S(1)}, u32[]{:S(2)}, u32[]{:S(2)}) %collective-permute-start.11) | collective-permute-done | bytes 524320 | tf_op jit(solution)/shard_map/ppermute | solution.py:370
  77.2 1.1 collective-permute-start.13
  78.3 1.7 shard_map.64.near_ref
  80.0 0.5 collective-permute-done.14.rest_6_.rest_8_
  80.5 11.2 %collective-permute-done.15.rest_7_.rest_9_ = f32[1024,128]{1,0:T(8,128)} collective-permute-done((f32[1024,128]{1,0:T(8,128)S(1)}, f32[1024,128]{1,0:T(8,128)}, u32[]{:S(2)}, u32[]{:S(2)}) %collective-permute-start.15) | collective-permute-done | bytes 524320 | tf_op jit(solution)/shard_map/ppermute | solution.py:370
  91.7 4.6 %shard_map.65 = f32[128,640]{1,0:T(8,128)S(1)} custom-call(s32[1]{0:T(128)} %bitcast.y_ref, f32[128,256]{1,0:T(8,128)S(1)} %shard_map.64.near_ref, f32[1024,128]{1,0:T(8,128)S(1)} %bitcast.10, f32[1024,128]{1,0:T(8,128)S(1)} %bitcast.16, f32[1024,128]{1,0:T(8,128)S(1)} %collective-permute-done.10.rest_2_.rest_4_, ...), custom_call_target="tpu_custom_call" | custom-call | flops 805306368 | bytes 4194304 | tf_op jit(solution)/shard_map/pallas_call | solution.py:227
  96.4 14.3 %all_to_all.10 = f32[16,8,640]{2,1,0:T(8,128)S(1)} all-to-all(f32[16,8,640]{2,1,0:T(8,128)S(1)} %bitcast.18), channel_id=1, replica_groups=mesh['row'=16,'vec'=8] {'row'}, dimensions={0} | all-to-all | bytes 655360 | tf_op jit(solution)/shard_map/all_to_all | solution.py:400
  110.7 0.1 broadcast_in_dim.17
  110.8 22.8 %all_to_all.11 = f32[64,8,640]{2,1,0:T(8,128)S(1)} all-to-all(f32[64,8,640]{2,1,0:T(8,128)S(1)} %broadcast_in_dim.17), channel_id=1, replica_groups={{0,2,4,6,8,10,12,14,16,18,20,22,24,26,28,30,32,34,36,38,40,42,44,46,48,..., dimensions={0} | all-to-all | bytes 2621440 | tf_op jit(solution)/shard_map/all_to_all | solution.py:409
  133.6 3.4 %collective-permute-start.16 = (f32[16,4,8,640]{3,2,1,0:T(8,128)S(1)}, f32[16,4,8,640]{3,2,1,0:T(8,128)S(1)}, u32[]{:S(2)}, u32[]{:S(2)}) collective-permute-start(f32[16,4,8,640]{3,2,1,0:T(8,128)S(1)} %bitcast.19), channel_id=1, source_target_pairs={{0,1},{1,0},{2,3},{3,2},{4,5},{5,4},{6,7},{7,6},{8,9},{9,8},{10,11... | collective-permute-start | bytes 3932168 | tf_op jit(solution)/shard_map/ppermute | solution.py:375
  137.0 0.4 collective-permute-start.19
  137.4 1.1 collective-permute-start.20
  138.5 0.6 collective-permute-start.17
  139.0 11.4 %collective-permute-done.19.rest_12_ = f32[1024,128]{1,0:T(8,128)S(1)} collective-permute-done((f32[1024,128]{1,0:T(8,128)S(1)}, f32[1024,128]{1,0:T(8,128)S(1)}, u32[]{:S(2)}, u32[]{:S(2)}) %collective-permute-start.19) | collective-permute-done | bytes 524320 | tf_op jit(solution)/shard_map/ppermute | solution.py:370
  150.5 0.9 collective-permute-start.21
  151.4 0.7 collective-permute-done.20.rest_13_
  152.0 1.1 collective-permute-start.22
  153.2 1.5 collective-permute-done.22.rest_15_
  154.7 20.9 %finish.1 = f32[2048,128]{1,0:T(8,128)} custom-call(s32[1]{0:T(128)} %bitcast.y_ref, f32[16,4,8,640]{3,2,1,0:T(8,128)S(1)} %bitcast.20, f32[16,4,8,640]{3,2,1,0:T(8,128)S(1)} %collective-permute-done.16.gb_ref, f32[1024,128]{1,0:T(8,128)S(1)} %bitcast.11, f32[1024,128]{1,0:T(8,128)S(1)} %bitcast.17, f32[1024,128]{1,0:T(8,128)S(1)} %collective-permute-done.8.rest_2_, ...), custom_call_target="tpu_custom_call" | custom-call | flops 9663676416 | bytes 9437184 | tf_op jit(solution)/shard_map/finish/pallas_call | solution.py:335
  (16 shorter events, 0.1 us)
Async XLA Ops:
  0.0 1.2 copy-start
  2.0 20.3 %collective-permute-start = (f32[8,128,128]{2,1,0:T(8,128)S(1)}, f32[8,128,128]{2,1,0:T(8,128)S(1)}, u32[]{:S(2)}, u32[]{:S(2)}) collective-permute-start(f32[8,128,128]{2,1,0:T(8,128)S(1)} %get-tuple-element.7.own_ref.rest_0_), channel_id=1, source_target_pairs={{120,0},{0,8},{8,16},{16,24},{24,32},{32,40},{40,48},{48,56},{56,6... | collective-permute-start | bytes 1572872 | tf_op jit(solution)/shard_map/ppermute | solution.py:367
  4.1 18.2 %collective-permute-start.1 = (f32[8,128,128]{2,1,0:T(8,128)S(1)}, f32[8,128,128]{2,1,0:T(8,128)S(1)}, u32[]{:S(2)}, u32[]{:S(2)}) collective-permute-start(f32[8,128,128]{2,1,0:T(8,128)S(1)} %get-tuple-element.7.own_ref.rest_0_), channel_id=1, source_target_pairs={{8,0},{16,8},{24,16},{32,24},{40,32},{48,40},{56,48},{64,56},{72,6... | collective-permute-start | bytes 1572872 | tf_op jit(solution)/shard_map/ppermute | solution.py:367
  9.0 23.9 %collective-permute-start.4 = (f32[8,128,128]{2,1,0:T(8,128)S(1)}, f32[8,128,128]{2,1,0:T(8,128)S(1)}, u32[]{:S(2)}, u32[]{:S(2)}) collective-permute-start(f32[8,128,128]{2,1,0:T(8,128)S(1)} %get-tuple-element.8.own_ref.rest_0_), channel_id=1, source_target_pairs={{120,0},{0,8},{8,16},{16,24},{24,32},{32,40},{40,48},{48,56},{56,6... | collective-permute-start | bytes 1572872 | tf_op jit(solution)/shard_map/ppermute | solution.py:367
  9.0 23.9 %collective-permute-start.5 = (f32[8,128,128]{2,1,0:T(8,128)S(1)}, f32[8,128,128]{2,1,0:T(8,128)S(1)}, u32[]{:S(2)}, u32[]{:S(2)}) collective-permute-start(f32[8,128,128]{2,1,0:T(8,128)S(1)} %get-tuple-element.8.own_ref.rest_0_), channel_id=1, source_target_pairs={{8,0},{16,8},{24,16},{32,24},{40,32},{48,40},{56,48},{64,56},{72,6... | collective-permute-start | bytes 1572872 | tf_op jit(solution)/shard_map/ppermute | solution.py:367
  28.0 15.4 %collective-permute-start.2 = (f32[8,128,128]{2,1,0:T(8,128)S(1)}, f32[8,128,128]{2,1,0:T(8,128)S(1)}, u32[]{:S(2)}, u32[]{:S(2)}) collective-permute-start(f32[8,128,128]{2,1,0:T(8,128)S(1)} %field.4.own_ref), channel_id=1, source_target_pairs={{120,0},{0,8},{8,16},{16,24},{24,32},{32,40},{40,48},{48,56},{56,6... | collective-permute-start | bytes 1572872 | tf_op jit(solution)/shard_map/ppermute | solution.py:367
  28.1 15.3 %collective-permute-start.3 = (f32[8,128,128]{2,1,0:T(8,128)S(1)}, f32[8,128,128]{2,1,0:T(8,128)S(1)}, u32[]{:S(2)}, u32[]{:S(2)}) collective-permute-start(f32[8,128,128]{2,1,0:T(8,128)S(1)} %field.4.own_ref), channel_id=1, source_target_pairs={{8,0},{16,8},{24,16},{32,24},{40,32},{48,40},{56,48},{64,56},{72,6... | collective-permute-start | bytes 1572872 | tf_op jit(solution)/shard_map/ppermute | solution.py:367
  38.5 16.4 %collective-permute-start.6 = (f32[8,128,128]{2,1,0:T(8,128)S(1)}, f32[8,128,128]{2,1,0:T(8,128)S(1)}, u32[]{:S(2)}, u32[]{:S(2)}) collective-permute-start(f32[8,128,128]{2,1,0:T(8,128)S(1)} %field.6.own_ref), channel_id=1, source_target_pairs={{120,0},{0,8},{8,16},{16,24},{24,32},{32,40},{40,48},{48,56},{56,6... | collective-permute-start | bytes 1572872 | tf_op jit(solution)/shard_map/ppermute | solution.py:367
  38.6 16.3 %collective-permute-start.7 = (f32[8,128,128]{2,1,0:T(8,128)S(1)}, f32[8,128,128]{2,1,0:T(8,128)S(1)}, u32[]{:S(2)}, u32[]{:S(2)}) collective-permute-start(f32[8,128,128]{2,1,0:T(8,128)S(1)} %field.6.own_ref), channel_id=1, source_target_pairs={{8,0},{16,8},{24,16},{32,24},{40,32},{48,40},{56,48},{64,56},{72,6... | collective-permute-start | bytes 1572872 | tf_op jit(solution)/shard_map/ppermute | solution.py:367
  49.0 16.7 %collective-permute-start.8 = (f32[1024,128]{1,0:T(8,128)S(1)}, f32[1024,128]{1,0:T(8,128)S(1)}, u32[]{:S(2)}, u32[]{:S(2)}) collective-permute-start(f32[1024,128]{1,0:T(8,128)S(1)} %bitcast.6), channel_id=1, source_target_pairs={{0,1},{1,0},{2,3},{3,2},{4,5},{5,4},{6,7},{7,6},{8,9},{9,8},{10,11... | collective-permute-start | bytes 1572872 | tf_op jit(solution)/shard_map/ppermute | solution.py:375
  52.2 13.8 %collective-permute-start.10 = (f32[1024,128]{1,0:T(8,128)S(1)}, f32[1024,128]{1,0:T(8,128)S(1)}, u32[]{:S(2)}, u32[]{:S(2)}) collective-permute-start(f32[1024,128]{1,0:T(8,128)S(1)} %bitcast.7), channel_id=1, source_target_pairs={{2,0},{3,1},{4,2},{5,3},{6,4},{7,5},{0,6},{1,7},{10,8},{11,9},{12,... | collective-permute-start | bytes 1572872 | tf_op jit(solution)/shard_map/ppermute | solution.py:370
  60.6 16.6 %collective-permute-start.11 = (f32[1024,128]{1,0:T(8,128)S(1)}, f32[1024,128]{1,0:T(8,128)S(1)}, u32[]{:S(2)}, u32[]{:S(2)}) collective-permute-start(f32[1024,128]{1,0:T(8,128)S(1)} %bitcast.12), channel_id=1, source_target_pairs={{2,0},{3,1},{4,2},{5,3},{6,4},{7,5},{0,6},{1,7},{10,8},{11,9},{12,... | collective-permute-start | bytes 1572872 | tf_op jit(solution)/shard_map/ppermute | solution.py:370
  63.2 15.1 %collective-permute-start.9 = (f32[1024,128]{1,0:T(8,128)S(1)}, f32[1024,128]{1,0:T(8,128)S(1)}, u32[]{:S(2)}, u32[]{:S(2)}) collective-permute-start(f32[1024,128]{1,0:T(8,128)S(1)} %bitcast.13), channel_id=1, source_target_pairs={{0,1},{1,0},{2,3},{3,2},{4,5},{5,4},{6,7},{7,6},{8,9},{9,8},{10,11... | collective-permute-start | bytes 1572872 | tf_op jit(solution)/shard_map/ppermute | solution.py:375
  65.7 14.8 %collective-permute-start.14 = (f32[1024,128]{1,0:T(8,128)S(1)}, f32[1024,128]{1,0:T(8,128)}, u32[]{:S(2)}, u32[]{:S(2)}) collective-permute-start(f32[1024,128]{1,0:T(8,128)S(1)} %bitcast.8), channel_id=1, source_target_pairs={{6,0},{7,1},{0,2},{1,3},{2,4},{3,5},{4,6},{5,7},{14,8},{15,9},{8,1... | collective-permute-start | bytes 1572872 | tf_op jit(solution)/shard_map/ppermute | solution.py:370
  65.7 26.0 %collective-permute-start.15 = (f32[1024,128]{1,0:T(8,128)S(1)}, f32[1024,128]{1,0:T(8,128)}, u32[]{:S(2)}, u32[]{:S(2)}) collective-permute-start(f32[1024,128]{1,0:T(8,128)S(1)} %bitcast.14), channel_id=1, source_target_pairs={{6,0},{7,1},{0,2},{1,3},{2,4},{3,5},{4,6},{5,7},{14,8},{15,9},{8,1... | collective-permute-start | bytes 1572872 | tf_op jit(solution)/shard_map/ppermute | solution.py:370
  65.9 25.8 %collective-permute-start.12 = (f32[1024,128]{1,0:T(8,128)S(1)}, f32[1024,128]{1,0:T(8,128)}, u32[]{:S(2)}, u32[]{:S(2)}) collective-permute-start(f32[1024,128]{1,0:T(8,128)S(1)} %collective-permute-done.10.rest_2_.rest_4_), channel_id=1, source_target_pairs={{0,1},{1,0},{2,3},{3,2},{4,5},{5,4},{6,7},{7,6},{8,9},{9,8},{10,11... | collective-permute-start | bytes 1572872 | tf_op jit(solution)/shard_map/ppermute | solution.py:375
  77.2 14.6 %collective-permute-start.13 = (f32[1024,128]{1,0:T(8,128)S(1)}, f32[1024,128]{1,0:T(8,128)}, u32[]{:S(2)}, u32[]{:S(2)}) collective-permute-start(f32[1024,128]{1,0:T(8,128)S(1)} %collective-permute-done.11.rest_3_.rest_5_), channel_id=1, source_target_pairs={{0,1},{1,0},{2,3},{3,2},{4,5},{5,4},{6,7},{7,6},{8,9},{9,8},{10,11... | collective-permute-start | bytes 1572872 | tf_op jit(solution)/shard_map/ppermute | solution.py:375
  133.6 21.1 %collective-permute-start.16 = (f32[16,4,8,640]{3,2,1,0:T(8,128)S(1)}, f32[16,4,8,640]{3,2,1,0:T(8,128)S(1)}, u32[]{:S(2)}, u32[]{:S(2)}) collective-permute-start(f32[16,4,8,640]{3,2,1,0:T(8,128)S(1)} %bitcast.19), channel_id=1, source_target_pairs={{0,1},{1,0},{2,3},{3,2},{4,5},{5,4},{6,7},{7,6},{8,9},{9,8},{10,11... | collective-permute-start | bytes 3932168 | tf_op jit(solution)/shard_map/ppermute | solution.py:375
  137.0 13.5 %collective-permute-start.19 = (f32[1024,128]{1,0:T(8,128)S(1)}, f32[1024,128]{1,0:T(8,128)S(1)}, u32[]{:S(2)}, u32[]{:S(2)}) collective-permute-start(f32[1024,128]{1,0:T(8,128)S(1)} %collective-permute-done.10.rest_2_.rest_4_), channel_id=1, source_target_pairs={{2,0},{3,1},{4,2},{5,3},{6,4},{7,5},{0,6},{1,7},{10,8},{11,9},{12,... | collective-permute-start | bytes 1572872 | tf_op jit(solution)/shard_map/ppermute | solution.py:370
  137.4 14.6 %collective-permute-start.20 = (f32[1024,128]{1,0:T(8,128)}, f32[1024,128]{1,0:T(8,128)S(1)}, u32[]{:S(2)}, u32[]{:S(2)}) collective-permute-start(f32[1024,128]{1,0:T(8,128)} %collective-permute-done.15.rest_7_.rest_9_), channel_id=1, source_target_pairs={{6,0},{7,1},{0,2},{1,3},{2,4},{3,5},{4,6},{5,7},{14,8},{15,9},{8,1... | collective-permute-start | bytes 1572872 | tf_op jit(solution)/shard_map/ppermute | solution.py:370
  138.5 14.7 %collective-permute-start.17 = (f32[1024,128]{1,0:T(8,128)}, f32[1024,128]{1,0:T(8,128)S(1)}, u32[]{:S(2)}, u32[]{:S(2)}) collective-permute-start(f32[1024,128]{1,0:T(8,128)} %collective-permute-done.14.rest_6_.rest_8_), channel_id=1, source_target_pairs={{0,1},{1,0},{2,3},{3,2},{4,5},{5,4},{6,7},{7,6},{8,9},{9,8},{10,11... | collective-permute-start | bytes 1572872 | tf_op jit(solution)/shard_map/ppermute | solution.py:375
  139.0 14.1 %collective-permute-start.18 = (f32[1024,128]{1,0:T(8,128)}, f32[1024,128]{1,0:T(8,128)S(1)}, u32[]{:S(2)}, u32[]{:S(2)}) collective-permute-start(f32[1024,128]{1,0:T(8,128)} %collective-permute-done.15.rest_7_.rest_9_), channel_id=1, source_target_pairs={{0,1},{1,0},{2,3},{3,2},{4,5},{5,4},{6,7},{7,6},{8,9},{9,8},{10,11... | collective-permute-start | bytes 1572872 | tf_op jit(solution)/shard_map/ppermute | solution.py:375
  150.5 2.7 %collective-permute-start.21 = (f32[1024,128]{1,0:T(8,128)S(1)}, f32[1024,128]{1,0:T(8,128)S(1)}, u32[]{:S(2)}, u32[]{:S(2)}) collective-permute-start(f32[1024,128]{1,0:T(8,128)S(1)} %collective-permute-done.19.rest_12_), channel_id=1, source_target_pairs={{0,1},{1,0},{2,3},{3,2},{4,5},{5,4},{6,7},{7,6},{8,9},{9,8},{10,11... | collective-permute-start | bytes 1572872 | tf_op jit(solution)/shard_map/ppermute | solution.py:375
  152.0 2.7 %collective-permute-start.22 = (f32[1024,128]{1,0:T(8,128)S(1)}, f32[1024,128]{1,0:T(8,128)S(1)}, u32[]{:S(2)}, u32[]{:S(2)}) collective-permute-start(f32[1024,128]{1,0:T(8,128)S(1)} %collective-permute-done.20.rest_13_), channel_id=1, source_target_pairs={{0,1},{1,0},{2,3},{3,2},{4,5},{5,4},{6,7},{7,6},{8,9},{9,8},{10,11... | collective-permute-start | bytes 1572872 | tf_op jit(solution)/shard_map/ppermute | solution.py:375

commit v5 on v4

--- a/solution.py
+++ b/solution.py
@@ -92,15 +92,29 @@
     return pltpu.roll(x, x.shape[1] // 2, 1)
 
 
-def pack_kernel(v_ref, a_ref, b_ref):
-    low = lanes_low(v_ref.shape[1:])
+PACK_GROUPS = 4
+
+
+def pack_kernel(v_ref, a_ref, b_ref, buffer, arrived):
+    low = lanes_low(buffer.shape[1:])
     half = a_ref.shape[0]
-
-    @pl.loop(0, half)
-    def _(j):
-        one, two = v_ref[j], v_ref[j + half]
-        a_ref[j] = jnp.where(low, one, turn(two))
-        b_ref[j] = jnp.where(low, turn(one), two)
+    group = half // PACK_GROUPS
+    copies = []
+    for g in range(PACK_GROUPS):
+        for side in range(2):
+            blocks = pl.ds(side * half + g * group, group)
+            copy = pltpu.make_async_copy(
+                v_ref.at[blocks], buffer.at[blocks], arrived.at[2 * g + side]
+            )
+            copy.start()
+            copies.append(copy)
+    for g in range(PACK_GROUPS):
+        copies[2 * g].wait()
+        copies[2 * g + 1].wait()
+        for j in range(g * group, (g + 1) * group):
+            one, two = buffer[j], buffer[j + half]
+            a_ref[j] = jnp.where(low, one, turn(two))
+            b_ref[j] = jnp.where(low, turn(one), two)
 
 
 def pack(blocks):
@@ -109,8 +123,12 @@
     return pl.pallas_call(
         pack_kernel,
         out_shape=(shape, shape),
-        in_specs=[VMEM_SPEC],
+        in_specs=[pl.BlockSpec(memory_space=pl.ANY)],
         out_specs=(VMEM_SPEC, VMEM_SPEC),
+        scratch_shapes=[
+            pltpu.VMEM(blocks.shape, F32),
+            pltpu.SemaphoreType.DMA((2 * PACK_GROUPS,)),
+        ],
         compiler_params=pltpu.CompilerParams(vmem_limit_bytes=30 * 2**20),
         cost_estimate=cost(0, 8 * blocks.size),
         name="pack",
@@ -184,14 +202,15 @@
 NEAR_BLOCKS = 2
 
 
-def gram_product(left, right):
-    total = None
-    for part in range(2):
-        lhs = jnp.concatenate(split(natural(left, slice(None), part).T), axis=0)
-        rhs = jnp.concatenate(split(natural(right, slice(None), part)), axis=1)
-        term = mm(lhs, rhs)
-        total = term if total is None else total + term
-    return fold(total)
+def turned(refs, part):
+    half = refs[0].shape[1] // 2
+    lines = slice(part * half, (part + 1) * half)
+    both = jnp.concatenate([ref[...].T[lines] for ref in refs], axis=0)
+    return jnp.concatenate(split(both), axis=0)
+
+
+def paired(refs, part):
+    return jnp.concatenate(split(natural(refs, slice(None), part)), axis=1)
 
 
 def columns_of(ref, block):
@@ -200,38 +219,62 @@
 
 def near_kernel(*rest):
     own, beside = (rest[2 * n : 2 * n + 2] for n in range(2))
-    out_ref = rest[4]
+    out_ref, lhs = rest[4:]
+    for part in range(2):
+        lhs[part] = turned(own, part)
     for block, refs in enumerate((own, beside)):
-        columns_of(out_ref, block)[...] = gram_product(own, refs)
-
-
-def far_kernel(y_ref, near_ref, *rest):
-    own, up, up_s, down = (rest[2 * n : 2 * n + 2] for n in range(4))
-    out_ref = rest[8]
+        terms = [mm(lhs[part], paired(refs, part)) for part in range(2)]
+        columns_of(out_ref, block)[...] = fold(terms[0] + terms[1])
+
+
+def far_kernel(y_ref, near_ref, lhs_ref, *rest):
+    up, up_s, down = (rest[2 * n : 2 * n + 2] for n in range(3))
+    out_ref, rhs = rest[6:]
     out_ref[:, : NEAR_BLOCKS * 128] = near_ref[...]
-    columns_of(out_ref, 2)[...] = gram_product(own, up)
-    columns_of(out_ref, 3)[...] = gram_product(own, up_s)
-
-    @pl.when(y_ref[0] < 2)
-    def _():
-        columns_of(out_ref, 4)[...] = gram_product(down, up)
-
-    @pl.when(y_ref[0] >= 2)
-    def _():
-        columns_of(out_ref, 4)[...] = gram_product(down, up_s)
-
-
-def gram_call(kernel, blocks, products, before, pieces):
-    operands = [chunk for piece in pieces for chunk in piece]
+    for which, refs in enumerate((up, up_s)):
+        for part in range(2):
+            rhs[2 * which + part] = paired(refs, part)
+        terms = [mm(lhs_ref[part], rhs[2 * which + part]) for part in range(2)]
+        columns_of(out_ref, NEAR_BLOCKS + which)[...] = fold(terms[0] + terms[1])
+    side = jnp.where(y_ref[0] < 2, 0, 2)
+    terms = [mm(turned(down, part), rhs[side + part]) for part in range(2)]
+    columns_of(out_ref, 4)[...] = fold(terms[0] + terms[1])
+
+
+def flat(pieces):
+    return [chunk for piece in pieces for chunk in piece]
+
+
+def gram_near(pieces):
+    operands = flat(pieces)
     rows, cols = operands[0].shape
     return pl.pallas_call(
-        kernel,
-        out_shape=jax.ShapeDtypeStruct((cols, blocks * cols), F32),
-        in_specs=([SMEM_SPEC, VMEM_SPEC] if before else []) + [VMEM_SPEC] * len(operands),
+        near_kernel,
+        out_shape=(
+            jax.ShapeDtypeStruct((cols, NEAR_BLOCKS * cols), F32),
+            jax.ShapeDtypeStruct((2, 2 * cols, rows), BF),
+        ),
+        in_specs=[VMEM_SPEC] * len(operands),
+        out_specs=(VMEM_SPEC, VMEM_SPEC),
+        compiler_params=pltpu.CompilerParams(vmem_limit_bytes=30 * 2**20),
+        cost_estimate=cost(32 * rows * cols * cols, 16 * rows * cols),
+        name="gram_near",
+    )(*operands)
+
+
+def gram_far(y, near, lhs, pieces):
+    operands = flat(pieces)
+    rows, cols = operands[0].shape
+    return pl.pallas_call(
+        far_kernel,
+        out_shape=jax.ShapeDtypeStruct((cols, GRAM_BLOCKS * cols), F32),
+        in_specs=[SMEM_SPEC] + [VMEM_SPEC] * (2 + len(operands)),
         out_specs=VMEM_SPEC,
+        scratch_shapes=[pltpu.VMEM((4, rows, 2 * cols), BF)],
         compiler_params=pltpu.CompilerParams(vmem_limit_bytes=30 * 2**20),
-        cost_estimate=cost(16 * rows * cols * cols * products, 4 * rows * cols * len(operands)),
-    )(*before, *operands)
+        cost_estimate=cost(48 * rows * cols * cols, 24 * rows * cols),
+        name="gram_far",
+    )(y, near, lhs, *operands)
 
 
 KEEP = {0: 1, 3: 2, 4: 1, 8: 1}
@@ -325,8 +368,10 @@
             within = pl.ds(pl.multiple_of(step * chunk, chunk), chunk)
             rows = pl.ds(pl.multiple_of(part * half + step * chunk, chunk), chunk)
             parts = [natural(refs, within, part) for refs in x_refs]
-            lhs = jnp.concatenate(split(jnp.concatenate(parts, axis=1)), axis=0)
-            out_ref[rows, :] = fold(mm(lhs, ordered[...]))
+            high, low = split(jnp.concatenate(parts, axis=1))
+            full = mm(high, ordered[...])
+            cols = full.shape[1] // 2
+            out_ref[rows, :] = (full[:, :cols] + full[:, cols:]) + mm(low, ordered[:, :cols])
 
 
 def finish(total_rows, y, gram_a, gram_b, pieces):
@@ -394,8 +439,8 @@
         down_s.append(swap(down[-1]))
         across.append(from_y((up, down)[chunk][-1], (1, -1)[chunk]))
         across_s.append(swap(across[-1]))
-    near = gram_call(near_kernel, NEAR_BLOCKS, 2, (), (own, own_s))
-    share = gram_call(far_kernel, GRAM_BLOCKS, 3, (y, near), (own, up, up_s, down))
+    near, lhs = gram_near((own, own_s))
+    share = gram_far(y, near, lhs, (up, up_s, down))
     strip = share.shape[0] // row_count
     parts = lax.all_to_all(
         share.reshape(row_count, strip, -1), "row", split_axis=0, concat_axis=0, tiled=True

time: 176 us -> 175 us (level)
  waiting for transfers between devices: 35 us -> 32.7 us
  local copies, waits for them, and re-layouts: 1.4 us -> 3.23 us
    ppermute x6, waiting for transfers between devices: 33.4 us -> 31.2 us  [from_y(): lax.ppermute(value, 'vec', [((i + 2 * step) % vec_count, i) for i in rang...]
    unnamed x2 -> x8, local copies, waits for them, and re-layouts: 1.22 us -> 3.06 us
  transfers between devices with their start and end apart: 23 -> 23, of which waited for: 7 -> 5; matrix products, arithmetic and copies ran while one was open for 1% -> 1% of each run, Pallas kernels for 17% -> 18%
where the time goes in v5:
time: 175 us; the launch traced here: 174 us
  Pallas kernels  56.6 us (32%)
  starting transfers between devices  42.2 us (24%)
  blocking collectives  37.2 us (21%)
  waiting for transfers between devices  32.7 us (19%)
  local copies, waits for them, and re-layouts  3.23 us (2%)
    ppermute x6, waiting for transfers between devices, from_y(): lax.ppermute(value, 'vec', [((i + 2 * step) % vec_count, i) for i in rang...  31.2 us
    all_to_all x1, blocking collectives, on_device(): lax.all_to_all(jnp.broadcast_to(part[None], (members,) + part.shape), ('r...  22.9 us
    pallas_call x4, Pallas kernels, apply_field(): pl.pallas_call(functools.partial(field_kernel, second), out_shape=jax.Sha...  22.7 us
    ppermute x8, starting transfers between devices, from_row(): lax.ppermute(value, 'row', [((i + step) % row_count, i) for i in range(ro...  21.4 us
    pallas_call x1, Pallas kernels, finish(): pl.pallas_call(functools.partial(finish_kernel, total_rows), out_shape=ja...  20.6 us
    all_to_all x1, blocking collectives, on_device(): lax.all_to_all(share.reshape(row_count, strip, -1), 'row', split_axis=0,...  14.3 us
    ppermute x9, starting transfers between devices, swap(): return lax.ppermute(value, 'vec', [(i, i ^ 1) for i in range(vec_count)])  14 us
    ppermute x6, starting transfers between devices, from_y(): lax.ppermute(value, 'vec', [((i + 2 * step) % vec_count, i) for i in rang...  6.84 us
  transfers between devices with their start and end apart: 23, of which 5 were waited for; matrix products, arithmetic and copies ran while one was open for 1% of the time, Pallas kernels for 18%

profile of v5, /device:TPU:1, one launch (start us, length us, event | category | flops | bytes accessed | tf_op | source)
XLA Modules:
  0.0 174.3 jit_solution(5689149411360151827)
XLA Ops:
  0.0 1.2 copy-done
  1.2 1.9 %pack.1 = (f32[8,128,128]{2,1,0:T(8,128)S(1)}, f32[8,128,128]{2,1,0:T(8,128)S(1)}) custom-call(f32[16,128,128]{2,1,0:T(8,128)S(1)} %bitcast.19), custom_call_target="tpu_custom_call" | custom-call | bytes 2097152 | tf_op jit(solution)/shard_map/pack/pallas_call | solution.py:123
  3.2 2.1 %collective-permute-start = (f32[8,128,128]{2,1,0:T(8,128)S(1)}, f32[8,128,128]{2,1,0:T(8,128)S(1)}, u32[]{:S(2)}, u32[]{:S(2)}) collective-permute-start(f32[8,128,128]{2,1,0:T(8,128)S(1)} %get-tuple-element.9.own_ref.rest_0_), channel_id=1, source_target_pairs={{120,0},{0,8},{8,16},{16,24},{24,32},{32,40},{40,48},{48,56},{56,6... | collective-permute-start | bytes 1572872 | tf_op jit(solution)/shard_map/ppermute | solution.py:412
  5.3 4.8 %collective-permute-start.1 = (f32[8,128,128]{2,1,0:T(8,128)S(1)}, f32[8,128,128]{2,1,0:T(8,128)S(1)}, u32[]{:S(2)}, u32[]{:S(2)}) collective-permute-start(f32[8,128,128]{2,1,0:T(8,128)S(1)} %get-tuple-element.9.own_ref.rest_0_), channel_id=1, source_target_pairs={{8,0},{16,8},{24,16},{32,24},{40,32},{48,40},{56,48},{64,56},{72,6... | collective-permute-start | bytes 1572872 | tf_op jit(solution)/shard_map/ppermute | solution.py:412
  10.1 4.8 %collective-permute-start.5 = (f32[8,128,128]{2,1,0:T(8,128)S(1)}, f32[8,128,128]{2,1,0:T(8,128)S(1)}, u32[]{:S(2)}, u32[]{:S(2)}) collective-permute-start(f32[8,128,128]{2,1,0:T(8,128)S(1)} %get-tuple-element.10.own_ref.rest_0_), channel_id=1, source_target_pairs={{8,0},{16,8},{24,16},{32,24},{40,32},{48,40},{56,48},{64,56},{72,6... | collective-permute-start | bytes 1572872 | tf_op jit(solution)/shard_map/ppermute | solution.py:412
  14.9 0.8 fusion.2
  17.0 0.1 reshape.30.cols_ref
  17.1 6.3 %split_blocks.1.h_ref = bf16[16,12,256,128]{3,2,1,0:T(8,128)(2,1)S(1)} custom-call(f32[16,12,128,128]{3,2,1,0:T(8,128)} %h_ref.1), custom_call_target="tpu_custom_call" | custom-call | bytes 25165824 | tf_op jit(solution)/shard_map/split_blocks/pallas_call | solution.py:65
  23.4 0.1 pad_maximum_fusion.coef_ref
  23.5 0.0 collective-permute-done.left_ref
  23.5 0.0 collective-permute-done.1.right_ref
  23.5 5.7 %field.4.own_ref = f32[8,128,128]{2,1,0:T(8,128)S(1)} custom-call(s32[192]{0:T(256)S(1)} %reshape.30.cols_ref, f32[2]{0:T(128)S(1)} %pad_maximum_fusion.coef_ref, bf16[16,12,256,128]{3,2,1,0:T(8,128)(2,1)S(1)} %split_blocks.1.h_ref, f32[8,128,128]{2,1,0:T(8,128)S(1)} %collective-permute-done.left_ref, f32[8,128,128]{2,1,0:T(8,128)S(1)} %get-tuple-element.9.own_ref.rest_0_, ...), custom_call_target="tpu_custom_call" | custom-call | flops 3221225472 | bytes 12582912 | tf_op jit(solution)/shard_map/field/pallas_call | solution.py:183
  29.1 0.1 collective-permute-start.2
  29.2 4.8 %collective-permute-start.3 = (f32[8,128,128]{2,1,0:T(8,128)S(1)}, f32[8,128,128]{2,1,0:T(8,128)S(1)}, u32[]{:S(2)}, u32[]{:S(2)}) collective-permute-start(f32[8,128,128]{2,1,0:T(8,128)S(1)} %field.4.own_ref), channel_id=1, source_target_pairs={{8,0},{16,8},{24,16},{32,24},{40,32},{48,40},{56,48},{64,56},{72,6... | collective-permute-start | bytes 1572872 | tf_op jit(solution)/shard_map/ppermute | solution.py:412
  34.0 5.7 %field.6.own_ref = f32[8,128,128]{2,1,0:T(8,128)S(1)} custom-call(s32[192]{0:T(256)S(1)} %reshape.30.cols_ref, f32[2]{0:T(128)S(1)} %pad_maximum_fusion.coef_ref, bf16[16,12,256,128]{3,2,1,0:T(8,128)(2,1)S(1)} %split_blocks.1.h_ref, f32[8,128,128]{2,1,0:T(8,128)S(1)} %collective-permute-done.4.left_ref, ...), custom_call_target="tpu_custom_call" | custom-call | flops 3221225472 | bytes 12582912 | tf_op jit(solution)/shard_map/field/pallas_call | solution.py:183
  39.7 0.1 collective-permute-start.6
  39.7 4.8 %collective-permute-start.7 = (f32[8,128,128]{2,1,0:T(8,128)S(1)}, f32[8,128,128]{2,1,0:T(8,128)S(1)}, u32[]{:S(2)}, u32[]{:S(2)}) collective-permute-start(f32[8,128,128]{2,1,0:T(8,128)S(1)} %field.6.own_ref), channel_id=1, source_target_pairs={{8,0},{16,8},{24,16},{32,24},{40,32},{48,40},{56,48},{64,56},{72,6... | collective-permute-start | bytes 1572872 | tf_op jit(solution)/shard_map/ppermute | solution.py:412
  44.5 0.0 collective-permute-done.3.right_ref
  44.5 5.7 %field.5 = f32[8,128,128]{2,1,0:T(8,128)S(1)} custom-call(s32[192]{0:T(256)S(1)} %reshape.30.cols_ref, f32[2]{0:T(128)S(1)} %pad_maximum_fusion.coef_ref, bf16[16,12,256,128]{3,2,1,0:T(8,128)(2,1)S(1)} %split_blocks.1.h_ref, f32[8,128,128]{2,1,0:T(8,128)S(1)} %collective-permute-done.2.left_ref, f32[8,128,128]{2,1,0:T(8,128)S(1)} %field.4.own_ref, ...), custom_call_target="tpu_custom_call" | custom-call | flops 3221225472 | bytes 12582912 | tf_op jit(solution)/shard_map/field/pallas_call | solution.py:183
  50.2 3.1 %collective-permute-start.8 = (f32[1024,128]{1,0:T(8,128)S(1)}, f32[1024,128]{1,0:T(8,128)S(1)}, u32[]{:S(2)}, u32[]{:S(2)}) collective-permute-start(f32[1024,128]{1,0:T(8,128)S(1)} %bitcast.6), channel_id=1, source_target_pairs={{0,1},{1,0},{2,3},{3,2},{4,5},{5,4},{6,7},{7,6},{8,9},{9,8},{10,11... | collective-permute-start | bytes 1572872 | tf_op jit(solution)/shard_map/ppermute | solution.py:420
  53.3 2.7 %collective-permute-start.10 = (f32[1024,128]{1,0:T(8,128)S(1)}, f32[1024,128]{1,0:T(8,128)S(1)}, u32[]{:S(2)}, u32[]{:S(2)}) collective-permute-start(f32[1024,128]{1,0:T(8,128)S(1)} %bitcast.7), channel_id=1, source_target_pairs={{2,0},{3,1},{4,2},{5,3},{6,4},{7,5},{0,6},{1,7},{10,8},{11,9},{12,... | collective-permute-start | bytes 1572872 | tf_op jit(solution)/shard_map/ppermute | solution.py:415
  56.1 0.0 collective-permute-done.6.left_ref
  56.1 5.7 %field.7 = f32[8,128,128]{2,1,0:T(8,128)S(1)} custom-call(s32[192]{0:T(256)S(1)} %reshape.30.cols_ref, f32[2]{0:T(128)S(1)} %pad_maximum_fusion.coef_ref, bf16[16,12,256,128]{3,2,1,0:T(8,128)(2,1)S(1)} %split_blocks.1.h_ref, f32[8,128,128]{2,1,0:T(8,128)S(1)} %collective-permute-done.6.left_ref, f32[8,128,128]{2,1,0:T(8,128)S(1)} %field.6.own_ref, ...), custom_call_target="tpu_custom_call" | custom-call | flops 3221225472 | bytes 12582912 | tf_op jit(solution)/shard_map/field/pallas_call | solution.py:183
  61.7 2.6 %collective-permute-start.11 = (f32[1024,128]{1,0:T(8,128)S(1)}, f32[1024,128]{1,0:T(8,128)S(1)}, u32[]{:S(2)}, u32[]{:S(2)}) collective-permute-start(f32[1024,128]{1,0:T(8,128)S(1)} %bitcast.11), channel_id=1, source_target_pairs={{2,0},{3,1},{4,2},{5,3},{6,4},{7,5},{0,6},{1,7},{10,8},{11,9},{12,... | collective-permute-start | bytes 1572872 | tf_op jit(solution)/shard_map/ppermute | solution.py:415
  64.4 2.5 %collective-permute-start.9 = (f32[1024,128]{1,0:T(8,128)S(1)}, f32[1024,128]{1,0:T(8,128)}, u32[]{:S(2)}, u32[]{:S(2)}) collective-permute-start(f32[1024,128]{1,0:T(8,128)S(1)} %bitcast.12), channel_id=1, source_target_pairs={{0,1},{1,0},{2,3},{3,2},{4,5},{5,4},{6,7},{7,6},{8,9},{9,8},{10,11... | collective-permute-start | bytes 1572872 | tf_op jit(solution)/shard_map/ppermute | solution.py:420
  66.9 0.8 copy-done.1
  67.7 0.0 collective-permute-start.15
  67.7 1.2 collective-permute-start.12
  68.9 9.4 %collective-permute-done.11.rest_1_.rest_5_ = f32[1024,128]{1,0:T(8,128)S(1)} collective-permute-done((f32[1024,128]{1,0:T(8,128)S(1)}, f32[1024,128]{1,0:T(8,128)S(1)}, u32[]{:S(2)}, u32[]{:S(2)}) %collective-permute-start.11) | collective-permute-done | bytes 524320 | tf_op jit(solution)/shard_map/ppermute | solution.py:415
  78.3 1.1 collective-permute-start.13
  79.4 1.0 copy-done.2
  80.5 2.4 %gram_near.1 = (f32[128,256]{1,0:T(8,128)S(1)}, bf16[2,256,1024]{2,1,0:T(8,128)(2,1)S(1)}) custom-call(f32[1024,128]{1,0:T(8,128)S(1)} %bitcast.9, f32[1024,128]{1,0:T(8,128)S(1)} %bitcast.14, f32[1024,128]{1,0:T(8,128)S(1)} %copy-done.2, f32[1024,128]{1,0:T(8,128)} %collective-permute-done.9.rest_3_), custom_call_target="tpu_custom_call" | custom-call | flops 536870912 | bytes 2097152 | tf_op jit(solution)/shard_map/gram_near/pallas_call | solution.py:251
  82.9 9.9 %collective-permute-done.15.rest_5_.rest_9_ = f32[1024,128]{1,0:T(8,128)S(1)} collective-permute-done((f32[1024,128]{1,0:T(8,128)S(1)}, f32[1024,128]{1,0:T(8,128)S(1)}, u32[]{:S(2)}, u32[]{:S(2)}) %collective-permute-start.15) | collective-permute-done | bytes 524320 | tf_op jit(solution)/shard_map/ppermute | solution.py:415
  92.8 2.6 %gram_far.1 = f32[128,640]{1,0:T(8,128)S(1)} custom-call(s32[1]{0:T(128)} %bitcast.y_ref, f32[128,256]{1,0:T(8,128)S(1)} %get-tuple-element.11.near_ref, bf16[2,256,1024]{2,1,0:T(8,128)(2,1)S(1)} %get-tuple-element.12.lhs_ref, f32[1024,128]{1,0:T(8,128)S(1)} %collective-permute-done.10.rest_0_.rest_4_, ...), custom_call_target="tpu_custom_call" | custom-call | flops 805306368 | bytes 3145728 | tf_op jit(solution)/shard_map/gram_far/pallas_call | solution.py:268
  95.4 14.3 %all_to_all.10 = f32[16,8,640]{2,1,0:T(8,128)S(1)} all-to-all(f32[16,8,640]{2,1,0:T(8,128)S(1)} %bitcast.16), channel_id=1, replica_groups=mesh['row'=16,'vec'=8] {'row'}, dimensions={0} | all-to-all | bytes 655360 | tf_op jit(solution)/shard_map/all_to_all | solution.py:445
  109.8 0.1 broadcast_in_dim.17
  109.8 0.0 copy-start.3
  109.9 22.9 %all_to_all.11 = f32[64,8,640]{2,1,0:T(8,128)S(1)} all-to-all(f32[64,8,640]{2,1,0:T(8,128)S(1)} %broadcast_in_dim.17), channel_id=1, replica_groups={{0,2,4,6,8,10,12,14,16,18,20,22,24,26,28,30,32,34,36,38,40,42,44,46,48,..., dimensions={0} | all-to-all | bytes 2621440 | tf_op jit(solution)/shard_map/all_to_all | solution.py:454
  132.8 3.4 %collective-permute-start.16 = (f32[16,4,8,640]{3,2,1,0:T(8,128)S(1)}, f32[16,4,8,640]{3,2,1,0:T(8,128)S(1)}, u32[]{:S(2)}, u32[]{:S(2)}) collective-permute-start(f32[16,4,8,640]{3,2,1,0:T(8,128)S(1)} %bitcast.17), channel_id=1, source_target_pairs={{0,1},{1,0},{2,3},{3,2},{4,5},{5,4},{6,7},{7,6},{8,9},{9,8},{10,11... | collective-permute-start | bytes 3932168 | tf_op jit(solution)/shard_map/ppermute | solution.py:420
  136.2 0.4 collective-permute-start.19
  136.6 1.1 collective-permute-start.20
  137.7 0.6 collective-permute-start.17
  138.2 11.4 %collective-permute-done.19.rest_12_ = f32[1024,128]{1,0:T(8,128)S(1)} collective-permute-done((f32[1024,128]{1,0:T(8,128)S(1)}, f32[1024,128]{1,0:T(8,128)S(1)}, u32[]{:S(2)}, u32[]{:S(2)}) %collective-permute-start.19) | collective-permute-done | bytes 524320 | tf_op jit(solution)/shard_map/ppermute | solution.py:415
  149.7 0.9 collective-permute-start.21
  150.6 0.5 collective-permute-done.20.rest_13_
  151.0 1.1 collective-permute-start.22
  152.2 1.5 collective-permute-done.22.rest_15_
  153.7 20.6 %finish.1 = f32[2048,128]{1,0:T(8,128)} custom-call(s32[1]{0:T(128)} %bitcast.y_ref, f32[16,4,8,640]{3,2,1,0:T(8,128)S(1)} %bitcast.18, f32[16,4,8,640]{3,2,1,0:T(8,128)S(1)} %collective-permute-done.16.gb_ref, f32[1024,128]{1,0:T(8,128)S(1)} %bitcast.10, f32[1024,128]{1,0:T(8,128)S(1)} %bitcast.15, f32[1024,128]{1,0:T(8,128)S(1)} %copy-done.3, ...), custom_call_target="tpu_custom_call" | custom-call | flops 9663676416 | bytes 9437184 | tf_op jit(solution)/shard_map/finish/pallas_call | solution.py:380
  (22 shorter events, 0.1 us)
Async XLA Ops:
  0.0 1.2 copy-start
  3.2 20.3 %collective-permute-start = (f32[8,128,128]{2,1,0:T(8,128)S(1)}, f32[8,128,128]{2,1,0:T(8,128)S(1)}, u32[]{:S(2)}, u32[]{:S(2)}) collective-permute-start(f32[8,128,128]{2,1,0:T(8,128)S(1)} %get-tuple-element.9.own_ref.rest_0_), channel_id=1, source_target_pairs={{120,0},{0,8},{8,16},{16,24},{24,32},{32,40},{40,48},{48,56},{56,6... | collective-permute-start | bytes 1572872 | tf_op jit(solution)/shard_map/ppermute | solution.py:412
  5.3 18.2 %collective-permute-start.1 = (f32[8,128,128]{2,1,0:T(8,128)S(1)}, f32[8,128,128]{2,1,0:T(8,128)S(1)}, u32[]{:S(2)}, u32[]{:S(2)}) collective-permute-start(f32[8,128,128]{2,1,0:T(8,128)S(1)} %get-tuple-element.9.own_ref.rest_0_), channel_id=1, source_target_pairs={{8,0},{16,8},{24,16},{32,24},{40,32},{48,40},{56,48},{64,56},{72,6... | collective-permute-start | bytes 1572872 | tf_op jit(solution)/shard_map/ppermute | solution.py:412
  10.1 23.9 %collective-permute-start.4 = (f32[8,128,128]{2,1,0:T(8,128)S(1)}, f32[8,128,128]{2,1,0:T(8,128)S(1)}, u32[]{:S(2)}, u32[]{:S(2)}) collective-permute-start(f32[8,128,128]{2,1,0:T(8,128)S(1)} %get-tuple-element.10.own_ref.rest_0_), channel_id=1, source_target_pairs={{120,0},{0,8},{8,16},{16,24},{24,32},{32,40},{40,48},{48,56},{56,6... | collective-permute-start | bytes 1572872 | tf_op jit(solution)/shard_map/ppermute | solution.py:412
  10.1 23.9 %collective-permute-start.5 = (f32[8,128,128]{2,1,0:T(8,128)S(1)}, f32[8,128,128]{2,1,0:T(8,128)S(1)}, u32[]{:S(2)}, u32[]{:S(2)}) collective-permute-start(f32[8,128,128]{2,1,0:T(8,128)S(1)} %get-tuple-element.10.own_ref.rest_0_), channel_id=1, source_target_pairs={{8,0},{16,8},{24,16},{32,24},{40,32},{48,40},{56,48},{64,56},{72,6... | collective-permute-start | bytes 1572872 | tf_op jit(solution)/shard_map/ppermute | solution.py:412
  29.1 15.4 %collective-permute-start.2 = (f32[8,128,128]{2,1,0:T(8,128)S(1)}, f32[8,128,128]{2,1,0:T(8,128)S(1)}, u32[]{:S(2)}, u32[]{:S(2)}) collective-permute-start(f32[8,128,128]{2,1,0:T(8,128)S(1)} %field.4.own_ref), channel_id=1, source_target_pairs={{120,0},{0,8},{8,16},{16,24},{24,32},{32,40},{40,48},{48,56},{56,6... | collective-permute-start | bytes 1572872 | tf_op jit(solution)/shard_map/ppermute | solution.py:412
  29.2 15.3 %collective-permute-start.3 = (f32[8,128,128]{2,1,0:T(8,128)S(1)}, f32[8,128,128]{2,1,0:T(8,128)S(1)}, u32[]{:S(2)}, u32[]{:S(2)}) collective-permute-start(f32[8,128,128]{2,1,0:T(8,128)S(1)} %field.4.own_ref), channel_id=1, source_target_pairs={{8,0},{16,8},{24,16},{32,24},{40,32},{48,40},{56,48},{64,56},{72,6... | collective-permute-start | bytes 1572872 | tf_op jit(solution)/shard_map/ppermute | solution.py:412
  39.7 16.4 %collective-permute-start.6 = (f32[8,128,128]{2,1,0:T(8,128)S(1)}, f32[8,128,128]{2,1,0:T(8,128)S(1)}, u32[]{:S(2)}, u32[]{:S(2)}) collective-permute-start(f32[8,128,128]{2,1,0:T(8,128)S(1)} %field.6.own_ref), channel_id=1, source_target_pairs={{120,0},{0,8},{8,16},{16,24},{24,32},{32,40},{40,48},{48,56},{56,6... | collective-permute-start | bytes 1572872 | tf_op jit(solution)/shard_map/ppermute | solution.py:412
  39.7 16.3 %collective-permute-start.7 = (f32[8,128,128]{2,1,0:T(8,128)S(1)}, f32[8,128,128]{2,1,0:T(8,128)S(1)}, u32[]{:S(2)}, u32[]{:S(2)}) collective-permute-start(f32[8,128,128]{2,1,0:T(8,128)S(1)} %field.6.own_ref), channel_id=1, source_target_pairs={{8,0},{16,8},{24,16},{32,24},{40,32},{48,40},{56,48},{64,56},{72,6... | collective-permute-start | bytes 1572872 | tf_op jit(solution)/shard_map/ppermute | solution.py:412
  50.2 16.7 %collective-permute-start.8 = (f32[1024,128]{1,0:T(8,128)S(1)}, f32[1024,128]{1,0:T(8,128)S(1)}, u32[]{:S(2)}, u32[]{:S(2)}) collective-permute-start(f32[1024,128]{1,0:T(8,128)S(1)} %bitcast.6), channel_id=1, source_target_pairs={{0,1},{1,0},{2,3},{3,2},{4,5},{5,4},{6,7},{7,6},{8,9},{9,8},{10,11... | collective-permute-start | bytes 1572872 | tf_op jit(solution)/shard_map/ppermute | solution.py:420
  53.3 14.4 %collective-permute-start.10 = (f32[1024,128]{1,0:T(8,128)S(1)}, f32[1024,128]{1,0:T(8,128)S(1)}, u32[]{:S(2)}, u32[]{:S(2)}) collective-permute-start(f32[1024,128]{1,0:T(8,128)S(1)} %bitcast.7), channel_id=1, source_target_pairs={{2,0},{3,1},{4,2},{5,3},{6,4},{7,5},{0,6},{1,7},{10,8},{11,9},{12,... | collective-permute-start | bytes 1572872 | tf_op jit(solution)/shard_map/ppermute | solution.py:415
  61.7 16.6 %collective-permute-start.11 = (f32[1024,128]{1,0:T(8,128)S(1)}, f32[1024,128]{1,0:T(8,128)S(1)}, u32[]{:S(2)}, u32[]{:S(2)}) collective-permute-start(f32[1024,128]{1,0:T(8,128)S(1)} %bitcast.11), channel_id=1, source_target_pairs={{2,0},{3,1},{4,2},{5,3},{6,4},{7,5},{0,6},{1,7},{10,8},{11,9},{12,... | collective-permute-start | bytes 1572872 | tf_op jit(solution)/shard_map/ppermute | solution.py:415
  64.4 15.1 %collective-permute-start.9 = (f32[1024,128]{1,0:T(8,128)S(1)}, f32[1024,128]{1,0:T(8,128)}, u32[]{:S(2)}, u32[]{:S(2)}) collective-permute-start(f32[1024,128]{1,0:T(8,128)S(1)} %bitcast.12), channel_id=1, source_target_pairs={{0,1},{1,0},{2,3},{3,2},{4,5},{5,4},{6,7},{7,6},{8,9},{9,8},{10,11... | collective-permute-start | bytes 1572872 | tf_op jit(solution)/shard_map/ppermute | solution.py:420
  66.9 16.1 %collective-permute-start.14 = (f32[1024,128]{1,0:T(8,128)S(1)}, f32[1024,128]{1,0:T(8,128)S(1)}, u32[]{:S(2)}, u32[]{:S(2)}) collective-permute-start(f32[1024,128]{1,0:T(8,128)S(1)} %bitcast.8), channel_id=1, source_target_pairs={{6,0},{7,1},{0,2},{1,3},{2,4},{3,5},{4,6},{5,7},{14,8},{15,9},{8,1... | collective-permute-start | bytes 1572872 | tf_op jit(solution)/shard_map/ppermute | solution.py:415
  66.9 0.8 copy-start.1
  67.7 25.1 %collective-permute-start.15 = (f32[1024,128]{1,0:T(8,128)S(1)}, f32[1024,128]{1,0:T(8,128)S(1)}, u32[]{:S(2)}, u32[]{:S(2)}) collective-permute-start(f32[1024,128]{1,0:T(8,128)S(1)} %bitcast.13), channel_id=1, source_target_pairs={{6,0},{7,1},{0,2},{1,3},{2,4},{3,5},{4,6},{5,7},{14,8},{15,9},{8,1... | collective-permute-start | bytes 1572872 | tf_op jit(solution)/shard_map/ppermute | solution.py:415
  67.7 25.1 %collective-permute-start.12 = (f32[1024,128]{1,0:T(8,128)S(1)}, f32[1024,128]{1,0:T(8,128)}, u32[]{:S(2)}, u32[]{:S(2)}) collective-permute-start(f32[1024,128]{1,0:T(8,128)S(1)} %collective-permute-done.10.rest_0_.rest_4_), channel_id=1, source_target_pairs={{0,1},{1,0},{2,3},{3,2},{4,5},{5,4},{6,7},{7,6},{8,9},{9,8},{10,11... | collective-permute-start | bytes 1572872 | tf_op jit(solution)/shard_map/ppermute | solution.py:420
  78.3 14.5 %collective-permute-start.13 = (f32[1024,128]{1,0:T(8,128)S(1)}, f32[1024,128]{1,0:T(8,128)}, u32[]{:S(2)}, u32[]{:S(2)}) collective-permute-start(f32[1024,128]{1,0:T(8,128)S(1)} %collective-permute-done.11.rest_1_.rest_5_), channel_id=1, source_target_pairs={{0,1},{1,0},{2,3},{3,2},{4,5},{5,4},{6,7},{7,6},{8,9},{9,8},{10,11... | collective-permute-start | bytes 1572872 | tf_op jit(solution)/shard_map/ppermute | solution.py:420
  79.4 1.0 copy-start.2
  109.8 43.9 %copy-start.3 = (f32[1024,128]{1,0:T(8,128)S(1)}, f32[1024,128]{1,0:T(8,128)}, u32[]{:S(2)}) copy-start(f32[1024,128]{1,0:T(8,128)} %copy-done.1) | copy-start | bytes 1572868
  132.8 20.9 %collective-permute-start.16 = (f32[16,4,8,640]{3,2,1,0:T(8,128)S(1)}, f32[16,4,8,640]{3,2,1,0:T(8,128)S(1)}, u32[]{:S(2)}, u32[]{:S(2)}) collective-permute-start(f32[16,4,8,640]{3,2,1,0:T(8,128)S(1)} %bitcast.17), channel_id=1, source_target_pairs={{0,1},{1,0},{2,3},{3,2},{4,5},{5,4},{6,7},{7,6},{8,9},{9,8},{10,11... | collective-permute-start | bytes 3932168 | tf_op jit(solution)/shard_map/ppermute | solution.py:420
  136.2 13.5 %collective-permute-start.19 = (f32[1024,128]{1,0:T(8,128)S(1)}, f32[1024,128]{1,0:T(8,128)S(1)}, u32[]{:S(2)}, u32[]{:S(2)}) collective-permute-start(f32[1024,128]{1,0:T(8,128)S(1)} %collective-permute-done.10.rest_0_.rest_4_), channel_id=1, source_target_pairs={{2,0},{3,1},{4,2},{5,3},{6,4},{7,5},{0,6},{1,7},{10,8},{11,9},{12,... | collective-permute-start | bytes 1572872 | tf_op jit(solution)/shard_map/ppermute | solution.py:415
  136.6 14.4 %collective-permute-start.20 = (f32[1024,128]{1,0:T(8,128)S(1)}, f32[1024,128]{1,0:T(8,128)S(1)}, u32[]{:S(2)}, u32[]{:S(2)}) collective-permute-start(f32[1024,128]{1,0:T(8,128)S(1)} %collective-permute-done.15.rest_5_.rest_9_), channel_id=1, source_target_pairs={{6,0},{7,1},{0,2},{1,3},{2,4},{3,5},{4,6},{5,7},{14,8},{15,9},{8,1... | collective-permute-start | bytes 1572872 | tf_op jit(solution)/shard_map/ppermute | solution.py:415
  137.7 14.5 %collective-permute-start.17 = (f32[1024,128]{1,0:T(8,128)S(1)}, f32[1024,128]{1,0:T(8,128)S(1)}, u32[]{:S(2)}, u32[]{:S(2)}) collective-permute-start(f32[1024,128]{1,0:T(8,128)S(1)} %collective-permute-done.14.rest_4_.rest_8_), channel_id=1, source_target_pairs={{0,1},{1,0},{2,3},{3,2},{4,5},{5,4},{6,7},{7,6},{8,9},{9,8},{10,11... | collective-permute-start | bytes 1572872 | tf_op jit(solution)/shard_map/ppermute | solution.py:420
  138.2 13.9 %collective-permute-start.18 = (f32[1024,128]{1,0:T(8,128)S(1)}, f32[1024,128]{1,0:T(8,128)S(1)}, u32[]{:S(2)}, u32[]{:S(2)}) collective-permute-start(f32[1024,128]{1,0:T(8,128)S(1)} %collective-permute-done.15.rest_5_.rest_9_), channel_id=1, source_target_pairs={{0,1},{1,0},{2,3},{3,2},{4,5},{5,4},{6,7},{7,6},{8,9},{9,8},{10,11... | collective-permute-start | bytes 1572872 | tf_op jit(solution)/shard_map/ppermute | solution.py:420
  149.7 2.5 %collective-permute-start.21 = (f32[1024,128]{1,0:T(8,128)S(1)}, f32[1024,128]{1,0:T(8,128)S(1)}, u32[]{:S(2)}, u32[]{:S(2)}) collective-permute-start(f32[1024,128]{1,0:T(8,128)S(1)} %collective-permute-done.19.rest_12_), channel_id=1, source_target_pairs={{0,1},{1,0},{2,3},{3,2},{4,5},{5,4},{6,7},{7,6},{8,9},{9,8},{10,11... | collective-permute-start | bytes 1572872 | tf_op jit(solution)/shard_map/ppermute | solution.py:420
  151.0 2.7 %collective-permute-start.22 = (f32[1024,128]{1,0:T(8,128)S(1)}, f32[1024,128]{1,0:T(8,128)S(1)}, u32[]{:S(2)}, u32[]{:S(2)}) collective-permute-start(f32[1024,128]{1,0:T(8,128)S(1)} %collective-permute-done.20.rest_13_), channel_id=1, source_target_pairs={{0,1},{1,0},{2,3},{3,2},{4,5},{5,4},{6,7},{7,6},{8,9},{9,8},{10,11... | collective-permute-start | bytes 1572872 | tf_op jit(solution)/shard_map/ppermute | solution.py:420

commit v6 on v5

--- a/solution.py
+++ b/solution.py
@@ -92,29 +92,15 @@
     return pltpu.roll(x, x.shape[1] // 2, 1)
 
 
-PACK_GROUPS = 4
-
-
-def pack_kernel(v_ref, a_ref, b_ref, buffer, arrived):
-    low = lanes_low(buffer.shape[1:])
+def pack_kernel(v_ref, a_ref, b_ref):
+    low = lanes_low(v_ref.shape[1:])
     half = a_ref.shape[0]
-    group = half // PACK_GROUPS
-    copies = []
-    for g in range(PACK_GROUPS):
-        for side in range(2):
-            blocks = pl.ds(side * half + g * group, group)
-            copy = pltpu.make_async_copy(
-                v_ref.at[blocks], buffer.at[blocks], arrived.at[2 * g + side]
-            )
-            copy.start()
-            copies.append(copy)
-    for g in range(PACK_GROUPS):
-        copies[2 * g].wait()
-        copies[2 * g + 1].wait()
-        for j in range(g * group, (g + 1) * group):
-            one, two = buffer[j], buffer[j + half]
-            a_ref[j] = jnp.where(low, one, turn(two))
-            b_ref[j] = jnp.where(low, turn(one), two)
+
+    @pl.loop(0, half, unroll=2)
+    def _(j):
+        one, two = v_ref[j], v_ref[j + half]
+        a_ref[j] = jnp.where(low, one, turn(two))
+        b_ref[j] = jnp.where(low, turn(one), two)
 
 
 def pack(blocks):
@@ -123,12 +109,8 @@
     return pl.pallas_call(
         pack_kernel,
         out_shape=(shape, shape),
-        in_specs=[pl.BlockSpec(memory_space=pl.ANY)],
+        in_specs=[VMEM_SPEC],
         out_specs=(VMEM_SPEC, VMEM_SPEC),
-        scratch_shapes=[
-            pltpu.VMEM(blocks.shape, F32),
-            pltpu.SemaphoreType.DMA((2 * PACK_GROUPS,)),
-        ],
         compiler_params=pltpu.CompilerParams(vmem_limit_bytes=30 * 2**20),
         cost_estimate=cost(0, 8 * blocks.size),
         name="pack",
@@ -227,15 +209,29 @@
         columns_of(out_ref, block)[...] = fold(terms[0] + terms[1])
 
 
+def fetched(sources, held, arrived):
+    copies = [
+        pltpu.make_async_copy(ref, held.at[n], arrived.at[n]) for n, ref in enumerate(sources)
+    ]
+    for copy in copies:
+        copy.start()
+    return copies, [held.at[n] for n in range(len(sources))]
+
+
 def far_kernel(y_ref, near_ref, lhs_ref, *rest):
-    up, up_s, down = (rest[2 * n : 2 * n + 2] for n in range(3))
-    out_ref, rhs = rest[6:]
+    out_ref, rhs, held, arrived = rest[6:]
+    copies, refs = fetched(rest[:6], held, arrived)
+    up, up_s, down = (refs[2 * n : 2 * n + 2] for n in range(3))
     out_ref[:, : NEAR_BLOCKS * 128] = near_ref[...]
     for which, refs in enumerate((up, up_s)):
+        for copy in copies[2 * which : 2 * which + 2]:
+            copy.wait()
         for part in range(2):
             rhs[2 * which + part] = paired(refs, part)
         terms = [mm(lhs_ref[part], rhs[2 * which + part]) for part in range(2)]
         columns_of(out_ref, NEAR_BLOCKS + which)[...] = fold(terms[0] + terms[1])
+    for copy in copies[4:]:
+        copy.wait()
     side = jnp.where(y_ref[0] < 2, 0, 2)
     terms = [mm(turned(down, part), rhs[side + part]) for part in range(2)]
     columns_of(out_ref, 4)[...] = fold(terms[0] + terms[1])
@@ -268,9 +264,14 @@
     return pl.pallas_call(
         far_kernel,
         out_shape=jax.ShapeDtypeStruct((cols, GRAM_BLOCKS * cols), F32),
-        in_specs=[SMEM_SPEC] + [VMEM_SPEC] * (2 + len(operands)),
+        in_specs=[SMEM_SPEC, VMEM_SPEC, VMEM_SPEC]
+        + [pl.BlockSpec(memory_space=pl.ANY)] * len(operands),
         out_specs=VMEM_SPEC,
-        scratch_shapes=[pltpu.VMEM((4, rows, 2 * cols), BF)],
+        scratch_shapes=[
+            pltpu.VMEM((4, rows, 2 * cols), BF),
+            pltpu.VMEM((len(operands), rows, cols), F32),
+            pltpu.SemaphoreType.DMA((len(operands),)),
+        ],
         compiler_params=pltpu.CompilerParams(vmem_limit_bytes=30 * 2**20),
         cost_estimate=cost(48 * rows * cols * cols, 24 * rows * cols),
         name="gram_far",
@@ -283,8 +284,10 @@
 
 
 def finish_kernel(total_rows, y_ref, ga_ref, gb_ref, *rest):
-    x_refs = [rest[2 * n : 2 * n + 2] for n in range(len(PIECES))]
-    out_ref, gram, gram_low, state, factor, ordered = rest[2 * len(PIECES) :]
+    sources = rest[: 2 * len(PIECES)]
+    out_ref, gram, gram_low, state, factor, ordered, held, arrived = rest[2 * len(PIECES) :]
+    copies, held_refs = fetched(sources, held, arrived)
+    x_refs = [held_refs[2 * n : 2 * n + 2] for n in range(len(PIECES))]
     grams = (ga_ref, gb_ref)
     y = y_ref[0]
 
@@ -359,11 +362,13 @@
         axis=0,
     )
     ordered[...] = rhs
-    chunk = 256
+    for copy in copies:
+        copy.wait()
+    chunk = 512
     half = out_ref.shape[0] // 2
     for part in range(2):
 
-        @pl.loop(0, half // chunk, unroll=2)
+        @pl.loop(0, half // chunk)
         def _(step):
             within = pl.ds(pl.multiple_of(step * chunk, chunk), chunk)
             rows = pl.ds(pl.multiple_of(part * half + step * chunk, chunk), chunk)
@@ -380,7 +385,8 @@
     return pl.pallas_call(
         functools.partial(finish_kernel, total_rows),
         out_shape=jax.ShapeDtypeStruct((rows, cols), F32),
-        in_specs=[SMEM_SPEC] + [VMEM_SPEC] * (2 + len(operands)),
+        in_specs=[SMEM_SPEC, VMEM_SPEC, VMEM_SPEC]
+        + [pl.BlockSpec(memory_space=pl.ANY)] * len(operands),
         out_specs=VMEM_SPEC,
         scratch_shapes=[
             pltpu.VMEM((NV, NV), BF),
@@ -388,6 +394,8 @@
             pltpu.VMEM((3, cols, NV), F32),
             pltpu.VMEM((NV, 2 * cols), BF),
             pltpu.VMEM((NV, 2 * cols), BF),
+            pltpu.VMEM((len(operands), rows // 2, cols), F32),
+            pltpu.SemaphoreType.DMA((len(operands),)),
         ],
         compiler_params=pltpu.CompilerParams(vmem_limit_bytes=40 * 2**20),
         cost_estimate=cost(12 * 6 * cols * NV * NV, 4 * rows * cols * 9),

time: 175 us -> 173 us (0.989)
  Pallas kernels: 56.6 us -> 54.5 us
where the time goes in v6:
time: 173 us; the launch traced here: 172 us
  Pallas kernels  54.5 us (32%)
  starting transfers between devices  42.2 us (24%)
  blocking collectives  37.2 us (22%)
  waiting for transfers between devices  32.7 us (19%)
  local copies, waits for them, and re-layouts  3.23 us (2%)
    ppermute x6, waiting for transfers between devices, from_y(): lax.ppermute(value, 'vec', [((i + 2 * step) % vec_count, i) for i in rang...  31.2 us
    all_to_all x1, blocking collectives, on_device(): lax.all_to_all(jnp.broadcast_to(part[None], (members,) + part.shape), ('r...  22.9 us
    pallas_call x4, Pallas kernels, apply_field(): pl.pallas_call(functools.partial(field_kernel, second), out_shape=jax.Sha...  22.7 us
    ppermute x8, starting transfers between devices, from_row(): lax.ppermute(value, 'row', [((i + step) % row_count, i) for i in range(ro...  21.4 us
    pallas_call x1, Pallas kernels, finish(): pl.pallas_call(functools.partial(finish_kernel, total_rows), out_shape=ja...  19.7 us
    all_to_all x1, blocking collectives, on_device(): lax.all_to_all(share.reshape(row_count, strip, -1), 'row', split_axis=0,...  14.3 us
    ppermute x9, starting transfers between devices, swap(): return lax.ppermute(value, 'vec', [(i, i ^ 1) for i in range(vec_count)])  14 us
    ppermute x6, starting transfers between devices, from_y(): lax.ppermute(value, 'vec', [((i + 2 * step) % vec_count, i) for i in rang...  6.84 us
  transfers between devices with their start and end apart: 23, of which 5 were waited for; matrix products, arithmetic and copies ran while one was open for 1% of the time, Pallas kernels for 18%

profile of v6, /device:TPU:1, one launch (start us, length us, event | category | flops | bytes accessed | tf_op | source)
XLA Modules:
  0.0 172.4 jit_solution(1783231533434841788)
XLA Ops:
  0.0 1.2 copy-done
  1.2 0.5 pack.1
  1.8 2.1 %collective-permute-start = (f32[8,128,128]{2,1,0:T(8,128)S(1)}, f32[8,128,128]{2,1,0:T(8,128)S(1)}, u32[]{:S(2)}, u32[]{:S(2)}) collective-permute-start(f32[8,128,128]{2,1,0:T(8,128)S(1)} %get-tuple-element.9.own_ref.rest_0_), channel_id=1, source_target_pairs={{120,0},{0,8},{8,16},{16,24},{24,32},{32,40},{40,48},{48,56},{56,6... | collective-permute-start | bytes 1572872 | tf_op jit(solution)/shard_map/ppermute | solution.py:420
  3.9 4.8 %collective-permute-start.1 = (f32[8,128,128]{2,1,0:T(8,128)S(1)}, f32[8,128,128]{2,1,0:T(8,128)S(1)}, u32[]{:S(2)}, u32[]{:S(2)}) collective-permute-start(f32[8,128,128]{2,1,0:T(8,128)S(1)} %get-tuple-element.9.own_ref.rest_0_), channel_id=1, source_target_pairs={{8,0},{16,8},{24,16},{32,24},{40,32},{48,40},{56,48},{64,56},{72,6... | collective-permute-start | bytes 1572872 | tf_op jit(solution)/shard_map/ppermute | solution.py:420
  8.7 0.0 collective-permute-start.4
  8.7 4.8 %collective-permute-start.5 = (f32[8,128,128]{2,1,0:T(8,128)S(1)}, f32[8,128,128]{2,1,0:T(8,128)S(1)}, u32[]{:S(2)}, u32[]{:S(2)}) collective-permute-start(f32[8,128,128]{2,1,0:T(8,128)S(1)} %get-tuple-element.10.own_ref.rest_0_), channel_id=1, source_target_pairs={{8,0},{16,8},{24,16},{32,24},{40,32},{48,40},{56,48},{64,56},{72,6... | collective-permute-start | bytes 1572872 | tf_op jit(solution)/shard_map/ppermute | solution.py:420
  13.5 0.8 fusion.2
  15.5 0.1 reshape.30.cols_ref
  15.6 6.3 %split_blocks.1.h_ref = bf16[16,12,256,128]{3,2,1,0:T(8,128)(2,1)S(1)} custom-call(f32[16,12,128,128]{3,2,1,0:T(8,128)} %h_ref.1), custom_call_target="tpu_custom_call" | custom-call | bytes 25165824 | tf_op jit(solution)/shard_map/split_blocks/pallas_call | solution.py:65
  22.0 0.1 pad_maximum_fusion.coef_ref
  22.0 0.0 collective-permute-done.left_ref
  22.1 0.0 collective-permute-done.1.right_ref
  22.1 5.7 %field.4.own_ref = f32[8,128,128]{2,1,0:T(8,128)S(1)} custom-call(s32[192]{0:T(256)S(1)} %reshape.30.cols_ref, f32[2]{0:T(128)S(1)} %pad_maximum_fusion.coef_ref, bf16[16,12,256,128]{3,2,1,0:T(8,128)(2,1)S(1)} %split_blocks.1.h_ref, f32[8,128,128]{2,1,0:T(8,128)S(1)} %collective-permute-done.left_ref, f32[8,128,128]{2,1,0:T(8,128)S(1)} %get-tuple-element.9.own_ref.rest_0_, ...), custom_call_target="tpu_custom_call" | custom-call | flops 3221225472 | bytes 12582912 | tf_op jit(solution)/shard_map/field/pallas_call | solution.py:165
  27.7 0.1 collective-permute-start.2
  27.8 4.8 %collective-permute-start.3 = (f32[8,128,128]{2,1,0:T(8,128)S(1)}, f32[8,128,128]{2,1,0:T(8,128)S(1)}, u32[]{:S(2)}, u32[]{:S(2)}) collective-permute-start(f32[8,128,128]{2,1,0:T(8,128)S(1)} %field.4.own_ref), channel_id=1, source_target_pairs={{8,0},{16,8},{24,16},{32,24},{40,32},{48,40},{56,48},{64,56},{72,6... | collective-permute-start | bytes 1572872 | tf_op jit(solution)/shard_map/ppermute | solution.py:420
  32.6 0.0 collective-permute-done.4.left_ref
  32.6 5.7 %field.6.own_ref = f32[8,128,128]{2,1,0:T(8,128)S(1)} custom-call(s32[192]{0:T(256)S(1)} %reshape.30.cols_ref, f32[2]{0:T(128)S(1)} %pad_maximum_fusion.coef_ref, bf16[16,12,256,128]{3,2,1,0:T(8,128)(2,1)S(1)} %split_blocks.1.h_ref, f32[8,128,128]{2,1,0:T(8,128)S(1)} %collective-permute-done.4.left_ref, ...), custom_call_target="tpu_custom_call" | custom-call | flops 3221225472 | bytes 12582912 | tf_op jit(solution)/shard_map/field/pallas_call | solution.py:165
  38.2 0.1 collective-permute-start.6
  38.3 4.8 %collective-permute-start.7 = (f32[8,128,128]{2,1,0:T(8,128)S(1)}, f32[8,128,128]{2,1,0:T(8,128)S(1)}, u32[]{:S(2)}, u32[]{:S(2)}) collective-permute-start(f32[8,128,128]{2,1,0:T(8,128)S(1)} %field.6.own_ref), channel_id=1, source_target_pairs={{8,0},{16,8},{24,16},{32,24},{40,32},{48,40},{56,48},{64,56},{72,6... | collective-permute-start | bytes 1572872 | tf_op jit(solution)/shard_map/ppermute | solution.py:420
  43.1 5.7 %field.5 = f32[8,128,128]{2,1,0:T(8,128)S(1)} custom-call(s32[192]{0:T(256)S(1)} %reshape.30.cols_ref, f32[2]{0:T(128)S(1)} %pad_maximum_fusion.coef_ref, bf16[16,12,256,128]{3,2,1,0:T(8,128)(2,1)S(1)} %split_blocks.1.h_ref, f32[8,128,128]{2,1,0:T(8,128)S(1)} %collective-permute-done.2.left_ref, f32[8,128,128]{2,1,0:T(8,128)S(1)} %field.4.own_ref, ...), custom_call_target="tpu_custom_call" | custom-call | flops 3221225472 | bytes 12582912 | tf_op jit(solution)/shard_map/field/pallas_call | solution.py:165
  48.8 3.1 %collective-permute-start.8 = (f32[1024,128]{1,0:T(8,128)S(1)}, f32[1024,128]{1,0:T(8,128)S(1)}, u32[]{:S(2)}, u32[]{:S(2)}) collective-permute-start(f32[1024,128]{1,0:T(8,128)S(1)} %bitcast.6), channel_id=1, source_target_pairs={{0,1},{1,0},{2,3},{3,2},{4,5},{5,4},{6,7},{7,6},{8,9},{9,8},{10,11... | collective-permute-start | bytes 1572872 | tf_op jit(solution)/shard_map/ppermute | solution.py:428
  51.9 2.7 %collective-permute-start.10 = (f32[1024,128]{1,0:T(8,128)S(1)}, f32[1024,128]{1,0:T(8,128)S(1)}, u32[]{:S(2)}, u32[]{:S(2)}) collective-permute-start(f32[1024,128]{1,0:T(8,128)S(1)} %bitcast.7), channel_id=1, source_target_pairs={{2,0},{3,1},{4,2},{5,3},{6,4},{7,5},{0,6},{1,7},{10,8},{11,9},{12,... | collective-permute-start | bytes 1572872 | tf_op jit(solution)/shard_map/ppermute | solution.py:423
  54.7 5.7 %field.7 = f32[8,128,128]{2,1,0:T(8,128)S(1)} custom-call(s32[192]{0:T(256)S(1)} %reshape.30.cols_ref, f32[2]{0:T(128)S(1)} %pad_maximum_fusion.coef_ref, bf16[16,12,256,128]{3,2,1,0:T(8,128)(2,1)S(1)} %split_blocks.1.h_ref, f32[8,128,128]{2,1,0:T(8,128)S(1)} %collective-permute-done.6.left_ref, f32[8,128,128]{2,1,0:T(8,128)S(1)} %field.6.own_ref, ...), custom_call_target="tpu_custom_call" | custom-call | flops 3221225472 | bytes 12582912 | tf_op jit(solution)/shard_map/field/pallas_call | solution.py:165
  60.3 2.6 %collective-permute-start.11 = (f32[1024,128]{1,0:T(8,128)S(1)}, f32[1024,128]{1,0:T(8,128)S(1)}, u32[]{:S(2)}, u32[]{:S(2)}) collective-permute-start(f32[1024,128]{1,0:T(8,128)S(1)} %bitcast.11), channel_id=1, source_target_pairs={{2,0},{3,1},{4,2},{5,3},{6,4},{7,5},{0,6},{1,7},{10,8},{11,9},{12,... | collective-permute-start | bytes 1572872 | tf_op jit(solution)/shard_map/ppermute | solution.py:423
  62.9 2.5 %collective-permute-start.9 = (f32[1024,128]{1,0:T(8,128)S(1)}, f32[1024,128]{1,0:T(8,128)}, u32[]{:S(2)}, u32[]{:S(2)}) collective-permute-start(f32[1024,128]{1,0:T(8,128)S(1)} %bitcast.12), channel_id=1, source_target_pairs={{0,1},{1,0},{2,3},{3,2},{4,5},{5,4},{6,7},{7,6},{8,9},{9,8},{10,11... | collective-permute-start | bytes 1572872 | tf_op jit(solution)/shard_map/ppermute | solution.py:428
  65.5 0.8 copy-done.1
  66.2 0.0 collective-permute-start.15
  66.3 1.2 collective-permute-start.12
  67.5 9.4 %collective-permute-done.11.rest_1_.rest_5_ = f32[1024,128]{1,0:T(8,128)S(1)} collective-permute-done((f32[1024,128]{1,0:T(8,128)S(1)}, f32[1024,128]{1,0:T(8,128)S(1)}, u32[]{:S(2)}, u32[]{:S(2)}) %collective-permute-start.11) | collective-permute-done | bytes 524320 | tf_op jit(solution)/shard_map/ppermute | solution.py:423
  76.9 1.1 collective-permute-start.13
  78.0 1.0 copy-done.2
  79.1 2.4 %gram_near.1 = (f32[128,256]{1,0:T(8,128)S(1)}, bf16[2,256,1024]{2,1,0:T(8,128)(2,1)S(1)}) custom-call(f32[1024,128]{1,0:T(8,128)S(1)} %bitcast.9, f32[1024,128]{1,0:T(8,128)S(1)} %bitcast.14, f32[1024,128]{1,0:T(8,128)S(1)} %copy-done.2, f32[1024,128]{1,0:T(8,128)} %collective-permute-done.9.rest_3_), custom_call_target="tpu_custom_call" | custom-call | flops 536870912 | bytes 2097152 | tf_op jit(solution)/shard_map/gram_near/pallas_call | solution.py:247
  81.5 9.9 %collective-permute-done.15.rest_5_.rest_9_ = f32[1024,128]{1,0:T(8,128)S(1)} collective-permute-done((f32[1024,128]{1,0:T(8,128)S(1)}, f32[1024,128]{1,0:T(8,128)S(1)}, u32[]{:S(2)}, u32[]{:S(2)}) %collective-permute-start.15) | collective-permute-done | bytes 524320 | tf_op jit(solution)/shard_map/ppermute | solution.py:423
  91.4 2.9 %gram_far.1 = f32[128,640]{1,0:T(8,128)S(1)} custom-call(s32[1]{0:T(128)} %bitcast.y_ref, f32[128,256]{1,0:T(8,128)S(1)} %get-tuple-element.11.near_ref, bf16[2,256,1024]{2,1,0:T(8,128)(2,1)S(1)} %get-tuple-element.12.lhs_ref, f32[1024,128]{1,0:T(8,128)S(1)} %collective-permute-done.10.rest_0_.rest_4_, ...), custom_call_target="tpu_custom_call" | custom-call | flops 805306368 | bytes 3145728 | tf_op jit(solution)/shard_map/gram_far/pallas_call | solution.py:264
  94.2 14.3 %all_to_all.10 = f32[16,8,640]{2,1,0:T(8,128)S(1)} all-to-all(f32[16,8,640]{2,1,0:T(8,128)S(1)} %bitcast.16), channel_id=1, replica_groups=mesh['row'=16,'vec'=8] {'row'}, dimensions={0} | all-to-all | bytes 655360 | tf_op jit(solution)/shard_map/all_to_all | solution.py:453
  108.6 0.1 broadcast_in_dim.17
  108.7 0.0 copy-start.3
  108.7 22.9 %all_to_all.11 = f32[64,8,640]{2,1,0:T(8,128)S(1)} all-to-all(f32[64,8,640]{2,1,0:T(8,128)S(1)} %broadcast_in_dim.17), channel_id=1, replica_groups={{0,2,4,6,8,10,12,14,16,18,20,22,24,26,28,30,32,34,36,38,40,42,44,46,48,..., dimensions={0} | all-to-all | bytes 2621440 | tf_op jit(solution)/shard_map/all_to_all | solution.py:462
  131.6 3.4 %collective-permute-start.16 = (f32[16,4,8,640]{3,2,1,0:T(8,128)S(1)}, f32[16,4,8,640]{3,2,1,0:T(8,128)S(1)}, u32[]{:S(2)}, u32[]{:S(2)}) collective-permute-start(f32[16,4,8,640]{3,2,1,0:T(8,128)S(1)} %bitcast.17), channel_id=1, source_target_pairs={{0,1},{1,0},{2,3},{3,2},{4,5},{5,4},{6,7},{7,6},{8,9},{9,8},{10,11... | collective-permute-start | bytes 3932168 | tf_op jit(solution)/shard_map/ppermute | solution.py:428
  135.0 0.4 collective-permute-start.19
  135.4 1.1 collective-permute-start.20
  136.5 0.6 collective-permute-start.17
  137.1 11.4 %collective-permute-done.19.rest_12_ = f32[1024,128]{1,0:T(8,128)S(1)} collective-permute-done((f32[1024,128]{1,0:T(8,128)S(1)}, f32[1024,128]{1,0:T(8,128)S(1)}, u32[]{:S(2)}, u32[]{:S(2)}) %collective-permute-start.19) | collective-permute-done | bytes 524320 | tf_op jit(solution)/shard_map/ppermute | solution.py:423
  148.5 0.9 collective-permute-start.21
  149.4 0.5 collective-permute-done.20.rest_13_
  149.9 1.1 collective-permute-start.22
  151.0 1.5 collective-permute-done.22.rest_15_
  152.5 19.7 %finish.1 = f32[2048,128]{1,0:T(8,128)} custom-call(s32[1]{0:T(128)} %bitcast.y_ref, f32[16,4,8,640]{3,2,1,0:T(8,128)S(1)} %bitcast.18, f32[16,4,8,640]{3,2,1,0:T(8,128)S(1)} %collective-permute-done.16.gb_ref, f32[1024,128]{1,0:T(8,128)S(1)} %bitcast.10, f32[1024,128]{1,0:T(8,128)S(1)} %bitcast.15, f32[1024,128]{1,0:T(8,128)S(1)} %copy-done.3, ...), custom_call_target="tpu_custom_call" | custom-call | flops 9663676416 | bytes 9437184 | tf_op jit(solution)/shard_map/finish/pallas_call | solution.py:385
  (22 shorter events, 0.1 us)
Async XLA Ops:
  0.0 1.2 copy-start
  1.8 20.3 %collective-permute-start = (f32[8,128,128]{2,1,0:T(8,128)S(1)}, f32[8,128,128]{2,1,0:T(8,128)S(1)}, u32[]{:S(2)}, u32[]{:S(2)}) collective-permute-start(f32[8,128,128]{2,1,0:T(8,128)S(1)} %get-tuple-element.9.own_ref.rest_0_), channel_id=1, source_target_pairs={{120,0},{0,8},{8,16},{16,24},{24,32},{32,40},{40,48},{48,56},{56,6... | collective-permute-start | bytes 1572872 | tf_op jit(solution)/shard_map/ppermute | solution.py:420
  3.9 18.2 %collective-permute-start.1 = (f32[8,128,128]{2,1,0:T(8,128)S(1)}, f32[8,128,128]{2,1,0:T(8,128)S(1)}, u32[]{:S(2)}, u32[]{:S(2)}) collective-permute-start(f32[8,128,128]{2,1,0:T(8,128)S(1)} %get-tuple-element.9.own_ref.rest_0_), channel_id=1, source_target_pairs={{8,0},{16,8},{24,16},{32,24},{40,32},{48,40},{56,48},{64,56},{72,6... | collective-permute-start | bytes 1572872 | tf_op jit(solution)/shard_map/ppermute | solution.py:420
  8.7 23.9 %collective-permute-start.4 = (f32[8,128,128]{2,1,0:T(8,128)S(1)}, f32[8,128,128]{2,1,0:T(8,128)S(1)}, u32[]{:S(2)}, u32[]{:S(2)}) collective-permute-start(f32[8,128,128]{2,1,0:T(8,128)S(1)} %get-tuple-element.10.own_ref.rest_0_), channel_id=1, source_target_pairs={{120,0},{0,8},{8,16},{16,24},{24,32},{32,40},{40,48},{48,56},{56,6... | collective-permute-start | bytes 1572872 | tf_op jit(solution)/shard_map/ppermute | solution.py:420
  8.7 23.9 %collective-permute-start.5 = (f32[8,128,128]{2,1,0:T(8,128)S(1)}, f32[8,128,128]{2,1,0:T(8,128)S(1)}, u32[]{:S(2)}, u32[]{:S(2)}) collective-permute-start(f32[8,128,128]{2,1,0:T(8,128)S(1)} %get-tuple-element.10.own_ref.rest_0_), channel_id=1, source_target_pairs={{8,0},{16,8},{24,16},{32,24},{40,32},{48,40},{56,48},{64,56},{72,6... | collective-permute-start | bytes 1572872 | tf_op jit(solution)/shard_map/ppermute | solution.py:420
  27.7 15.4 %collective-permute-start.2 = (f32[8,128,128]{2,1,0:T(8,128)S(1)}, f32[8,128,128]{2,1,0:T(8,128)S(1)}, u32[]{:S(2)}, u32[]{:S(2)}) collective-permute-start(f32[8,128,128]{2,1,0:T(8,128)S(1)} %field.4.own_ref), channel_id=1, source_target_pairs={{120,0},{0,8},{8,16},{16,24},{24,32},{32,40},{40,48},{48,56},{56,6... | collective-permute-start | bytes 1572872 | tf_op jit(solution)/shard_map/ppermute | solution.py:420
  27.8 15.3 %collective-permute-start.3 = (f32[8,128,128]{2,1,0:T(8,128)S(1)}, f32[8,128,128]{2,1,0:T(8,128)S(1)}, u32[]{:S(2)}, u32[]{:S(2)}) collective-permute-start(f32[8,128,128]{2,1,0:T(8,128)S(1)} %field.4.own_ref), channel_id=1, source_target_pairs={{8,0},{16,8},{24,16},{32,24},{40,32},{48,40},{56,48},{64,56},{72,6... | collective-permute-start | bytes 1572872 | tf_op jit(solution)/shard_map/ppermute | solution.py:420
  38.2 16.4 %collective-permute-start.6 = (f32[8,128,128]{2,1,0:T(8,128)S(1)}, f32[8,128,128]{2,1,0:T(8,128)S(1)}, u32[]{:S(2)}, u32[]{:S(2)}) collective-permute-start(f32[8,128,128]{2,1,0:T(8,128)S(1)} %field.6.own_ref), channel_id=1, source_target_pairs={{120,0},{0,8},{8,16},{16,24},{24,32},{32,40},{40,48},{48,56},{56,6... | collective-permute-start | bytes 1572872 | tf_op jit(solution)/shard_map/ppermute | solution.py:420
  38.3 16.3 %collective-permute-start.7 = (f32[8,128,128]{2,1,0:T(8,128)S(1)}, f32[8,128,128]{2,1,0:T(8,128)S(1)}, u32[]{:S(2)}, u32[]{:S(2)}) collective-permute-start(f32[8,128,128]{2,1,0:T(8,128)S(1)} %field.6.own_ref), channel_id=1, source_target_pairs={{8,0},{16,8},{24,16},{32,24},{40,32},{48,40},{56,48},{64,56},{72,6... | collective-permute-start | bytes 1572872 | tf_op jit(solution)/shard_map/ppermute | solution.py:420
  48.8 16.7 %collective-permute-start.8 = (f32[1024,128]{1,0:T(8,128)S(1)}, f32[1024,128]{1,0:T(8,128)S(1)}, u32[]{:S(2)}, u32[]{:S(2)}) collective-permute-start(f32[1024,128]{1,0:T(8,128)S(1)} %bitcast.6), channel_id=1, source_target_pairs={{0,1},{1,0},{2,3},{3,2},{4,5},{5,4},{6,7},{7,6},{8,9},{9,8},{10,11... | collective-permute-start | bytes 1572872 | tf_op jit(solution)/shard_map/ppermute | solution.py:428
  51.9 14.4 %collective-permute-start.10 = (f32[1024,128]{1,0:T(8,128)S(1)}, f32[1024,128]{1,0:T(8,128)S(1)}, u32[]{:S(2)}, u32[]{:S(2)}) collective-permute-start(f32[1024,128]{1,0:T(8,128)S(1)} %bitcast.7), channel_id=1, source_target_pairs={{2,0},{3,1},{4,2},{5,3},{6,4},{7,5},{0,6},{1,7},{10,8},{11,9},{12,... | collective-permute-start | bytes 1572872 | tf_op jit(solution)/shard_map/ppermute | solution.py:423
  60.3 16.6 %collective-permute-start.11 = (f32[1024,128]{1,0:T(8,128)S(1)}, f32[1024,128]{1,0:T(8,128)S(1)}, u32[]{:S(2)}, u32[]{:S(2)}) collective-permute-start(f32[1024,128]{1,0:T(8,128)S(1)} %bitcast.11), channel_id=1, source_target_pairs={{2,0},{3,1},{4,2},{5,3},{6,4},{7,5},{0,6},{1,7},{10,8},{11,9},{12,... | collective-permute-start | bytes 1572872 | tf_op jit(solution)/shard_map/ppermute | solution.py:423
  62.9 15.1 %collective-permute-start.9 = (f32[1024,128]{1,0:T(8,128)S(1)}, f32[1024,128]{1,0:T(8,128)}, u32[]{:S(2)}, u32[]{:S(2)}) collective-permute-start(f32[1024,128]{1,0:T(8,128)S(1)} %bitcast.12), channel_id=1, source_target_pairs={{0,1},{1,0},{2,3},{3,2},{4,5},{5,4},{6,7},{7,6},{8,9},{9,8},{10,11... | collective-permute-start | bytes 1572872 | tf_op jit(solution)/shard_map/ppermute | solution.py:428
  65.4 16.1 %collective-permute-start.14 = (f32[1024,128]{1,0:T(8,128)S(1)}, f32[1024,128]{1,0:T(8,128)S(1)}, u32[]{:S(2)}, u32[]{:S(2)}) collective-permute-start(f32[1024,128]{1,0:T(8,128)S(1)} %bitcast.8), channel_id=1, source_target_pairs={{6,0},{7,1},{0,2},{1,3},{2,4},{3,5},{4,6},{5,7},{14,8},{15,9},{8,1... | collective-permute-start | bytes 1572872 | tf_op jit(solution)/shard_map/ppermute | solution.py:423
  65.5 0.8 copy-start.1
  66.2 25.1 %collective-permute-start.15 = (f32[1024,128]{1,0:T(8,128)S(1)}, f32[1024,128]{1,0:T(8,128)S(1)}, u32[]{:S(2)}, u32[]{:S(2)}) collective-permute-start(f32[1024,128]{1,0:T(8,128)S(1)} %bitcast.13), channel_id=1, source_target_pairs={{6,0},{7,1},{0,2},{1,3},{2,4},{3,5},{4,6},{5,7},{14,8},{15,9},{8,1... | collective-permute-start | bytes 1572872 | tf_op jit(solution)/shard_map/ppermute | solution.py:423
  66.3 25.1 %collective-permute-start.12 = (f32[1024,128]{1,0:T(8,128)S(1)}, f32[1024,128]{1,0:T(8,128)}, u32[]{:S(2)}, u32[]{:S(2)}) collective-permute-start(f32[1024,128]{1,0:T(8,128)S(1)} %collective-permute-done.10.rest_0_.rest_4_), channel_id=1, source_target_pairs={{0,1},{1,0},{2,3},{3,2},{4,5},{5,4},{6,7},{7,6},{8,9},{9,8},{10,11... | collective-permute-start | bytes 1572872 | tf_op jit(solution)/shard_map/ppermute | solution.py:428
  76.9 14.5 %collective-permute-start.13 = (f32[1024,128]{1,0:T(8,128)S(1)}, f32[1024,128]{1,0:T(8,128)}, u32[]{:S(2)}, u32[]{:S(2)}) collective-permute-start(f32[1024,128]{1,0:T(8,128)S(1)} %collective-permute-done.11.rest_1_.rest_5_), channel_id=1, source_target_pairs={{0,1},{1,0},{2,3},{3,2},{4,5},{5,4},{6,7},{7,6},{8,9},{9,8},{10,11... | collective-permute-start | bytes 1572872 | tf_op jit(solution)/shard_map/ppermute | solution.py:428
  78.0 1.0 copy-start.2
  108.7 43.9 %copy-start.3 = (f32[1024,128]{1,0:T(8,128)S(1)}, f32[1024,128]{1,0:T(8,128)}, u32[]{:S(2)}) copy-start(f32[1024,128]{1,0:T(8,128)} %copy-done.1) | copy-start | bytes 1572868
  131.6 20.9 %collective-permute-start.16 = (f32[16,4,8,640]{3,2,1,0:T(8,128)S(1)}, f32[16,4,8,640]{3,2,1,0:T(8,128)S(1)}, u32[]{:S(2)}, u32[]{:S(2)}) collective-permute-start(f32[16,4,8,640]{3,2,1,0:T(8,128)S(1)} %bitcast.17), channel_id=1, source_target_pairs={{0,1},{1,0},{2,3},{3,2},{4,5},{5,4},{6,7},{7,6},{8,9},{9,8},{10,11... | collective-permute-start | bytes 3932168 | tf_op jit(solution)/shard_map/ppermute | solution.py:428
  135.0 13.5 %collective-permute-start.19 = (f32[1024,128]{1,0:T(8,128)S(1)}, f32[1024,128]{1,0:T(8,128)S(1)}, u32[]{:S(2)}, u32[]{:S(2)}) collective-permute-start(f32[1024,128]{1,0:T(8,128)S(1)} %collective-permute-done.10.rest_0_.rest_4_), channel_id=1, source_target_pairs={{2,0},{3,1},{4,2},{5,3},{6,4},{7,5},{0,6},{1,7},{10,8},{11,9},{12,... | collective-permute-start | bytes 1572872 | tf_op jit(solution)/shard_map/ppermute | solution.py:423
  135.4 14.4 %collective-permute-start.20 = (f32[1024,128]{1,0:T(8,128)S(1)}, f32[1024,128]{1,0:T(8,128)S(1)}, u32[]{:S(2)}, u32[]{:S(2)}) collective-permute-start(f32[1024,128]{1,0:T(8,128)S(1)} %collective-permute-done.15.rest_5_.rest_9_), channel_id=1, source_target_pairs={{6,0},{7,1},{0,2},{1,3},{2,4},{3,5},{4,6},{5,7},{14,8},{15,9},{8,1... | collective-permute-start | bytes 1572872 | tf_op jit(solution)/shard_map/ppermute | solution.py:423
  136.5 14.5 %collective-permute-start.17 = (f32[1024,128]{1,0:T(8,128)S(1)}, f32[1024,128]{1,0:T(8,128)S(1)}, u32[]{:S(2)}, u32[]{:S(2)}) collective-permute-start(f32[1024,128]{1,0:T(8,128)S(1)} %collective-permute-done.14.rest_4_.rest_8_), channel_id=1, source_target_pairs={{0,1},{1,0},{2,3},{3,2},{4,5},{5,4},{6,7},{7,6},{8,9},{9,8},{10,11... | collective-permute-start | bytes 1572872 | tf_op jit(solution)/shard_map/ppermute | solution.py:428
  137.1 13.9 %collective-permute-start.18 = (f32[1024,128]{1,0:T(8,128)S(1)}, f32[1024,128]{1,0:T(8,128)S(1)}, u32[]{:S(2)}, u32[]{:S(2)}) collective-permute-start(f32[1024,128]{1,0:T(8,128)S(1)} %collective-permute-done.15.rest_5_.rest_9_), channel_id=1, source_target_pairs={{0,1},{1,0},{2,3},{3,2},{4,5},{5,4},{6,7},{7,6},{8,9},{9,8},{10,11... | collective-permute-start | bytes 1572872 | tf_op jit(solution)/shard_map/ppermute | solution.py:428
  148.5 2.5 %collective-permute-start.21 = (f32[1024,128]{1,0:T(8,128)S(1)}, f32[1024,128]{1,0:T(8,128)S(1)}, u32[]{:S(2)}, u32[]{:S(2)}) collective-permute-start(f32[1024,128]{1,0:T(8,128)S(1)} %collective-permute-done.19.rest_12_), channel_id=1, source_target_pairs={{0,1},{1,0},{2,3},{3,2},{4,5},{5,4},{6,7},{7,6},{8,9},{9,8},{10,11... | collective-permute-start | bytes 1572872 | tf_op jit(solution)/shard_map/ppermute | solution.py:428
  149.9 2.7 %collective-permute-start.22 = (f32[1024,128]{1,0:T(8,128)S(1)}, f32[1024,128]{1,0:T(8,128)S(1)}, u32[]{:S(2)}, u32[]{:S(2)}) collective-permute-start(f32[1024,128]{1,0:T(8,128)S(1)} %collective-permute-done.20.rest_13_), channel_id=1, source_target_pairs={{0,1},{1,0},{2,3},{3,2},{4,5},{5,4},{6,7},{7,6},{8,9},{9,8},{10,11... | collective-permute-start | bytes 1572872 | tf_op jit(solution)/shard_map/ppermute | solution.py:428

commit v7 on v6

--- a/solution.py
+++ b/solution.py
@@ -204,6 +204,7 @@
     out_ref, lhs = rest[4:]
     for part in range(2):
         lhs[part] = turned(own, part)
+        lhs[2 + part] = turned(beside, part)
     for block, refs in enumerate((own, beside)):
         terms = [mm(lhs[part], paired(refs, part)) for part in range(2)]
         columns_of(out_ref, block)[...] = fold(terms[0] + terms[1])
@@ -218,22 +219,21 @@
     return copies, [held.at[n] for n in range(len(sources))]
 
 
-def far_kernel(y_ref, near_ref, lhs_ref, *rest):
-    out_ref, rhs, held, arrived = rest[6:]
-    copies, refs = fetched(rest[:6], held, arrived)
-    up, up_s, down = (refs[2 * n : 2 * n + 2] for n in range(3))
+def far_kernel(near_ref, lhs_ref, *rest):
+    out_ref, rhs, held, arrived = rest[4:]
+    copies, refs = fetched(rest[:4], held, arrived)
+    up, down = refs[:2], refs[2:]
     out_ref[:, : NEAR_BLOCKS * 128] = near_ref[...]
-    for which, refs in enumerate((up, up_s)):
-        for copy in copies[2 * which : 2 * which + 2]:
-            copy.wait()
-        for part in range(2):
-            rhs[2 * which + part] = paired(refs, part)
-        terms = [mm(lhs_ref[part], rhs[2 * which + part]) for part in range(2)]
+    for copy in copies[:2]:
+        copy.wait()
+    for part in range(2):
+        rhs[part] = paired(up, part)
+    for which in range(2):
+        terms = [mm(lhs_ref[2 * which + part], rhs[part]) for part in range(2)]
         columns_of(out_ref, NEAR_BLOCKS + which)[...] = fold(terms[0] + terms[1])
-    for copy in copies[4:]:
+    for copy in copies[2:]:
         copy.wait()
-    side = jnp.where(y_ref[0] < 2, 0, 2)
-    terms = [mm(turned(down, part), rhs[side + part]) for part in range(2)]
+    terms = [mm(turned(down, part), rhs[part]) for part in range(2)]
     columns_of(out_ref, 4)[...] = fold(terms[0] + terms[1])
 
 
@@ -248,7 +248,7 @@
         near_kernel,
         out_shape=(
             jax.ShapeDtypeStruct((cols, NEAR_BLOCKS * cols), F32),
-            jax.ShapeDtypeStruct((2, 2 * cols, rows), BF),
+            jax.ShapeDtypeStruct((4, 2 * cols, rows), BF),
         ),
         in_specs=[VMEM_SPEC] * len(operands),
         out_specs=(VMEM_SPEC, VMEM_SPEC),
@@ -258,24 +258,23 @@
     )(*operands)
 
 
-def gram_far(y, near, lhs, pieces):
+def gram_far(near, lhs, pieces):
     operands = flat(pieces)
     rows, cols = operands[0].shape
     return pl.pallas_call(
         far_kernel,
         out_shape=jax.ShapeDtypeStruct((cols, GRAM_BLOCKS * cols), F32),
-        in_specs=[SMEM_SPEC, VMEM_SPEC, VMEM_SPEC]
-        + [pl.BlockSpec(memory_space=pl.ANY)] * len(operands),
+        in_specs=[VMEM_SPEC, VMEM_SPEC] + [pl.BlockSpec(memory_space=pl.ANY)] * len(operands),
         out_specs=VMEM_SPEC,
         scratch_shapes=[
-            pltpu.VMEM((4, rows, 2 * cols), BF),
+            pltpu.VMEM((2, rows, 2 * cols), BF),
             pltpu.VMEM((len(operands), rows, cols), F32),
             pltpu.SemaphoreType.DMA((len(operands),)),
         ],
         compiler_params=pltpu.CompilerParams(vmem_limit_bytes=30 * 2**20),
         cost_estimate=cost(48 * rows * cols * cols, 24 * rows * cols),
         name="gram_far",
-    )(y, near, lhs, *operands)
+    )(near, lhs, *operands)
 
 
 KEEP = {0: 1, 3: 2, 4: 1, 8: 1}
@@ -320,8 +319,8 @@
             put(here, 4 * (1 - k) + row, block(k, row, 1) * square)
             for one, two, b in (
                 (here, 4 * k + after, 2),
-                (here, 4 * (1 - k) + after, 3),
-                (4 * k + before, 4 * side + after, 4),
+                (4 * (1 - k) + row, 4 * k + after, 3),
+                (4 * side + before, 4 * k + after, 4),
             ):
                 value = block(k, row, b) * square
                 put(one, two, value)
@@ -354,9 +353,12 @@
     factor[:, :128] = high
     factor[:, 128:] = low
 
+    def core(k, dy):
+        return jnp.where(y < 2, k, 1 - k) if dy == 3 else k
+
     rhs = jnp.concatenate(
         [
-            factor[pl.ds(pl.multiple_of((4 * k + lax.rem(y + dy, 4)) * 128, 128), 128), :]
+            factor[pl.ds(pl.multiple_of((4 * core(k, dy) + lax.rem(y + dy, 4)) * 128, 128), 128), :]
             for k, dy in PIECES
         ],
         axis=0,
@@ -424,8 +426,17 @@
             value, "vec", [((i + 2 * step) % vec_count, i) for i in range(vec_count)]
         )
 
+    def from_last(value):
+        return lax.ppermute(
+            value, "vec", [((i - 2) % vec_count ^ (i >= 4), i) for i in range(vec_count)]
+        )
+
     def swap(value):
         return lax.ppermute(value, "vec", [(i, i ^ 1) for i in range(vec_count)])
+
+    def across_last(value):
+        sources = [(i - 2) % vec_count for i in range(vec_count)]
+        return lax.ppermute(value, "vec", [(s ^ (s >= 4), i) for i, s in enumerate(sources)])
 
     blocks = pack(vectors.reshape(block_rows, block_size, panel_cols))
     split_h = split_blocks(hamiltonian)
@@ -441,14 +452,14 @@
         second = applied(True, first, blocks[chunk])
         own.append(second.reshape(rows_dev // 2, panel_cols))
         up.append(from_y(own[-1], 1))
-        down.append(from_y(own[-1], -1))
+        down.append(from_last(own[-1]))
         own_s.append(swap(own[-1]))
         up_s.append(swap(up[-1]))
         down_s.append(swap(down[-1]))
-        across.append(from_y((up, down)[chunk][-1], (1, -1)[chunk]))
+        across.append(across_last(down[-1]) if chunk else from_y(up[-1], 1))
         across_s.append(swap(across[-1]))
     near, lhs = gram_near((own, own_s))
-    share = gram_far(y, near, lhs, (up, up_s, down))
+    share = gram_far(near, lhs, (up, down))
     strip = share.shape[0] // row_count
     parts = lax.all_to_all(
         share.reshape(row_count, strip, -1), "row", split_axis=0, concat_axis=0, tiled=True

time: 173 us -> 180 us (1.040)
  waiting for transfers between devices: 32.7 us -> 38.4 us
  starting transfers between devices: 42.2 us -> 37.7 us
  local copies, waits for them, and re-layouts: 3.23 us -> 7.16 us
  blocking collectives: 37.2 us -> 39.2 us
    ppermute x0 -> x3, waiting for transfers between devices: none -> 4.72 us  [the longest x2 3.42 us: from_last(): lax.ppermute(value, 'vec', [((i - 2) % vec_count ^ (i >= 4), i) for i in...]
    unnamed x8 -> x18, local copies, waits for them, and re-layouts: 3.06 us -> 6.99 us
    ppermute x6 -> x3, waiting for transfers between devices: 31.2 us -> 27.7 us  [from_y(): lax.ppermute(value, 'vec', [((i + 2 * step) % vec_count, i) for i in rang...]
    ppermute x9, starting transfers between devices: 14 us -> 10.5 us  [swap(): return lax.ppermute(value, 'vec', [(i, i ^ 1) for i in range(vec_count)])]
    ppermute x6 -> x3, starting transfers between devices: 6.84 us -> 3.6 us  [from_y(): lax.ppermute(value, 'vec', [((i + 2 * step) % vec_count, i) for i in rang...]
    ppermute x8, waiting for transfers between devices: 0.02 us -> 2.56 us  [from_row(): lax.ppermute(value, 'row', [((i + step) % row_count, i) for i in range(ro...]
    all_to_all x1, blocking collectives: 22.9 us -> 25.2 us  [on_device(): lax.all_to_all(jnp.broadcast_to(part[None], (members,) + part.shape), ('r...]
    ppermute x0 -> x3, starting transfers between devices: none -> 2.15 us  [the longest x2 1.08 us: from_last(): lax.ppermute(value, 'vec', [((i - 2) % vec_count ^ (i >= 4), i) for i in...]
  transfers between devices with their start and end apart: 23 -> 23, of which waited for: 5 -> 9; matrix products, arithmetic and copies ran while one was open for 1% -> 1% of each run, Pallas kernels for 18% -> 17%
where the time goes in v7:
time: 180 us; the launch traced here: 179 us
  Pallas kernels  54.1 us (30%)
  blocking collectives  39.2 us (22%)
  waiting for transfers between devices  38.4 us (21%)
  starting transfers between devices  37.7 us (21%)
  local copies, waits for them, and re-layouts  7.16 us (4%)
    ppermute x3, waiting for transfers between devices, from_y(): lax.ppermute(value, 'vec', [((i + 2 * step) % vec_count, i) for i in rang...  27.7 us
    all_to_all x1, blocking collectives, on_device(): lax.all_to_all(jnp.broadcast_to(part[None], (members,) + part.shape), ('r...  25.2 us
    pallas_call x4, Pallas kernels, apply_field(): pl.pallas_call(functools.partial(field_kernel, second), out_shape=jax.Sha...  22.7 us
    ppermute x8, starting transfers between devices, from_row(): lax.ppermute(value, 'row', [((i + step) % row_count, i) for i in range(ro...  21.4 us
    pallas_call x1, Pallas kernels, finish(): pl.pallas_call(functools.partial(finish_kernel, total_rows), out_shape=ja...  20.8 us
    all_to_all x1, blocking collectives, on_device(): lax.all_to_all(share.reshape(row_count, strip, -1), 'row', split_axis=0,...  13.9 us
    ppermute x9, starting transfers between devices, swap(): return lax.ppermute(value, 'vec', [(i, i ^ 1) for i in range(vec_count)])  10.5 us
    unnamed x18, local copies, waits for them, and re-layouts  6.99 us
  transfers between devices with their start and end apart: 23, of which 9 were waited for; matrix products, arithmetic and copies ran while one was open for 1% of the time, Pallas kernels for 17%

profile of v7, /device:TPU:1, one launch (start us, length us, event | category | flops | bytes accessed | tf_op | source)
XLA Modules:
  0.0 179.1 jit_solution(2866355940978841456)
XLA Ops:
  0.0 1.2 copy-done
  1.2 0.5 pack.1
  1.8 2.1 %collective-permute-start = (f32[8,128,128]{2,1,0:T(8,128)S(1)}, f32[8,128,128]{2,1,0:T(8,128)S(1)}, u32[]{:S(2)}, u32[]{:S(2)}) collective-permute-start(f32[8,128,128]{2,1,0:T(8,128)S(1)} %get-tuple-element.9.own_ref.rest_0_), channel_id=1, source_target_pairs={{120,0},{0,8},{8,16},{16,24},{24,32},{32,40},{40,48},{48,56},{56,6... | collective-permute-start | bytes 1572872 | tf_op jit(solution)/shard_map/ppermute | solution.py:422
  3.9 4.8 %collective-permute-start.1 = (f32[8,128,128]{2,1,0:T(8,128)S(1)}, f32[8,128,128]{2,1,0:T(8,128)S(1)}, u32[]{:S(2)}, u32[]{:S(2)}) collective-permute-start(f32[8,128,128]{2,1,0:T(8,128)S(1)} %get-tuple-element.9.own_ref.rest_0_), channel_id=1, source_target_pairs={{8,0},{16,8},{24,16},{32,24},{40,32},{48,40},{56,48},{64,56},{72,6... | collective-permute-start | bytes 1572872 | tf_op jit(solution)/shard_map/ppermute | solution.py:422
  8.7 4.8 %collective-permute-start.5 = (f32[8,128,128]{2,1,0:T(8,128)S(1)}, f32[8,128,128]{2,1,0:T(8,128)S(1)}, u32[]{:S(2)}, u32[]{:S(2)}) collective-permute-start(f32[8,128,128]{2,1,0:T(8,128)S(1)} %get-tuple-element.10.own_ref.rest_0_), channel_id=1, source_target_pairs={{8,0},{16,8},{24,16},{32,24},{40,32},{48,40},{56,48},{64,56},{72,6... | collective-permute-start | bytes 1572872 | tf_op jit(solution)/shard_map/ppermute | solution.py:422
  14.8 0.8 fusion.2
  15.7 0.1 reshape.30.cols_ref
  15.8 6.3 %split_blocks.1.h_ref = bf16[16,12,256,128]{3,2,1,0:T(8,128)(2,1)S(1)} custom-call(f32[16,12,128,128]{3,2,1,0:T(8,128)} %h_ref.1), custom_call_target="tpu_custom_call" | custom-call | bytes 25165824 | tf_op jit(solution)/shard_map/split_blocks/pallas_call | solution.py:65
  22.1 5.7 %field.4.own_ref = f32[8,128,128]{2,1,0:T(8,128)S(1)} custom-call(s32[192]{0:T(256)S(1)} %reshape.30.cols_ref, f32[2]{0:T(128)S(1)} %pad_maximum_fusion.coef_ref, bf16[16,12,256,128]{3,2,1,0:T(8,128)(2,1)S(1)} %split_blocks.1.h_ref, f32[8,128,128]{2,1,0:T(8,128)S(1)} %collective-permute-done.left_ref, f32[8,128,128]{2,1,0:T(8,128)S(1)} %get-tuple-element.9.own_ref.rest_0_, ...), custom_call_target="tpu_custom_call" | custom-call | flops 3221225472 | bytes 12582912 | tf_op jit(solution)/shard_map/field/pallas_call | solution.py:165
  27.8 4.8 %collective-permute-start.3 = (f32[8,128,128]{2,1,0:T(8,128)S(1)}, f32[8,128,128]{2,1,0:T(8,128)S(1)}, u32[]{:S(2)}, u32[]{:S(2)}) collective-permute-start(f32[8,128,128]{2,1,0:T(8,128)S(1)} %field.4.own_ref), channel_id=1, source_target_pairs={{8,0},{16,8},{24,16},{32,24},{40,32},{48,40},{56,48},{64,56},{72,6... | collective-permute-start | bytes 1572872 | tf_op jit(solution)/shard_map/ppermute | solution.py:422
  32.6 5.7 %field.6.own_ref = f32[8,128,128]{2,1,0:T(8,128)S(1)} custom-call(s32[192]{0:T(256)S(1)} %reshape.30.cols_ref, f32[2]{0:T(128)S(1)} %pad_maximum_fusion.coef_ref, bf16[16,12,256,128]{3,2,1,0:T(8,128)(2,1)S(1)} %split_blocks.1.h_ref, f32[8,128,128]{2,1,0:T(8,128)S(1)} %collective-permute-done.4.left_ref, ...), custom_call_target="tpu_custom_call" | custom-call | flops 3221225472 | bytes 12582912 | tf_op jit(solution)/shard_map/field/pallas_call | solution.py:165
  38.3 4.8 %collective-permute-start.7 = (f32[8,128,128]{2,1,0:T(8,128)S(1)}, f32[8,128,128]{2,1,0:T(8,128)S(1)}, u32[]{:S(2)}, u32[]{:S(2)}) collective-permute-start(f32[8,128,128]{2,1,0:T(8,128)S(1)} %field.6.own_ref), channel_id=1, source_target_pairs={{8,0},{16,8},{24,16},{32,24},{40,32},{48,40},{56,48},{64,56},{72,6... | collective-permute-start | bytes 1572872 | tf_op jit(solution)/shard_map/ppermute | solution.py:422
  43.1 5.7 %field.5 = f32[8,128,128]{2,1,0:T(8,128)S(1)} custom-call(s32[192]{0:T(256)S(1)} %reshape.30.cols_ref, f32[2]{0:T(128)S(1)} %pad_maximum_fusion.coef_ref, bf16[16,12,256,128]{3,2,1,0:T(8,128)(2,1)S(1)} %split_blocks.1.h_ref, f32[8,128,128]{2,1,0:T(8,128)S(1)} %collective-permute-done.2.left_ref, f32[8,128,128]{2,1,0:T(8,128)S(1)} %field.4.own_ref, ...), custom_call_target="tpu_custom_call" | custom-call | flops 3221225472 | bytes 12582912 | tf_op jit(solution)/shard_map/field/pallas_call | solution.py:165
  48.8 3.1 %collective-permute-start.8 = (f32[1024,128]{1,0:T(8,128)S(1)}, f32[1024,128]{1,0:T(8,128)S(1)}, u32[]{:S(2)}, u32[]{:S(2)}) collective-permute-start(f32[1024,128]{1,0:T(8,128)S(1)} %bitcast.6), channel_id=1, source_target_pairs={{0,1},{1,0},{2,3},{3,2},{4,5},{5,4},{6,7},{7,6},{8,9},{9,8},{10,11... | collective-permute-start | bytes 1572872 | tf_op jit(solution)/shard_map/ppermute | solution.py:435
  51.9 2.5 %collective-permute-done.6.left_ref = f32[8,128,128]{2,1,0:T(8,128)S(1)} collective-permute-done((f32[8,128,128]{2,1,0:T(8,128)S(1)}, f32[8,128,128]{2,1,0:T(8,128)S(1)}, u32[]{:S(2)}, u32[]{:S(2)}) %collective-permute-start.6) | collective-permute-done | bytes 524320 | tf_op jit(solution)/shard_map/ppermute | solution.py:422
  54.5 5.7 %field.7 = f32[8,128,128]{2,1,0:T(8,128)S(1)} custom-call(s32[192]{0:T(256)S(1)} %reshape.30.cols_ref, f32[2]{0:T(128)S(1)} %pad_maximum_fusion.coef_ref, bf16[16,12,256,128]{3,2,1,0:T(8,128)(2,1)S(1)} %split_blocks.1.h_ref, f32[8,128,128]{2,1,0:T(8,128)S(1)} %collective-permute-done.6.left_ref, f32[8,128,128]{2,1,0:T(8,128)S(1)} %field.6.own_ref, ...), custom_call_target="tpu_custom_call" | custom-call | flops 3221225472 | bytes 12582912 | tf_op jit(solution)/shard_map/field/pallas_call | solution.py:165
  60.1 2.5 %collective-permute-start.9 = (f32[1024,128]{1,0:T(8,128)S(1)}, f32[1024,128]{1,0:T(8,128)S(1)}, u32[]{:S(2)}, u32[]{:S(2)}) collective-permute-start(f32[1024,128]{1,0:T(8,128)S(1)} %bitcast.11), channel_id=1, source_target_pairs={{0,1},{1,0},{2,3},{3,2},{4,5},{5,4},{6,7},{7,6},{8,9},{9,8},{10,11... | collective-permute-start | bytes 1572872 | tf_op jit(solution)/shard_map/ppermute | solution.py:435
  62.6 2.7 %collective-permute-start.10 = (f32[1024,128]{1,0:T(8,128)S(1)}, f32[1024,128]{1,0:T(8,128)S(1)}, u32[]{:S(2)}, u32[]{:S(2)}) collective-permute-start(f32[1024,128]{1,0:T(8,128)S(1)} %bitcast.7), channel_id=1, source_target_pairs={{2,0},{3,1},{4,2},{5,3},{6,4},{7,5},{0,6},{1,7},{10,8},{11,9},{12,... | collective-permute-start | bytes 1572872 | tf_op jit(solution)/shard_map/ppermute | solution.py:425
  65.4 0.5 collective-permute-start.11
  65.8 1.0 collective-permute-start.12
  66.9 1.8 gram_near.1
  68.7 7.9 %collective-permute-done.10.rest_0_.rest_4_ = f32[1024,128]{1,0:T(8,128)S(1)} collective-permute-done((f32[1024,128]{1,0:T(8,128)S(1)}, f32[1024,128]{1,0:T(8,128)S(1)}, u32[]{:S(2)}, u32[]{:S(2)}) %collective-permute-start.10) | collective-permute-done | bytes 524320 | tf_op jit(solution)/shard_map/ppermute | solution.py:425
  76.6 11.2 %collective-permute-done.11.rest_1_.rest_5_ = f32[1024,128]{1,0:T(8,128)S(1)} collective-permute-done((f32[1024,128]{1,0:T(8,128)S(1)}, f32[1024,128]{1,0:T(8,128)S(1)}, u32[]{:S(2)}, u32[]{:S(2)}) %collective-permute-start.11) | collective-permute-done | bytes 524320 | tf_op jit(solution)/shard_map/ppermute | solution.py:425
  87.8 3.4 %collective-permute-done.13.rest_3_.rest_9_ = f32[1024,128]{1,0:T(8,128)} collective-permute-done((f32[1024,128]{1,0:T(8,128)S(1)}, f32[1024,128]{1,0:T(8,128)}, u32[]{:S(2)}, u32[]{:S(2)}) %collective-permute-start.13) | collective-permute-done | bytes 524320 | tf_op jit(solution)/shard_map/ppermute | solution.py:430
  91.2 2.1 %gram_far.1 = f32[128,640]{1,0:T(8,128)S(1)} custom-call(f32[128,256]{1,0:T(8,128)S(1)} %get-tuple-element.11.near_ref, bf16[4,256,1024]{2,1,0:T(8,128)(2,1)S(1)} %get-tuple-element.12.lhs_ref, f32[1024,128]{1,0:T(8,128)S(1)} %collective-permute-done.10.rest_0_.rest_4_, f32[1024,128]{1,0:T(8,128)S(1)} %collective-permute-done.11.rest_1_.rest_5_, ...), custom_call_target="tpu_custom_call" | custom-call | flops 805306368 | bytes 3145728 | tf_op jit(solution)/shard_map/gram_far/pallas_call | solution.py:264
  93.3 13.9 %all_to_all.10 = f32[16,8,640]{2,1,0:T(8,128)S(1)} all-to-all(f32[16,8,640]{2,1,0:T(8,128)S(1)} %bitcast.16), channel_id=1, replica_groups=mesh['row'=16,'vec'=8] {'row'}, dimensions={0} | all-to-all | bytes 655360 | tf_op jit(solution)/shard_map/all_to_all | solution.py:464
  107.3 0.1 broadcast_in_dim.17
  107.4 25.2 %all_to_all.11 = f32[64,8,640]{2,1,0:T(8,128)S(1)} all-to-all(f32[64,8,640]{2,1,0:T(8,128)S(1)} %broadcast_in_dim.17), channel_id=1, replica_groups={{0,2,4,6,8,10,12,14,16,18,20,22,24,26,28,30,32,34,36,38,40,42,44,46,48,..., dimensions={0} | all-to-all | bytes 2621440 | tf_op jit(solution)/shard_map/all_to_all | solution.py:473
  132.6 2.8 %collective-permute-start.14 = (f32[16,4,8,640]{3,2,1,0:T(8,128)S(1)}, f32[16,4,8,640]{3,2,1,0:T(8,128)}, u32[]{:S(2)}, u32[]{:S(2)}) collective-permute-start(f32[16,4,8,640]{3,2,1,0:T(8,128)S(1)} %bitcast.17), channel_id=1, source_target_pairs={{0,1},{1,0},{2,3},{3,2},{4,5},{5,4},{6,7},{7,6},{8,9},{9,8},{10,11... | collective-permute-start | bytes 3932168 | tf_op jit(solution)/shard_map/ppermute | solution.py:435
  135.4 0.5 collective-permute-start.16
  135.9 0.4 collective-permute-start.19
  136.3 1.1 collective-permute-start.20
  137.3 1.4 collective-permute-done.15.rest_6_
  138.8 0.8 copy-done.5
  139.6 0.4 collective-permute-start.17
  140.0 0.8 copy-done.7
  140.8 0.1 collective-permute-start.18
  140.9 8.6 %collective-permute-done.19.rest_12_ = f32[1024,128]{1,0:T(8,128)} collective-permute-done((f32[1024,128]{1,0:T(8,128)S(1)}, f32[1024,128]{1,0:T(8,128)}, u32[]{:S(2)}, u32[]{:S(2)}) %collective-permute-start.19) | collective-permute-done | bytes 524320 | tf_op jit(solution)/shard_map/ppermute | solution.py:425
  149.5 0.9 collective-permute-start.21
  150.3 1.3 collective-permute-done.20.rest_13_
  151.6 0.3 collective-permute-start.22
  151.9 0.3 collective-permute-done.21.rest_14_
  152.2 1.7 collective-permute-done.22.rest_15_
  153.9 1.0 copy-done.2
  154.9 1.0 copy-done.4
  156.0 1.0 copy-done.6
  157.0 1.0 copy-done.8
  158.0 20.8 %finish.1 = f32[2048,128]{1,0:T(8,128)} custom-call(s32[1]{0:T(128)} %bitcast.y_ref, f32[16,4,8,640]{3,2,1,0:T(8,128)S(1)} %bitcast.18, f32[16,4,8,640]{3,2,1,0:T(8,128)} %collective-permute-done.14.gb_ref, f32[1024,128]{1,0:T(8,128)S(1)} %bitcast.10, f32[1024,128]{1,0:T(8,128)S(1)} %bitcast.15, f32[1024,128]{1,0:T(8,128)S(1)} %copy-done.2, ...), custom_call_target="tpu_custom_call" | custom-call | flops 9663676416 | bytes 9437184 | tf_op jit(solution)/shard_map/finish/pallas_call | solution.py:387
  (32 shorter events, 0.4 us)
Async XLA Ops:
  0.0 1.2 copy-start
  1.8 20.3 %collective-permute-start = (f32[8,128,128]{2,1,0:T(8,128)S(1)}, f32[8,128,128]{2,1,0:T(8,128)S(1)}, u32[]{:S(2)}, u32[]{:S(2)}) collective-permute-start(f32[8,128,128]{2,1,0:T(8,128)S(1)} %get-tuple-element.9.own_ref.rest_0_), channel_id=1, source_target_pairs={{120,0},{0,8},{8,16},{16,24},{24,32},{32,40},{40,48},{48,56},{56,6... | collective-permute-start | bytes 1572872 | tf_op jit(solution)/shard_map/ppermute | solution.py:422
  3.9 18.2 %collective-permute-start.1 = (f32[8,128,128]{2,1,0:T(8,128)S(1)}, f32[8,128,128]{2,1,0:T(8,128)S(1)}, u32[]{:S(2)}, u32[]{:S(2)}) collective-permute-start(f32[8,128,128]{2,1,0:T(8,128)S(1)} %get-tuple-element.9.own_ref.rest_0_), channel_id=1, source_target_pairs={{8,0},{16,8},{24,16},{32,24},{40,32},{48,40},{56,48},{64,56},{72,6... | collective-permute-start | bytes 1572872 | tf_op jit(solution)/shard_map/ppermute | solution.py:422
  8.7 23.9 %collective-permute-start.4 = (f32[8,128,128]{2,1,0:T(8,128)S(1)}, f32[8,128,128]{2,1,0:T(8,128)S(1)}, u32[]{:S(2)}, u32[]{:S(2)}) collective-permute-start(f32[8,128,128]{2,1,0:T(8,128)S(1)} %get-tuple-element.10.own_ref.rest_0_), channel_id=1, source_target_pairs={{120,0},{0,8},{8,16},{16,24},{24,32},{32,40},{40,48},{48,56},{56,6... | collective-permute-start | bytes 1572872 | tf_op jit(solution)/shard_map/ppermute | solution.py:422
  8.7 23.9 %collective-permute-start.5 = (f32[8,128,128]{2,1,0:T(8,128)S(1)}, f32[8,128,128]{2,1,0:T(8,128)S(1)}, u32[]{:S(2)}, u32[]{:S(2)}) collective-permute-start(f32[8,128,128]{2,1,0:T(8,128)S(1)} %get-tuple-element.10.own_ref.rest_0_), channel_id=1, source_target_pairs={{8,0},{16,8},{24,16},{32,24},{40,32},{48,40},{56,48},{64,56},{72,6... | collective-permute-start | bytes 1572872 | tf_op jit(solution)/shard_map/ppermute | solution.py:422
  27.7 15.4 %collective-permute-start.2 = (f32[8,128,128]{2,1,0:T(8,128)S(1)}, f32[8,128,128]{2,1,0:T(8,128)S(1)}, u32[]{:S(2)}, u32[]{:S(2)}) collective-permute-start(f32[8,128,128]{2,1,0:T(8,128)S(1)} %field.4.own_ref), channel_id=1, source_target_pairs={{120,0},{0,8},{8,16},{16,24},{24,32},{32,40},{40,48},{48,56},{56,6... | collective-permute-start | bytes 1572872 | tf_op jit(solution)/shard_map/ppermute | solution.py:422
  27.8 15.3 %collective-permute-start.3 = (f32[8,128,128]{2,1,0:T(8,128)S(1)}, f32[8,128,128]{2,1,0:T(8,128)S(1)}, u32[]{:S(2)}, u32[]{:S(2)}) collective-permute-start(f32[8,128,128]{2,1,0:T(8,128)S(1)} %field.4.own_ref), channel_id=1, source_target_pairs={{8,0},{16,8},{24,16},{32,24},{40,32},{48,40},{56,48},{64,56},{72,6... | collective-permute-start | bytes 1572872 | tf_op jit(solution)/shard_map/ppermute | solution.py:422
  38.3 16.2 %collective-permute-start.6 = (f32[8,128,128]{2,1,0:T(8,128)S(1)}, f32[8,128,128]{2,1,0:T(8,128)S(1)}, u32[]{:S(2)}, u32[]{:S(2)}) collective-permute-start(f32[8,128,128]{2,1,0:T(8,128)S(1)} %field.6.own_ref), channel_id=1, source_target_pairs={{120,0},{0,8},{8,16},{16,24},{24,32},{32,40},{40,48},{48,56},{56,6... | collective-permute-start | bytes 1572872 | tf_op jit(solution)/shard_map/ppermute | solution.py:422
  38.3 16.1 %collective-permute-start.7 = (f32[8,128,128]{2,1,0:T(8,128)S(1)}, f32[8,128,128]{2,1,0:T(8,128)S(1)}, u32[]{:S(2)}, u32[]{:S(2)}) collective-permute-start(f32[8,128,128]{2,1,0:T(8,128)S(1)} %field.6.own_ref), channel_id=1, source_target_pairs={{8,0},{16,8},{24,16},{32,24},{40,32},{48,40},{56,48},{64,56},{72,6... | collective-permute-start | bytes 1572872 | tf_op jit(solution)/shard_map/ppermute | solution.py:422
  48.8 18.0 %collective-permute-start.8 = (f32[1024,128]{1,0:T(8,128)S(1)}, f32[1024,128]{1,0:T(8,128)S(1)}, u32[]{:S(2)}, u32[]{:S(2)}) collective-permute-start(f32[1024,128]{1,0:T(8,128)S(1)} %bitcast.6), channel_id=1, source_target_pairs={{0,1},{1,0},{2,3},{3,2},{4,5},{5,4},{6,7},{7,6},{8,9},{9,8},{10,11... | collective-permute-start | bytes 1572872 | tf_op jit(solution)/shard_map/ppermute | solution.py:435
  60.1 6.8 %collective-permute-start.9 = (f32[1024,128]{1,0:T(8,128)S(1)}, f32[1024,128]{1,0:T(8,128)S(1)}, u32[]{:S(2)}, u32[]{:S(2)}) collective-permute-start(f32[1024,128]{1,0:T(8,128)S(1)} %bitcast.11), channel_id=1, source_target_pairs={{0,1},{1,0},{2,3},{3,2},{4,5},{5,4},{6,7},{7,6},{8,9},{9,8},{10,11... | collective-permute-start | bytes 1572872 | tf_op jit(solution)/shard_map/ppermute | solution.py:435
  62.6 13.9 %collective-permute-start.10 = (f32[1024,128]{1,0:T(8,128)S(1)}, f32[1024,128]{1,0:T(8,128)S(1)}, u32[]{:S(2)}, u32[]{:S(2)}) collective-permute-start(f32[1024,128]{1,0:T(8,128)S(1)} %bitcast.7), channel_id=1, source_target_pairs={{2,0},{3,1},{4,2},{5,3},{6,4},{7,5},{0,6},{1,7},{10,8},{11,9},{12,... | collective-permute-start | bytes 1572872 | tf_op jit(solution)/shard_map/ppermute | solution.py:425
  65.4 22.4 %collective-permute-start.11 = (f32[1024,128]{1,0:T(8,128)S(1)}, f32[1024,128]{1,0:T(8,128)S(1)}, u32[]{:S(2)}, u32[]{:S(2)}) collective-permute-start(f32[1024,128]{1,0:T(8,128)S(1)} %bitcast.12), channel_id=1, source_target_pairs={{2,0},{3,1},{4,2},{5,3},{6,4},{7,5},{0,6},{1,7},{10,8},{11,9},{12,... | collective-permute-start | bytes 1572872 | tf_op jit(solution)/shard_map/ppermute | solution.py:425
  65.8 22.0 %collective-permute-start.12 = (f32[1024,128]{1,0:T(8,128)S(1)}, f32[1024,128]{1,0:T(8,128)}, u32[]{:S(2)}, u32[]{:S(2)}) collective-permute-start(f32[1024,128]{1,0:T(8,128)S(1)} %bitcast.8), channel_id=1, source_target_pairs={{6,0},{7,1},{0,2},{1,3},{3,4},{2,5},{5,6},{4,7},{14,8},{15,9},{8,1... | collective-permute-start | bytes 1572872 | tf_op jit(solution)/shard_map/ppermute | solution.py:430
  66.8 24.4 %copy-start.1 = (f32[1024,128]{1,0:T(8,128)}, f32[1024,128]{1,0:T(8,128)S(1)}, u32[]{:S(2)}) copy-start(f32[1024,128]{1,0:T(8,128)S(1)} %collective-permute-done.8.rest_2_) | copy-start | bytes 1572868
  66.8 24.4 %collective-permute-start.13 = (f32[1024,128]{1,0:T(8,128)S(1)}, f32[1024,128]{1,0:T(8,128)}, u32[]{:S(2)}, u32[]{:S(2)}) collective-permute-start(f32[1024,128]{1,0:T(8,128)S(1)} %bitcast.13), channel_id=1, source_target_pairs={{6,0},{7,1},{0,2},{1,3},{3,4},{2,5},{5,6},{4,7},{14,8},{15,9},{8,1... | collective-permute-start | bytes 1572872 | tf_op jit(solution)/shard_map/ppermute | solution.py:430
  66.9 26.4 %copy-start.3 = (f32[1024,128]{1,0:T(8,128)}, f32[1024,128]{1,0:T(8,128)S(1)}, u32[]{:S(2)}) copy-start(f32[1024,128]{1,0:T(8,128)S(1)} %collective-permute-done.9.rest_3_) | copy-start | bytes 1572868
  132.6 21.3 %collective-permute-start.14 = (f32[16,4,8,640]{3,2,1,0:T(8,128)S(1)}, f32[16,4,8,640]{3,2,1,0:T(8,128)}, u32[]{:S(2)}, u32[]{:S(2)}) collective-permute-start(f32[16,4,8,640]{3,2,1,0:T(8,128)S(1)} %bitcast.17), channel_id=1, source_target_pairs={{0,1},{1,0},{2,3},{3,2},{4,5},{5,4},{6,7},{7,6},{8,9},{9,8},{10,11... | collective-permute-start | bytes 3932168 | tf_op jit(solution)/shard_map/ppermute | solution.py:435
  135.4 3.4 %collective-permute-start.15 = (f32[1024,128]{1,0:T(8,128)S(1)}, f32[1024,128]{1,0:T(8,128)S(1)}, u32[]{:S(2)}, u32[]{:S(2)}) collective-permute-start(f32[1024,128]{1,0:T(8,128)S(1)} %collective-permute-done.10.rest_0_.rest_4_), channel_id=1, source_target_pairs={{0,1},{1,0},{2,3},{3,2},{4,5},{5,4},{6,7},{7,6},{8,9},{9,8},{10,11... | collective-permute-start | bytes 1572872 | tf_op jit(solution)/shard_map/ppermute | solution.py:435
  135.4 4.6 %collective-permute-start.16 = (f32[1024,128]{1,0:T(8,128)S(1)}, f32[1024,128]{1,0:T(8,128)S(1)}, u32[]{:S(2)}, u32[]{:S(2)}) collective-permute-start(f32[1024,128]{1,0:T(8,128)S(1)} %collective-permute-done.11.rest_1_.rest_5_), channel_id=1, source_target_pairs={{0,1},{1,0},{2,3},{3,2},{4,5},{5,4},{6,7},{7,6},{8,9},{9,8},{10,11... | collective-permute-start | bytes 1572872 | tf_op jit(solution)/shard_map/ppermute | solution.py:435
  135.9 13.6 %collective-permute-start.19 = (f32[1024,128]{1,0:T(8,128)S(1)}, f32[1024,128]{1,0:T(8,128)}, u32[]{:S(2)}, u32[]{:S(2)}) collective-permute-start(f32[1024,128]{1,0:T(8,128)S(1)} %collective-permute-done.10.rest_0_.rest_4_), channel_id=1, source_target_pairs={{2,0},{3,1},{4,2},{5,3},{6,4},{7,5},{0,6},{1,7},{10,8},{11,9},{12,... | collective-permute-start | bytes 1572872 | tf_op jit(solution)/shard_map/ppermute | solution.py:425
  136.3 15.3 %collective-permute-start.20 = (f32[1024,128]{1,0:T(8,128)}, f32[1024,128]{1,0:T(8,128)}, u32[]{:S(2)}, u32[]{:S(2)}) collective-permute-start(f32[1024,128]{1,0:T(8,128)} %collective-permute-done.13.rest_3_.rest_9_), channel_id=1, source_target_pairs={{7,0},{6,1},{0,2},{1,3},{2,4},{3,5},{5,6},{4,7},{15,8},{14,9},{8,1... | collective-permute-start | bytes 1572872 | tf_op jit(solution)/shard_map/ppermute | solution.py:439
  138.8 0.8 copy-start.5
  139.6 12.3 %collective-permute-start.17 = (f32[1024,128]{1,0:T(8,128)}, f32[1024,128]{1,0:T(8,128)}, u32[]{:S(2)}, u32[]{:S(2)}) collective-permute-start(f32[1024,128]{1,0:T(8,128)} %collective-permute-done.12.rest_2_.rest_8_), channel_id=1, source_target_pairs={{0,1},{1,0},{2,3},{3,2},{4,5},{5,4},{6,7},{7,6},{8,9},{9,8},{10,11... | collective-permute-start | bytes 1572872 | tf_op jit(solution)/shard_map/ppermute | solution.py:435
  140.0 0.8 copy-start.7
  140.8 11.2 %collective-permute-start.18 = (f32[1024,128]{1,0:T(8,128)}, f32[1024,128]{1,0:T(8,128)}, u32[]{:S(2)}, u32[]{:S(2)}) collective-permute-start(f32[1024,128]{1,0:T(8,128)} %collective-permute-done.13.rest_3_.rest_9_), channel_id=1, source_target_pairs={{0,1},{1,0},{2,3},{3,2},{4,5},{5,4},{6,7},{7,6},{8,9},{9,8},{10,11... | collective-permute-start | bytes 1572872 | tf_op jit(solution)/shard_map/ppermute | solution.py:435
  149.5 2.7 %collective-permute-start.21 = (f32[1024,128]{1,0:T(8,128)}, f32[1024,128]{1,0:T(8,128)}, u32[]{:S(2)}, u32[]{:S(2)}) collective-permute-start(f32[1024,128]{1,0:T(8,128)} %collective-permute-done.19.rest_12_), channel_id=1, source_target_pairs={{0,1},{1,0},{2,3},{3,2},{4,5},{5,4},{6,7},{7,6},{8,9},{9,8},{10,11... | collective-permute-start | bytes 1572872 | tf_op jit(solution)/shard_map/ppermute | solution.py:435
  151.6 2.3 %collective-permute-start.22 = (f32[1024,128]{1,0:T(8,128)}, f32[1024,128]{1,0:T(8,128)}, u32[]{:S(2)}, u32[]{:S(2)}) collective-permute-start(f32[1024,128]{1,0:T(8,128)} %collective-permute-done.20.rest_13_), channel_id=1, source_target_pairs={{0,1},{1,0},{2,3},{3,2},{4,5},{5,4},{6,7},{7,6},{8,9},{9,8},{10,11... | collective-permute-start | bytes 1572872 | tf_op jit(solution)/shard_map/ppermute | solution.py:435
  153.9 1.0 copy-start.2
  154.9 1.0 copy-start.4
  156.0 1.0 copy-start.6
  157.0 1.0 copy-start.8

commit v8 on v7

--- a/solution.py
+++ b/solution.py
@@ -277,6 +277,28 @@
     )(near, lhs, *operands)
 
 
+def total_kernel(parts_ref, out_ref):
+    total = parts_ref[0]
+    for n in range(1, parts_ref.shape[0]):
+        total += parts_ref[n]
+
+    @pl.loop(0, out_ref.shape[0], unroll=4)
+    def _(n):
+        out_ref[n] = total
+
+
+def strip_total(parts, copies):
+    return pl.pallas_call(
+        total_kernel,
+        out_shape=jax.ShapeDtypeStruct((copies,) + parts.shape[1:], F32),
+        in_specs=[VMEM_SPEC],
+        out_specs=VMEM_SPEC,
+        compiler_params=pltpu.CompilerParams(vmem_limit_bytes=8 * 2**20),
+        cost_estimate=cost(parts.size, 8 * parts.size),
+        name="total",
+    )(parts)
+
+
 KEEP = {0: 1, 3: 2, 4: 1, 8: 1}
 BASE = {2: 1, 6: 1, 10: 1, 11: 2}
 PIECES = ((0, 0), (1, 0), (0, 1), (1, 1), (0, 3), (1, 3), (0, 2), (1, 2))
@@ -388,7 +410,7 @@
         functools.partial(finish_kernel, total_rows),
         out_shape=jax.ShapeDtypeStruct((rows, cols), F32),
         in_specs=[SMEM_SPEC, VMEM_SPEC, VMEM_SPEC]
-        + [pl.BlockSpec(memory_space=pl.ANY)] * len(operands),
+        + [pl.BlockSpec(memory_space=pltpu.HBM)] * len(operands),
         out_specs=VMEM_SPEC,
         scratch_shapes=[
             pltpu.VMEM((NV, NV), BF),
@@ -446,32 +468,33 @@
         left = from_row(operand, -1)
         return apply_field(second, cols, coef, split_h, left, operand, right, prev)
 
-    own, own_s, up, up_s, down, down_s, across, across_s = ([] for _ in range(8))
+    own, beside, own_s, up, up_s, down, down_s, across, across_s = ([] for _ in range(9))
     for chunk in range(CHUNKS):
         first = applied(False, blocks[chunk])
         second = applied(True, first, blocks[chunk])
         own.append(second.reshape(rows_dev // 2, panel_cols))
         up.append(from_y(own[-1], 1))
         down.append(from_last(own[-1]))
-        own_s.append(swap(own[-1]))
+        beside.append(swap(own[-1]))
+        own_s.append(swap(lax.optimization_barrier(own[-1])))
         up_s.append(swap(up[-1]))
         down_s.append(swap(down[-1]))
         across.append(across_last(down[-1]) if chunk else from_y(up[-1], 1))
         across_s.append(swap(across[-1]))
-    near, lhs = gram_near((own, own_s))
+    near, lhs = gram_near((own, beside))
     share = gram_far(near, lhs, (up, down))
     strip = share.shape[0] // row_count
     parts = lax.all_to_all(
         share.reshape(row_count, strip, -1), "row", split_axis=0, concat_axis=0, tiled=True
     )
-    part = jnp.sum(parts, axis=0)
     groups = [
         [r * vec_count + v for r in range(row_count) for v in range(core, vec_count, 2)]
         for core in range(2)
     ]
     members = row_count * vec_count // 2
+    part = strip_total(parts, members)
     gram_a = lax.all_to_all(
-        jnp.broadcast_to(part[None], (members,) + part.shape),
+        part,
         ("row", "vec"),
         split_axis=0,
         concat_axis=0,

time: 180 us -> 181 us (level)
  blocking collectives: 39.2 us -> 13.9 us
  waiting for transfers between devices: 38.4 us -> 55.9 us
  starting transfers between devices: 37.7 us -> 45.7 us
    all_to_all x1 -> x0, blocking collectives: 25.2 us -> none  [on_device(): lax.all_to_all(jnp.broadcast_to(part[None], (members,) + part.shape), ('r...]
    all_to_all x0 -> x1, waiting for transfers between devices: none -> 17.4 us  [on_device(): lax.all_to_all(part, ('row', 'vec'), split_axis=0, concat_axis=0, tiled=T...]
    all_to_all x0 -> x1, starting transfers between devices: none -> 5.81 us  [on_device(): lax.all_to_all(part, ('row', 'vec'), split_axis=0, concat_axis=0, tiled=T...]
    ppermute x9 -> x11, starting transfers between devices: 10.5 us -> 12.8 us  [swap(): return lax.ppermute(value, 'vec', [(i, i ^ 1) for i in range(vec_count)])]
  transfers between devices with their start and end apart: 23 -> 26, of which waited for: 9 -> 11; matrix products, arithmetic and copies ran while one was open for 1% -> 1% of each run, Pallas kernels for 17% -> 17%
where the time goes in v8:
time: 181 us; the launch traced here: 180 us
  waiting for transfers between devices  55.9 us (31%)
  Pallas kernels  54.9 us (30%)
  starting transfers between devices  45.7 us (25%)
  blocking collectives  13.9 us (8%)
  local copies, waits for them, and re-layouts  7.07 us (4%)
    ppermute x3, waiting for transfers between devices, from_y(): lax.ppermute(value, 'vec', [((i + 2 * step) % vec_count, i) for i in rang...  27.8 us
    pallas_call x4, Pallas kernels, apply_field(): pl.pallas_call(functools.partial(field_kernel, second), out_shape=jax.Sha...  22.3 us
    ppermute x8, starting transfers between devices, from_row(): lax.ppermute(value, 'row', [((i + step) % row_count, i) for i in range(ro...  21.4 us
    pallas_call x1, Pallas kernels, finish(): pl.pallas_call(functools.partial(finish_kernel, total_rows), out_shape=ja...  20.8 us
    all_to_all x1, waiting for transfers between devices, on_device(): lax.all_to_all(part, ('row', 'vec'), split_axis=0, concat_axis=0, tiled=T...  17.4 us
    all_to_all x1, blocking collectives, on_device(): lax.all_to_all(share.reshape(row_count, strip, -1), 'row', split_axis=0,...  13.9 us
    ppermute x11, starting transfers between devices, swap(): return lax.ppermute(value, 'vec', [(i, i ^ 1) for i in range(vec_count)])  12.8 us
    unnamed x18, local copies, waits for them, and re-layouts  6.99 us
  transfers between devices with their start and end apart: 26, of which 11 were waited for; matrix products, arithmetic and copies ran while one was open for 1% of the time, Pallas kernels for 17%

profile of v8, /device:TPU:1, one launch (start us, length us, event | category | flops | bytes accessed | tf_op | source)
XLA Modules:
  0.0 180.0 jit_solution(10570385964765863457)
XLA Ops:
  0.0 1.2 copy-done
  1.2 0.5 pack.1
  1.8 2.1 %collective-permute-start = (f32[8,128,128]{2,1,0:T(8,128)S(1)}, f32[8,128,128]{2,1,0:T(8,128)S(1)}, u32[]{:S(2)}, u32[]{:S(2)}) collective-permute-start(f32[8,128,128]{2,1,0:T(8,128)S(1)} %get-tuple-element.9.own_ref.rest_0_), channel_id=1, source_target_pairs={{120,0},{0,8},{8,16},{16,24},{24,32},{32,40},{40,48},{48,56},{56,6... | collective-permute-start | bytes 1572872 | tf_op jit(solution)/shard_map/ppermute | solution.py:444
  3.9 4.8 %collective-permute-start.1 = (f32[8,128,128]{2,1,0:T(8,128)S(1)}, f32[8,128,128]{2,1,0:T(8,128)S(1)}, u32[]{:S(2)}, u32[]{:S(2)}) collective-permute-start(f32[8,128,128]{2,1,0:T(8,128)S(1)} %get-tuple-element.9.own_ref.rest_0_), channel_id=1, source_target_pairs={{8,0},{16,8},{24,16},{32,24},{40,32},{48,40},{56,48},{64,56},{72,6... | collective-permute-start | bytes 1572872 | tf_op jit(solution)/shard_map/ppermute | solution.py:444
  8.7 4.8 %collective-permute-start.5 = (f32[8,128,128]{2,1,0:T(8,128)S(1)}, f32[8,128,128]{2,1,0:T(8,128)S(1)}, u32[]{:S(2)}, u32[]{:S(2)}) collective-permute-start(f32[8,128,128]{2,1,0:T(8,128)S(1)} %get-tuple-element.10.own_ref.rest_0_), channel_id=1, source_target_pairs={{8,0},{16,8},{24,16},{32,24},{40,32},{48,40},{56,48},{64,56},{72,6... | collective-permute-start | bytes 1572872 | tf_op jit(solution)/shard_map/ppermute | solution.py:444
  14.8 0.8 fusion.2
  15.8 6.3 %split_blocks.1.h_ref = bf16[16,12,256,128]{3,2,1,0:T(8,128)(2,1)S(1)} custom-call(f32[16,12,128,128]{3,2,1,0:T(8,128)} %h_ref.1), custom_call_target="tpu_custom_call" | custom-call | bytes 25165824 | tf_op jit(solution)/shard_map/split_blocks/pallas_call | solution.py:65
  22.1 5.6 %field.4.own_ref = f32[8,128,128]{2,1,0:T(8,128)S(1)} custom-call(s32[192]{0:T(256)S(1)} %reshape.29.cols_ref, f32[2]{0:T(128)S(1)} %pad_maximum_fusion.coef_ref, bf16[16,12,256,128]{3,2,1,0:T(8,128)(2,1)S(1)} %split_blocks.1.h_ref, f32[8,128,128]{2,1,0:T(8,128)S(1)} %collective-permute-done.left_ref, f32[8,128,128]{2,1,0:T(8,128)S(1)} %get-tuple-element.9.own_ref.rest_0_, ...), custom_call_target="tpu_custom_call" | custom-call | flops 3221225472 | bytes 12582912 | tf_op jit(solution)/shard_map/field/pallas_call | solution.py:165
  27.7 4.8 %collective-permute-start.3 = (f32[8,128,128]{2,1,0:T(8,128)S(1)}, f32[8,128,128]{2,1,0:T(8,128)S(1)}, u32[]{:S(2)}, u32[]{:S(2)}) collective-permute-start(f32[8,128,128]{2,1,0:T(8,128)S(1)} %field.4.own_ref), channel_id=1, source_target_pairs={{8,0},{16,8},{24,16},{32,24},{40,32},{48,40},{56,48},{64,56},{72,6... | collective-permute-start | bytes 1572872 | tf_op jit(solution)/shard_map/ppermute | solution.py:444
  32.5 5.6 %field.6.own_ref = f32[8,128,128]{2,1,0:T(8,128)S(1)} custom-call(s32[192]{0:T(256)S(1)} %reshape.29.cols_ref, f32[2]{0:T(128)S(1)} %pad_maximum_fusion.coef_ref, bf16[16,12,256,128]{3,2,1,0:T(8,128)(2,1)S(1)} %split_blocks.1.h_ref, f32[8,128,128]{2,1,0:T(8,128)S(1)} %collective-permute-done.4.left_ref, ...), custom_call_target="tpu_custom_call" | custom-call | flops 3221225472 | bytes 12582912 | tf_op jit(solution)/shard_map/field/pallas_call | solution.py:165
  38.2 4.8 %collective-permute-start.7 = (f32[8,128,128]{2,1,0:T(8,128)S(1)}, f32[8,128,128]{2,1,0:T(8,128)S(1)}, u32[]{:S(2)}, u32[]{:S(2)}) collective-permute-start(f32[8,128,128]{2,1,0:T(8,128)S(1)} %field.6.own_ref), channel_id=1, source_target_pairs={{8,0},{16,8},{24,16},{32,24},{40,32},{48,40},{56,48},{64,56},{72,6... | collective-permute-start | bytes 1572872 | tf_op jit(solution)/shard_map/ppermute | solution.py:444
  43.0 5.6 %field.5 = f32[8,128,128]{2,1,0:T(8,128)S(1)} custom-call(s32[192]{0:T(256)S(1)} %reshape.29.cols_ref, f32[2]{0:T(128)S(1)} %pad_maximum_fusion.coef_ref, bf16[16,12,256,128]{3,2,1,0:T(8,128)(2,1)S(1)} %split_blocks.1.h_ref, f32[8,128,128]{2,1,0:T(8,128)S(1)} %collective-permute-done.2.left_ref, f32[8,128,128]{2,1,0:T(8,128)S(1)} %field.4.own_ref, ...), custom_call_target="tpu_custom_call" | custom-call | flops 3221225472 | bytes 12582912 | tf_op jit(solution)/shard_map/field/pallas_call | solution.py:165
  48.6 3.2 %collective-permute-start.8 = (f32[1024,128]{1,0:T(8,128)S(1)}, f32[1024,128]{1,0:T(8,128)S(1)}, u32[]{:S(2)}, u32[]{:S(2)}) collective-permute-start(f32[1024,128]{1,0:T(8,128)S(1)} %bitcast.6), channel_id=1, source_target_pairs={{0,1},{1,0},{2,3},{3,2},{4,5},{5,4},{6,7},{7,6},{8,9},{9,8},{10,11... | collective-permute-start | bytes 1572872 | tf_op jit(solution)/shard_map/ppermute | solution.py:457
  51.8 2.6 %collective-permute-done.6.left_ref = f32[8,128,128]{2,1,0:T(8,128)S(1)} collective-permute-done((f32[8,128,128]{2,1,0:T(8,128)S(1)}, f32[8,128,128]{2,1,0:T(8,128)S(1)}, u32[]{:S(2)}, u32[]{:S(2)}) %collective-permute-start.6) | collective-permute-done | bytes 524320 | tf_op jit(solution)/shard_map/ppermute | solution.py:444
  54.5 5.6 %field.7 = f32[8,128,128]{2,1,0:T(8,128)S(1)} custom-call(s32[192]{0:T(256)S(1)} %reshape.29.cols_ref, f32[2]{0:T(128)S(1)} %pad_maximum_fusion.coef_ref, bf16[16,12,256,128]{3,2,1,0:T(8,128)(2,1)S(1)} %split_blocks.1.h_ref, f32[8,128,128]{2,1,0:T(8,128)S(1)} %collective-permute-done.6.left_ref, f32[8,128,128]{2,1,0:T(8,128)S(1)} %field.6.own_ref, ...), custom_call_target="tpu_custom_call" | custom-call | flops 3221225472 | bytes 12582912 | tf_op jit(solution)/shard_map/field/pallas_call | solution.py:165
  60.1 2.4 %collective-permute-start.9 = (f32[1024,128]{1,0:T(8,128)S(1)}, f32[1024,128]{1,0:T(8,128)S(1)}, u32[]{:S(2)}, u32[]{:S(2)}) collective-permute-start(f32[1024,128]{1,0:T(8,128)S(1)} %bitcast.12), channel_id=1, source_target_pairs={{0,1},{1,0},{2,3},{3,2},{4,5},{5,4},{6,7},{7,6},{8,9},{9,8},{10,11... | collective-permute-start | bytes 1572872 | tf_op jit(solution)/shard_map/ppermute | solution.py:457
  62.5 2.7 %collective-permute-start.10 = (f32[1024,128]{1,0:T(8,128)S(1)}, f32[1024,128]{1,0:T(8,128)S(1)}, u32[]{:S(2)}, u32[]{:S(2)}) collective-permute-start(f32[1024,128]{1,0:T(8,128)S(1)} %bitcast.7), channel_id=1, source_target_pairs={{2,0},{3,1},{4,2},{5,3},{6,4},{7,5},{0,6},{1,7},{10,8},{11,9},{12,... | collective-permute-start | bytes 1572872 | tf_op jit(solution)/shard_map/ppermute | solution.py:447
  65.2 0.5 collective-permute-start.11
  65.7 1.0 collective-permute-start.12
  66.7 1.8 gram_near.1
  68.4 7.9 %collective-permute-done.10.rest_0_.rest_4_ = f32[1024,128]{1,0:T(8,128)S(1)} collective-permute-done((f32[1024,128]{1,0:T(8,128)S(1)}, f32[1024,128]{1,0:T(8,128)S(1)}, u32[]{:S(2)}, u32[]{:S(2)}) %collective-permute-start.10) | collective-permute-done | bytes 524320 | tf_op jit(solution)/shard_map/ppermute | solution.py:447
  76.4 11.2 %collective-permute-done.11.rest_1_.rest_5_ = f32[1024,128]{1,0:T(8,128)S(1)} collective-permute-done((f32[1024,128]{1,0:T(8,128)S(1)}, f32[1024,128]{1,0:T(8,128)S(1)}, u32[]{:S(2)}, u32[]{:S(2)}) %collective-permute-start.11) | collective-permute-done | bytes 524320 | tf_op jit(solution)/shard_map/ppermute | solution.py:447
  87.6 3.3 %collective-permute-done.13.rest_3_.rest_9_ = f32[1024,128]{1,0:T(8,128)S(1)} collective-permute-done((f32[1024,128]{1,0:T(8,128)S(1)}, f32[1024,128]{1,0:T(8,128)S(1)}, u32[]{:S(2)}, u32[]{:S(2)}) %collective-permute-start.13) | collective-permute-done | bytes 524320 | tf_op jit(solution)/shard_map/ppermute | solution.py:452
  90.9 2.0 %gram_far.1 = f32[128,640]{1,0:T(8,128)S(1)} custom-call(f32[128,256]{1,0:T(8,128)S(1)} %get-tuple-element.11.near_ref, bf16[4,256,1024]{2,1,0:T(8,128)(2,1)S(1)} %get-tuple-element.12.lhs_ref, f32[1024,128]{1,0:T(8,128)S(1)} %collective-permute-done.10.rest_0_.rest_4_, f32[1024,128]{1,0:T(8,128)S(1)} %collective-permute-done.11.rest_1_.rest_5_, ...), custom_call_target="tpu_custom_call" | custom-call | flops 805306368 | bytes 3145728 | tf_op jit(solution)/shard_map/gram_far/pallas_call | solution.py:264
  93.0 13.9 %all_to_all.10.parts_ref = f32[16,8,640]{2,1,0:T(8,128)S(1)} all-to-all(f32[16,8,640]{2,1,0:T(8,128)S(1)} %bitcast.18), channel_id=1, replica_groups=mesh['row'=16,'vec'=8] {'row'}, dimensions={0} | all-to-all | bytes 655360 | tf_op jit(solution)/shard_map/all_to_all | solution.py:487
  106.9 1.2 total.1
  108.1 5.8 %all-to-all-start.1 = ((f32[64,8,640]{2,1,0:T(8,128)}), f32[64,8,640]{2,1,0:T(8,128)S(1)}, u32[]{:S(2)}, u32[]{:S(2)}) async-start(f32[64,8,640]{2,1,0:T(8,128)} %total.1), calls=%async_computation.1 | async-start | bytes 2621440 | tf_op jit(solution)/shard_map/all_to_all | solution.py:496
  113.9 1.8 collective-permute-start.15
  115.8 17.4 %all-to-all-done.1 = f32[64,8,640]{2,1,0:T(8,128)S(1)} async-done(((f32[64,8,640]{2,1,0:T(8,128)}), f32[64,8,640]{2,1,0:T(8,128)S(1)}, u32[]{:S(2)}, u32[]{:S(2)}) %all-to-all-start.1) | async-done | bytes 1310752 | tf_op jit(solution)/shard_map/all_to_all | solution.py:496
  133.2 3.2 %collective-permute-start.14 = (f32[16,4,8,640]{3,2,1,0:T(8,128)S(1)}, f32[16,4,8,640]{3,2,1,0:T(8,128)}, u32[]{:S(2)}, u32[]{:S(2)}) collective-permute-start(f32[16,4,8,640]{3,2,1,0:T(8,128)S(1)} %bitcast.19), channel_id=1, source_target_pairs={{0,1},{1,0},{2,3},{3,2},{4,5},{5,4},{6,7},{7,6},{8,9},{9,8},{10,11... | collective-permute-start | bytes 3932168 | tf_op jit(solution)/shard_map/ppermute | solution.py:457
  136.3 0.5 collective-permute-start.18
  136.8 0.4 collective-permute-start.21
  137.2 1.1 collective-permute-start.22
  138.3 1.4 collective-permute-done.17.rest_6_
  139.7 0.8 copy-done.5
  140.5 0.4 collective-permute-start.19
  140.9 0.8 copy-done.7
  141.8 8.6 %collective-permute-done.21.rest_12_ = f32[1024,128]{1,0:T(8,128)} collective-permute-done((f32[1024,128]{1,0:T(8,128)S(1)}, f32[1024,128]{1,0:T(8,128)}, u32[]{:S(2)}, u32[]{:S(2)}) %collective-permute-start.21) | collective-permute-done | bytes 524320 | tf_op jit(solution)/shard_map/ppermute | solution.py:447
  150.4 0.9 collective-permute-start.23
  151.3 1.3 collective-permute-done.22.rest_13_
  152.6 0.3 collective-permute-start.24
  152.9 0.3 collective-permute-done.23.rest_14_
  153.2 1.7 collective-permute-done.24.rest_15_
  154.8 1.0 copy-done.2
  155.9 1.0 copy-done.4
  156.9 1.0 copy-done.6
  158.0 1.0 copy-done.8
  159.0 20.8 %finish.1 = f32[2048,128]{1,0:T(8,128)} custom-call(s32[1]{0:T(128)} %bitcast.y_ref, f32[16,4,8,640]{3,2,1,0:T(8,128)S(1)} %bitcast.20, f32[16,4,8,640]{3,2,1,0:T(8,128)} %collective-permute-done.14.gb_ref, f32[1024,128]{1,0:T(8,128)S(1)} %bitcast.11, f32[1024,128]{1,0:T(8,128)S(1)} %bitcast.17, f32[1024,128]{1,0:T(8,128)} %collective-permute-done.15.rest_2_, ...), custom_call_target="tpu_custom_call" | custom-call | flops 9663676416 | bytes 9437184 | tf_op jit(solution)/shard_map/finish/pallas_call | solution.py:409
  (36 shorter events, 0.7 us)
Async XLA Ops:
  0.0 1.2 copy-start
  1.8 20.3 %collective-permute-start = (f32[8,128,128]{2,1,0:T(8,128)S(1)}, f32[8,128,128]{2,1,0:T(8,128)S(1)}, u32[]{:S(2)}, u32[]{:S(2)}) collective-permute-start(f32[8,128,128]{2,1,0:T(8,128)S(1)} %get-tuple-element.9.own_ref.rest_0_), channel_id=1, source_target_pairs={{120,0},{0,8},{8,16},{16,24},{24,32},{32,40},{40,48},{48,56},{56,6... | collective-permute-start | bytes 1572872 | tf_op jit(solution)/shard_map/ppermute | solution.py:444
  3.9 18.2 %collective-permute-start.1 = (f32[8,128,128]{2,1,0:T(8,128)S(1)}, f32[8,128,128]{2,1,0:T(8,128)S(1)}, u32[]{:S(2)}, u32[]{:S(2)}) collective-permute-start(f32[8,128,128]{2,1,0:T(8,128)S(1)} %get-tuple-element.9.own_ref.rest_0_), channel_id=1, source_target_pairs={{8,0},{16,8},{24,16},{32,24},{40,32},{48,40},{56,48},{64,56},{72,6... | collective-permute-start | bytes 1572872 | tf_op jit(solution)/shard_map/ppermute | solution.py:444
  8.7 23.8 %collective-permute-start.4 = (f32[8,128,128]{2,1,0:T(8,128)S(1)}, f32[8,128,128]{2,1,0:T(8,128)S(1)}, u32[]{:S(2)}, u32[]{:S(2)}) collective-permute-start(f32[8,128,128]{2,1,0:T(8,128)S(1)} %get-tuple-element.10.own_ref.rest_0_), channel_id=1, source_target_pairs={{120,0},{0,8},{8,16},{16,24},{24,32},{32,40},{40,48},{48,56},{56,6... | collective-permute-start | bytes 1572872 | tf_op jit(solution)/shard_map/ppermute | solution.py:444
  8.7 23.8 %collective-permute-start.5 = (f32[8,128,128]{2,1,0:T(8,128)S(1)}, f32[8,128,128]{2,1,0:T(8,128)S(1)}, u32[]{:S(2)}, u32[]{:S(2)}) collective-permute-start(f32[8,128,128]{2,1,0:T(8,128)S(1)} %get-tuple-element.10.own_ref.rest_0_), channel_id=1, source_target_pairs={{8,0},{16,8},{24,16},{32,24},{40,32},{48,40},{56,48},{64,56},{72,6... | collective-permute-start | bytes 1572872 | tf_op jit(solution)/shard_map/ppermute | solution.py:444
  27.6 15.4 %collective-permute-start.2 = (f32[8,128,128]{2,1,0:T(8,128)S(1)}, f32[8,128,128]{2,1,0:T(8,128)S(1)}, u32[]{:S(2)}, u32[]{:S(2)}) collective-permute-start(f32[8,128,128]{2,1,0:T(8,128)S(1)} %field.4.own_ref), channel_id=1, source_target_pairs={{120,0},{0,8},{8,16},{16,24},{24,32},{32,40},{40,48},{48,56},{56,6... | collective-permute-start | bytes 1572872 | tf_op jit(solution)/shard_map/ppermute | solution.py:444
  27.7 15.3 %collective-permute-start.3 = (f32[8,128,128]{2,1,0:T(8,128)S(1)}, f32[8,128,128]{2,1,0:T(8,128)S(1)}, u32[]{:S(2)}, u32[]{:S(2)}) collective-permute-start(f32[8,128,128]{2,1,0:T(8,128)S(1)} %field.4.own_ref), channel_id=1, source_target_pairs={{8,0},{16,8},{24,16},{32,24},{40,32},{48,40},{56,48},{64,56},{72,6... | collective-permute-start | bytes 1572872 | tf_op jit(solution)/shard_map/ppermute | solution.py:444
  38.1 16.4 %collective-permute-start.6 = (f32[8,128,128]{2,1,0:T(8,128)S(1)}, f32[8,128,128]{2,1,0:T(8,128)S(1)}, u32[]{:S(2)}, u32[]{:S(2)}) collective-permute-start(f32[8,128,128]{2,1,0:T(8,128)S(1)} %field.6.own_ref), channel_id=1, source_target_pairs={{120,0},{0,8},{8,16},{16,24},{24,32},{32,40},{40,48},{48,56},{56,6... | collective-permute-start | bytes 1572872 | tf_op jit(solution)/shard_map/ppermute | solution.py:444
  38.2 16.3 %collective-permute-start.7 = (f32[8,128,128]{2,1,0:T(8,128)S(1)}, f32[8,128,128]{2,1,0:T(8,128)S(1)}, u32[]{:S(2)}, u32[]{:S(2)}) collective-permute-start(f32[8,128,128]{2,1,0:T(8,128)S(1)} %field.6.own_ref), channel_id=1, source_target_pairs={{8,0},{16,8},{24,16},{32,24},{40,32},{48,40},{56,48},{64,56},{72,6... | collective-permute-start | bytes 1572872 | tf_op jit(solution)/shard_map/ppermute | solution.py:444
  48.6 18.1 %collective-permute-start.8 = (f32[1024,128]{1,0:T(8,128)S(1)}, f32[1024,128]{1,0:T(8,128)S(1)}, u32[]{:S(2)}, u32[]{:S(2)}) collective-permute-start(f32[1024,128]{1,0:T(8,128)S(1)} %bitcast.6), channel_id=1, source_target_pairs={{0,1},{1,0},{2,3},{3,2},{4,5},{5,4},{6,7},{7,6},{8,9},{9,8},{10,11... | collective-permute-start | bytes 1572872 | tf_op jit(solution)/shard_map/ppermute | solution.py:457
  60.1 6.6 %collective-permute-start.9 = (f32[1024,128]{1,0:T(8,128)S(1)}, f32[1024,128]{1,0:T(8,128)S(1)}, u32[]{:S(2)}, u32[]{:S(2)}) collective-permute-start(f32[1024,128]{1,0:T(8,128)S(1)} %bitcast.12), channel_id=1, source_target_pairs={{0,1},{1,0},{2,3},{3,2},{4,5},{5,4},{6,7},{7,6},{8,9},{9,8},{10,11... | collective-permute-start | bytes 1572872 | tf_op jit(solution)/shard_map/ppermute | solution.py:457
  62.5 13.9 %collective-permute-start.10 = (f32[1024,128]{1,0:T(8,128)S(1)}, f32[1024,128]{1,0:T(8,128)S(1)}, u32[]{:S(2)}, u32[]{:S(2)}) collective-permute-start(f32[1024,128]{1,0:T(8,128)S(1)} %bitcast.7), channel_id=1, source_target_pairs={{2,0},{3,1},{4,2},{5,3},{6,4},{7,5},{0,6},{1,7},{10,8},{11,9},{12,... | collective-permute-start | bytes 1572872 | tf_op jit(solution)/shard_map/ppermute | solution.py:447
  65.2 22.4 %collective-permute-start.11 = (f32[1024,128]{1,0:T(8,128)S(1)}, f32[1024,128]{1,0:T(8,128)S(1)}, u32[]{:S(2)}, u32[]{:S(2)}) collective-permute-start(f32[1024,128]{1,0:T(8,128)S(1)} %bitcast.13), channel_id=1, source_target_pairs={{2,0},{3,1},{4,2},{5,3},{6,4},{7,5},{0,6},{1,7},{10,8},{11,9},{12,... | collective-permute-start | bytes 1572872 | tf_op jit(solution)/shard_map/ppermute | solution.py:447
  65.7 22.0 %collective-permute-start.12 = (f32[1024,128]{1,0:T(8,128)S(1)}, f32[1024,128]{1,0:T(8,128)S(1)}, u32[]{:S(2)}, u32[]{:S(2)}) collective-permute-start(f32[1024,128]{1,0:T(8,128)S(1)} %bitcast.8), channel_id=1, source_target_pairs={{6,0},{7,1},{0,2},{1,3},{3,4},{2,5},{5,6},{4,7},{14,8},{15,9},{8,1... | collective-permute-start | bytes 1572872 | tf_op jit(solution)/shard_map/ppermute | solution.py:452
  66.7 24.3 %collective-permute-start.13 = (f32[1024,128]{1,0:T(8,128)S(1)}, f32[1024,128]{1,0:T(8,128)S(1)}, u32[]{:S(2)}, u32[]{:S(2)}) collective-permute-start(f32[1024,128]{1,0:T(8,128)S(1)} %bitcast.14), channel_id=1, source_target_pairs={{6,0},{7,1},{0,2},{1,3},{3,4},{2,5},{5,6},{4,7},{14,8},{15,9},{8,1... | collective-permute-start | bytes 1572872 | tf_op jit(solution)/shard_map/ppermute | solution.py:452
  87.6 5.3 %copy-start.1 = (f32[1024,128]{1,0:T(8,128)}, f32[1024,128]{1,0:T(8,128)S(1)}, u32[]{:S(2)}) copy-start(f32[1024,128]{1,0:T(8,128)S(1)} %collective-permute-done.12.rest_2_.rest_8_) | copy-start | bytes 1572868
  90.9 2.0 %copy-start.3 = (f32[1024,128]{1,0:T(8,128)}, f32[1024,128]{1,0:T(8,128)S(1)}, u32[]{:S(2)}) copy-start(f32[1024,128]{1,0:T(8,128)S(1)} %collective-permute-done.13.rest_3_.rest_9_) | copy-start | bytes 1572868
  108.1 25.1 %all-to-all-start.1 = ((f32[64,8,640]{2,1,0:T(8,128)}), f32[64,8,640]{2,1,0:T(8,128)S(1)}, u32[]{:S(2)}, u32[]{:S(2)}) async-start(f32[64,8,640]{2,1,0:T(8,128)} %total.1), calls=%async_computation.1 | async-start | bytes 2621440 | tf_op jit(solution)/shard_map/all_to_all | solution.py:496
  113.9 22.9 %collective-permute-start.15 = (f32[1024,128]{1,0:T(8,128)S(1)}, f32[1024,128]{1,0:T(8,128)}, u32[]{:S(2)}, u32[]{:S(2)}) collective-permute-start(f32[1024,128]{1,0:T(8,128)S(1)} %bitcast.10), channel_id=1, source_target_pairs={{0,1},{1,0},{2,3},{3,2},{4,5},{5,4},{6,7},{7,6},{8,9},{9,8},{10,11... | collective-permute-start | bytes 1572872 | tf_op jit(solution)/shard_map/ppermute | solution.py:457
  115.7 21.5 %collective-permute-start.16 = (f32[1024,128]{1,0:T(8,128)S(1)}, f32[1024,128]{1,0:T(8,128)}, u32[]{:S(2)}, u32[]{:S(2)}) collective-permute-start(f32[1024,128]{1,0:T(8,128)S(1)} %bitcast.16), channel_id=1, source_target_pairs={{0,1},{1,0},{2,3},{3,2},{4,5},{5,4},{6,7},{7,6},{8,9},{9,8},{10,11... | collective-permute-start | bytes 1572872 | tf_op jit(solution)/shard_map/ppermute | solution.py:457
  133.2 21.7 %collective-permute-start.14 = (f32[16,4,8,640]{3,2,1,0:T(8,128)S(1)}, f32[16,4,8,640]{3,2,1,0:T(8,128)}, u32[]{:S(2)}, u32[]{:S(2)}) collective-permute-start(f32[16,4,8,640]{3,2,1,0:T(8,128)S(1)} %bitcast.19), channel_id=1, source_target_pairs={{0,1},{1,0},{2,3},{3,2},{4,5},{5,4},{6,7},{7,6},{8,9},{9,8},{10,11... | collective-permute-start | bytes 3932168 | tf_op jit(solution)/shard_map/ppermute | solution.py:457
  136.3 3.4 %collective-permute-start.17 = (f32[1024,128]{1,0:T(8,128)S(1)}, f32[1024,128]{1,0:T(8,128)S(1)}, u32[]{:S(2)}, u32[]{:S(2)}) collective-permute-start(f32[1024,128]{1,0:T(8,128)S(1)} %collective-permute-done.10.rest_0_.rest_4_), channel_id=1, source_target_pairs={{0,1},{1,0},{2,3},{3,2},{4,5},{5,4},{6,7},{7,6},{8,9},{9,8},{10,11... | collective-permute-start | bytes 1572872 | tf_op jit(solution)/shard_map/ppermute | solution.py:457
  136.3 4.6 %collective-permute-start.18 = (f32[1024,128]{1,0:T(8,128)S(1)}, f32[1024,128]{1,0:T(8,128)S(1)}, u32[]{:S(2)}, u32[]{:S(2)}) collective-permute-start(f32[1024,128]{1,0:T(8,128)S(1)} %collective-permute-done.11.rest_1_.rest_5_), channel_id=1, source_target_pairs={{0,1},{1,0},{2,3},{3,2},{4,5},{5,4},{6,7},{7,6},{8,9},{9,8},{10,11... | collective-permute-start | bytes 1572872 | tf_op jit(solution)/shard_map/ppermute | solution.py:457
  136.8 13.6 %collective-permute-start.21 = (f32[1024,128]{1,0:T(8,128)S(1)}, f32[1024,128]{1,0:T(8,128)}, u32[]{:S(2)}, u32[]{:S(2)}) collective-permute-start(f32[1024,128]{1,0:T(8,128)S(1)} %collective-permute-done.10.rest_0_.rest_4_), channel_id=1, source_target_pairs={{2,0},{3,1},{4,2},{5,3},{6,4},{7,5},{0,6},{1,7},{10,8},{11,9},{12,... | collective-permute-start | bytes 1572872 | tf_op jit(solution)/shard_map/ppermute | solution.py:447
  137.2 15.3 %collective-permute-start.22 = (f32[1024,128]{1,0:T(8,128)}, f32[1024,128]{1,0:T(8,128)}, u32[]{:S(2)}, u32[]{:S(2)}) collective-permute-start(f32[1024,128]{1,0:T(8,128)} %copy-done.3), channel_id=1, source_target_pairs={{7,0},{6,1},{0,2},{1,3},{2,4},{3,5},{5,6},{4,7},{15,8},{14,9},{8,1... | collective-permute-start | bytes 1572872 | tf_op jit(solution)/shard_map/ppermute | solution.py:461
  139.7 0.8 copy-start.5
  140.5 12.3 %collective-permute-start.19 = (f32[1024,128]{1,0:T(8,128)}, f32[1024,128]{1,0:T(8,128)}, u32[]{:S(2)}, u32[]{:S(2)}) collective-permute-start(f32[1024,128]{1,0:T(8,128)} %copy-done.1), channel_id=1, source_target_pairs={{0,1},{1,0},{2,3},{3,2},{4,5},{5,4},{6,7},{7,6},{8,9},{9,8},{10,11... | collective-permute-start | bytes 1572872 | tf_op jit(solution)/shard_map/ppermute | solution.py:457
  140.9 0.8 copy-start.7
  141.7 11.2 %collective-permute-start.20 = (f32[1024,128]{1,0:T(8,128)}, f32[1024,128]{1,0:T(8,128)}, u32[]{:S(2)}, u32[]{:S(2)}) collective-permute-start(f32[1024,128]{1,0:T(8,128)} %copy-done.3), channel_id=1, source_target_pairs={{0,1},{1,0},{2,3},{3,2},{4,5},{5,4},{6,7},{7,6},{8,9},{9,8},{10,11... | collective-permute-start | bytes 1572872 | tf_op jit(solution)/shard_map/ppermute | solution.py:457
  150.4 2.7 %collective-permute-start.23 = (f32[1024,128]{1,0:T(8,128)}, f32[1024,128]{1,0:T(8,128)}, u32[]{:S(2)}, u32[]{:S(2)}) collective-permute-start(f32[1024,128]{1,0:T(8,128)} %collective-permute-done.21.rest_12_), channel_id=1, source_target_pairs={{0,1},{1,0},{2,3},{3,2},{4,5},{5,4},{6,7},{7,6},{8,9},{9,8},{10,11... | collective-permute-start | bytes 1572872 | tf_op jit(solution)/shard_map/ppermute | solution.py:457
  152.6 2.3 %collective-permute-start.24 = (f32[1024,128]{1,0:T(8,128)}, f32[1024,128]{1,0:T(8,128)}, u32[]{:S(2)}, u32[]{:S(2)}) collective-permute-start(f32[1024,128]{1,0:T(8,128)} %collective-permute-done.22.rest_13_), channel_id=1, source_target_pairs={{0,1},{1,0},{2,3},{3,2},{4,5},{5,4},{6,7},{7,6},{8,9},{9,8},{10,11... | collective-permute-start | bytes 1572872 | tf_op jit(solution)/shard_map/ppermute | solution.py:457
  154.8 1.0 copy-start.2
  155.9 1.0 copy-start.4
  156.9 1.0 copy-start.6
  158.0 1.0 copy-start.8

commit v9 on v8

--- a/solution.py
+++ b/solution.py
@@ -306,10 +306,14 @@
 
 def finish_kernel(total_rows, y_ref, ga_ref, gb_ref, *rest):
     sources = rest[: 2 * len(PIECES)]
-    out_ref, gram, gram_low, state, factor, ordered, held, arrived = rest[2 * len(PIECES) :]
+    out_ref, gram, gram_low, state, factor, ordered, held, arrived, other, other_in = rest[
+        2 * len(PIECES) :
+    ]
+    other_copy = pltpu.make_async_copy(gb_ref, other, other_in)
+    other_copy.start()
     copies, held_refs = fetched(sources, held, arrived)
     x_refs = [held_refs[2 * n : 2 * n + 2] for n in range(len(PIECES))]
-    grams = (ga_ref, gb_ref)
+    grams = (ga_ref, other)
     y = y_ref[0]
 
     diagonal = lax.broadcasted_iota(jnp.int32, (128, 128), 0) == lax.broadcasted_iota(
@@ -318,13 +322,6 @@
 
     def block(k, row, b):
         return grams[k][:, row, :, b * 128 : (b + 1) * 128].reshape(128, 128)
-
-    trace = jnp.zeros((128, 128), F32)
-    for k in range(2):
-        for row in range(4):
-            trace += jnp.where(diagonal, block(k, row, 0), 0.0)
-    energy = jnp.sum(jnp.sum(trace, axis=0, keepdims=True), axis=1, keepdims=True)
-    square = NV / (4 * (energy + 1e-06))
 
     def put(at_row, at_col, value):
         high, low = split(value)
@@ -332,26 +329,34 @@
         gram[rows, cols] = high
         gram_low[rows, cols] = low
 
+    trace = jnp.zeros((128, 128), F32)
     for k in range(2):
+        if k:
+            other_copy.wait()
         for row in range(4):
             here = 4 * k + row
             after, before = (row + 1) % 4, (row + 3) % 4
             side = k if row < 2 else 1 - k
-            put(here, here, block(k, row, 0) * square)
-            put(here, 4 * (1 - k) + row, block(k, row, 1) * square)
+            own = block(k, row, 0)
+            trace += jnp.where(diagonal, own, 0.0)
+            put(here, here, own)
+            put(here, 4 * (1 - k) + row, block(k, row, 1))
             for one, two, b in (
                 (here, 4 * k + after, 2),
                 (4 * (1 - k) + row, 4 * k + after, 3),
                 (4 * side + before, 4 * k + after, 4),
             ):
-                value = block(k, row, b) * square
+                value = block(k, row, b)
                 put(one, two, value)
                 put(two, one, value.T)
+    energy = jnp.sum(jnp.sum(trace, axis=0, keepdims=True), axis=1, keepdims=True)
+    square = NV / (4 * (energy + 1e-06))
+    half_square = 0.5 * square
 
     mine = pl.ds(pl.multiple_of(y * 128, 128), 128)
     column = lax.broadcasted_iota(jnp.int32, (128, NV), 1) - y * 128
     unit = (column == lax.broadcasted_iota(jnp.int32, (128, NV), 0)).astype(F32)
-    state[0] = 1.5 * unit - 0.5 * (gram[mine, :].astype(F32) + gram_low[mine, :].astype(F32))
+    state[0] = 1.5 * unit - half_square * (gram[mine, :].astype(F32) + gram_low[mine, :].astype(F32))
 
     @pl.loop(0, 12)
     def _(step):
@@ -365,10 +370,10 @@
         slot = jnp.int32(0)
         for at, value in BASE.items():
             slot = jnp.where(step == at, value, slot)
-        high, low = split(current)
+        high, low = split(current * half_square)
         twice = mm(jnp.concatenate([high, low], axis=0), gram[...])
         product = (twice[:128] + twice[128:]) + mm(high, gram_low[...])
-        state[0] = 1.5 * state[slot] - 0.5 * product
+        state[0] = 1.5 * state[slot] - product
 
     scale = jnp.sqrt(square) * math.sqrt(total_rows)
     high, low = split(state[0].T * scale)
@@ -409,8 +414,8 @@
     return pl.pallas_call(
         functools.partial(finish_kernel, total_rows),
         out_shape=jax.ShapeDtypeStruct((rows, cols), F32),
-        in_specs=[SMEM_SPEC, VMEM_SPEC, VMEM_SPEC]
-        + [pl.BlockSpec(memory_space=pltpu.HBM)] * len(operands),
+        in_specs=[SMEM_SPEC, VMEM_SPEC]
+        + [pl.BlockSpec(memory_space=pl.ANY)] * (1 + len(operands)),
         out_specs=VMEM_SPEC,
         scratch_shapes=[
             pltpu.VMEM((NV, NV), BF),
@@ -420,6 +425,8 @@
             pltpu.VMEM((NV, 2 * cols), BF),
             pltpu.VMEM((len(operands), rows // 2, cols), F32),
             pltpu.SemaphoreType.DMA((len(operands),)),
+            pltpu.VMEM(gram_b.shape, F32),
+            pltpu.SemaphoreType.DMA(()),
         ],
         compiler_params=pltpu.CompilerParams(vmem_limit_bytes=40 * 2**20),
         cost_estimate=cost(12 * 6 * cols * NV * NV, 4 * rows * cols * 9),

time: 181 us -> 180 us (level)
  no operation moved by 1% of the time
where the time goes in v9:
time: 180 us; the launch traced here: 179 us
  waiting for transfers between devices  55.9 us (31%)
  Pallas kernels  54.1 us (30%)
  starting transfers between devices  45.7 us (25%)
  blocking collectives  13.9 us (8%)
  local copies, waits for them, and re-layouts  7.07 us (4%)
    ppermute x3, waiting for transfers between devices, from_y(): lax.ppermute(value, 'vec', [((i + 2 * step) % vec_count, i) for i in rang...  27.8 us
    pallas_call x4, Pallas kernels, apply_field(): pl.pallas_call(functools.partial(field_kernel, second), out_shape=jax.Sha...  22.3 us
    ppermute x8, starting transfers between devices, from_row(): lax.ppermute(value, 'row', [((i + step) % row_count, i) for i in range(ro...  21.4 us
    pallas_call x1, Pallas kernels, finish(): pl.pallas_call(functools.partial(finish_kernel, total_rows), out_shape=ja...  20.1 us
    all_to_all x1, waiting for transfers between devices, on_device(): lax.all_to_all(part, ('row', 'vec'), split_axis=0, concat_axis=0, tiled=T...  17.4 us
    all_to_all x1, blocking collectives, on_device(): lax.all_to_all(share.reshape(row_count, strip, -1), 'row', split_axis=0,...  13.9 us
    ppermute x11, starting transfers between devices, swap(): return lax.ppermute(value, 'vec', [(i, i ^ 1) for i in range(vec_count)])  12.8 us
    unnamed x18, local copies, waits for them, and re-layouts  6.99 us
  transfers between devices with their start and end apart: 26, of which 11 were waited for; matrix products, arithmetic and copies ran while one was open for 1% of the time, Pallas kernels for 17%

profile of v9, /device:TPU:1, one launch (start us, length us, event | category | flops | bytes accessed | tf_op | source)
XLA Modules:
  0.0 179.3 jit_solution(4591625829657848233)
XLA Ops:
  0.0 1.2 copy-done
  1.2 0.5 pack.1
  1.8 2.1 %collective-permute-start = (f32[8,128,128]{2,1,0:T(8,128)S(1)}, f32[8,128,128]{2,1,0:T(8,128)S(1)}, u32[]{:S(2)}, u32[]{:S(2)}) collective-permute-start(f32[8,128,128]{2,1,0:T(8,128)S(1)} %get-tuple-element.9.own_ref.rest_0_), channel_id=1, source_target_pairs={{120,0},{0,8},{8,16},{16,24},{24,32},{32,40},{40,48},{48,56},{56,6... | collective-permute-start | bytes 1572872 | tf_op jit(solution)/shard_map/ppermute | solution.py:451
  3.9 4.8 %collective-permute-start.1 = (f32[8,128,128]{2,1,0:T(8,128)S(1)}, f32[8,128,128]{2,1,0:T(8,128)S(1)}, u32[]{:S(2)}, u32[]{:S(2)}) collective-permute-start(f32[8,128,128]{2,1,0:T(8,128)S(1)} %get-tuple-element.9.own_ref.rest_0_), channel_id=1, source_target_pairs={{8,0},{16,8},{24,16},{32,24},{40,32},{48,40},{56,48},{64,56},{72,6... | collective-permute-start | bytes 1572872 | tf_op jit(solution)/shard_map/ppermute | solution.py:451
  8.7 4.8 %collective-permute-start.5 = (f32[8,128,128]{2,1,0:T(8,128)S(1)}, f32[8,128,128]{2,1,0:T(8,128)S(1)}, u32[]{:S(2)}, u32[]{:S(2)}) collective-permute-start(f32[8,128,128]{2,1,0:T(8,128)S(1)} %get-tuple-element.10.own_ref.rest_0_), channel_id=1, source_target_pairs={{8,0},{16,8},{24,16},{32,24},{40,32},{48,40},{56,48},{64,56},{72,6... | collective-permute-start | bytes 1572872 | tf_op jit(solution)/shard_map/ppermute | solution.py:451
  14.8 0.8 fusion.2
  15.8 6.3 %split_blocks.1.h_ref = bf16[16,12,256,128]{3,2,1,0:T(8,128)(2,1)S(1)} custom-call(f32[16,12,128,128]{3,2,1,0:T(8,128)} %h_ref.1), custom_call_target="tpu_custom_call" | custom-call | bytes 25165824 | tf_op jit(solution)/shard_map/split_blocks/pallas_call | solution.py:65
  22.1 5.6 %field.4.own_ref = f32[8,128,128]{2,1,0:T(8,128)S(1)} custom-call(s32[192]{0:T(256)S(1)} %reshape.29.cols_ref, f32[2]{0:T(128)S(1)} %pad_maximum_fusion.coef_ref, bf16[16,12,256,128]{3,2,1,0:T(8,128)(2,1)S(1)} %split_blocks.1.h_ref, f32[8,128,128]{2,1,0:T(8,128)S(1)} %collective-permute-done.left_ref, f32[8,128,128]{2,1,0:T(8,128)S(1)} %get-tuple-element.9.own_ref.rest_0_, ...), custom_call_target="tpu_custom_call" | custom-call | flops 3221225472 | bytes 12582912 | tf_op jit(solution)/shard_map/field/pallas_call | solution.py:165
  27.7 4.8 %collective-permute-start.3 = (f32[8,128,128]{2,1,0:T(8,128)S(1)}, f32[8,128,128]{2,1,0:T(8,128)S(1)}, u32[]{:S(2)}, u32[]{:S(2)}) collective-permute-start(f32[8,128,128]{2,1,0:T(8,128)S(1)} %field.4.own_ref), channel_id=1, source_target_pairs={{8,0},{16,8},{24,16},{32,24},{40,32},{48,40},{56,48},{64,56},{72,6... | collective-permute-start | bytes 1572872 | tf_op jit(solution)/shard_map/ppermute | solution.py:451
  32.5 5.6 %field.6.own_ref = f32[8,128,128]{2,1,0:T(8,128)S(1)} custom-call(s32[192]{0:T(256)S(1)} %reshape.29.cols_ref, f32[2]{0:T(128)S(1)} %pad_maximum_fusion.coef_ref, bf16[16,12,256,128]{3,2,1,0:T(8,128)(2,1)S(1)} %split_blocks.1.h_ref, f32[8,128,128]{2,1,0:T(8,128)S(1)} %collective-permute-done.4.left_ref, ...), custom_call_target="tpu_custom_call" | custom-call | flops 3221225472 | bytes 12582912 | tf_op jit(solution)/shard_map/field/pallas_call | solution.py:165
  38.2 4.8 %collective-permute-start.7 = (f32[8,128,128]{2,1,0:T(8,128)S(1)}, f32[8,128,128]{2,1,0:T(8,128)S(1)}, u32[]{:S(2)}, u32[]{:S(2)}) collective-permute-start(f32[8,128,128]{2,1,0:T(8,128)S(1)} %field.6.own_ref), channel_id=1, source_target_pairs={{8,0},{16,8},{24,16},{32,24},{40,32},{48,40},{56,48},{64,56},{72,6... | collective-permute-start | bytes 1572872 | tf_op jit(solution)/shard_map/ppermute | solution.py:451
  43.0 5.6 %field.5 = f32[8,128,128]{2,1,0:T(8,128)S(1)} custom-call(s32[192]{0:T(256)S(1)} %reshape.29.cols_ref, f32[2]{0:T(128)S(1)} %pad_maximum_fusion.coef_ref, bf16[16,12,256,128]{3,2,1,0:T(8,128)(2,1)S(1)} %split_blocks.1.h_ref, f32[8,128,128]{2,1,0:T(8,128)S(1)} %collective-permute-done.2.left_ref, f32[8,128,128]{2,1,0:T(8,128)S(1)} %field.4.own_ref, ...), custom_call_target="tpu_custom_call" | custom-call | flops 3221225472 | bytes 12582912 | tf_op jit(solution)/shard_map/field/pallas_call | solution.py:165
  48.6 3.2 %collective-permute-start.8 = (f32[1024,128]{1,0:T(8,128)S(1)}, f32[1024,128]{1,0:T(8,128)S(1)}, u32[]{:S(2)}, u32[]{:S(2)}) collective-permute-start(f32[1024,128]{1,0:T(8,128)S(1)} %bitcast.6), channel_id=1, source_target_pairs={{0,1},{1,0},{2,3},{3,2},{4,5},{5,4},{6,7},{7,6},{8,9},{9,8},{10,11... | collective-permute-start | bytes 1572872 | tf_op jit(solution)/shard_map/ppermute | solution.py:464
  51.8 2.6 %collective-permute-done.6.left_ref = f32[8,128,128]{2,1,0:T(8,128)S(1)} collective-permute-done((f32[8,128,128]{2,1,0:T(8,128)S(1)}, f32[8,128,128]{2,1,0:T(8,128)S(1)}, u32[]{:S(2)}, u32[]{:S(2)}) %collective-permute-start.6) | collective-permute-done | bytes 524320 | tf_op jit(solution)/shard_map/ppermute | solution.py:451
  54.5 5.6 %field.7 = f32[8,128,128]{2,1,0:T(8,128)S(1)} custom-call(s32[192]{0:T(256)S(1)} %reshape.29.cols_ref, f32[2]{0:T(128)S(1)} %pad_maximum_fusion.coef_ref, bf16[16,12,256,128]{3,2,1,0:T(8,128)(2,1)S(1)} %split_blocks.1.h_ref, f32[8,128,128]{2,1,0:T(8,128)S(1)} %collective-permute-done.6.left_ref, f32[8,128,128]{2,1,0:T(8,128)S(1)} %field.6.own_ref, ...), custom_call_target="tpu_custom_call" | custom-call | flops 3221225472 | bytes 12582912 | tf_op jit(solution)/shard_map/field/pallas_call | solution.py:165
  60.1 2.4 %collective-permute-start.9 = (f32[1024,128]{1,0:T(8,128)S(1)}, f32[1024,128]{1,0:T(8,128)S(1)}, u32[]{:S(2)}, u32[]{:S(2)}) collective-permute-start(f32[1024,128]{1,0:T(8,128)S(1)} %bitcast.12), channel_id=1, source_target_pairs={{0,1},{1,0},{2,3},{3,2},{4,5},{5,4},{6,7},{7,6},{8,9},{9,8},{10,11... | collective-permute-start | bytes 1572872 | tf_op jit(solution)/shard_map/ppermute | solution.py:464
  62.5 2.7 %collective-permute-start.10 = (f32[1024,128]{1,0:T(8,128)S(1)}, f32[1024,128]{1,0:T(8,128)S(1)}, u32[]{:S(2)}, u32[]{:S(2)}) collective-permute-start(f32[1024,128]{1,0:T(8,128)S(1)} %bitcast.7), channel_id=1, source_target_pairs={{2,0},{3,1},{4,2},{5,3},{6,4},{7,5},{0,6},{1,7},{10,8},{11,9},{12,... | collective-permute-start | bytes 1572872 | tf_op jit(solution)/shard_map/ppermute | solution.py:454
  65.2 0.5 collective-permute-start.11
  65.7 1.0 collective-permute-start.12
  66.7 1.8 gram_near.1
  68.4 7.9 %collective-permute-done.10.rest_0_.rest_4_ = f32[1024,128]{1,0:T(8,128)S(1)} collective-permute-done((f32[1024,128]{1,0:T(8,128)S(1)}, f32[1024,128]{1,0:T(8,128)S(1)}, u32[]{:S(2)}, u32[]{:S(2)}) %collective-permute-start.10) | collective-permute-done | bytes 524320 | tf_op jit(solution)/shard_map/ppermute | solution.py:454
  76.4 11.2 %collective-permute-done.11.rest_1_.rest_5_ = f32[1024,128]{1,0:T(8,128)S(1)} collective-permute-done((f32[1024,128]{1,0:T(8,128)S(1)}, f32[1024,128]{1,0:T(8,128)S(1)}, u32[]{:S(2)}, u32[]{:S(2)}) %collective-permute-start.11) | collective-permute-done | bytes 524320 | tf_op jit(solution)/shard_map/ppermute | solution.py:454
  87.6 3.3 %collective-permute-done.13.rest_3_.rest_9_ = f32[1024,128]{1,0:T(8,128)S(1)} collective-permute-done((f32[1024,128]{1,0:T(8,128)S(1)}, f32[1024,128]{1,0:T(8,128)S(1)}, u32[]{:S(2)}, u32[]{:S(2)}) %collective-permute-start.13) | collective-permute-done | bytes 524320 | tf_op jit(solution)/shard_map/ppermute | solution.py:459
  90.9 2.0 %gram_far.1 = f32[128,640]{1,0:T(8,128)S(1)} custom-call(f32[128,256]{1,0:T(8,128)S(1)} %get-tuple-element.11.near_ref, bf16[4,256,1024]{2,1,0:T(8,128)(2,1)S(1)} %get-tuple-element.12.lhs_ref, f32[1024,128]{1,0:T(8,128)S(1)} %collective-permute-done.10.rest_0_.rest_4_, f32[1024,128]{1,0:T(8,128)S(1)} %collective-permute-done.11.rest_1_.rest_5_, ...), custom_call_target="tpu_custom_call" | custom-call | flops 805306368 | bytes 3145728 | tf_op jit(solution)/shard_map/gram_far/pallas_call | solution.py:264
  93.0 13.9 %all_to_all.10.parts_ref = f32[16,8,640]{2,1,0:T(8,128)S(1)} all-to-all(f32[16,8,640]{2,1,0:T(8,128)S(1)} %bitcast.18), channel_id=1, replica_groups=mesh['row'=16,'vec'=8] {'row'}, dimensions={0} | all-to-all | bytes 655360 | tf_op jit(solution)/shard_map/all_to_all | solution.py:494
  106.9 1.2 total.1
  108.1 5.8 %all-to-all-start.1 = ((f32[64,8,640]{2,1,0:T(8,128)}), f32[64,8,640]{2,1,0:T(8,128)S(1)}, u32[]{:S(2)}, u32[]{:S(2)}) async-start(f32[64,8,640]{2,1,0:T(8,128)} %total.1), calls=%async_computation.1 | async-start | bytes 2621440 | tf_op jit(solution)/shard_map/all_to_all | solution.py:503
  113.9 1.8 collective-permute-start.15
  115.8 17.4 %all-to-all-done.1 = f32[64,8,640]{2,1,0:T(8,128)S(1)} async-done(((f32[64,8,640]{2,1,0:T(8,128)}), f32[64,8,640]{2,1,0:T(8,128)S(1)}, u32[]{:S(2)}, u32[]{:S(2)}) %all-to-all-start.1) | async-done | bytes 1310752 | tf_op jit(solution)/shard_map/all_to_all | solution.py:503
  133.2 3.2 %collective-permute-start.14 = (f32[16,4,8,640]{3,2,1,0:T(8,128)S(1)}, f32[16,4,8,640]{3,2,1,0:T(8,128)}, u32[]{:S(2)}, u32[]{:S(2)}) collective-permute-start(f32[16,4,8,640]{3,2,1,0:T(8,128)S(1)} %bitcast.19), channel_id=1, source_target_pairs={{0,1},{1,0},{2,3},{3,2},{4,5},{5,4},{6,7},{7,6},{8,9},{9,8},{10,11... | collective-permute-start | bytes 3932168 | tf_op jit(solution)/shard_map/ppermute | solution.py:464
  136.3 0.5 collective-permute-start.18
  136.8 0.4 collective-permute-start.21
  137.2 1.1 collective-permute-start.22
  138.3 1.4 collective-permute-done.17.rest_6_
  139.7 0.8 copy-done.5
  140.5 0.4 collective-permute-start.19
  140.9 0.8 copy-done.7
  141.8 8.6 %collective-permute-done.21.rest_12_ = f32[1024,128]{1,0:T(8,128)} collective-permute-done((f32[1024,128]{1,0:T(8,128)S(1)}, f32[1024,128]{1,0:T(8,128)}, u32[]{:S(2)}, u32[]{:S(2)}) %collective-permute-start.21) | collective-permute-done | bytes 524320 | tf_op jit(solution)/shard_map/ppermute | solution.py:454
  150.4 0.9 collective-permute-start.23
  151.3 1.3 collective-permute-done.22.rest_13_
  152.6 0.3 collective-permute-start.24
  152.9 0.3 collective-permute-done.23.rest_14_
  153.2 1.7 collective-permute-done.24.rest_15_
  154.8 1.0 copy-done.2
  155.9 1.0 copy-done.4
  156.9 1.0 copy-done.6
  158.0 1.0 copy-done.8
  159.0 20.1 %finish.1 = f32[2048,128]{1,0:T(8,128)} custom-call(s32[1]{0:T(128)} %bitcast.y_ref, f32[16,4,8,640]{3,2,1,0:T(8,128)S(1)} %bitcast.20, f32[16,4,8,640]{3,2,1,0:T(8,128)} %collective-permute-done.14.gb_ref, f32[1024,128]{1,0:T(8,128)S(1)} %bitcast.11, f32[1024,128]{1,0:T(8,128)S(1)} %bitcast.17, f32[1024,128]{1,0:T(8,128)} %collective-permute-done.15.rest_2_, ...), custom_call_target="tpu_custom_call" | custom-call | flops 9663676416 | bytes 9437184 | tf_op jit(solution)/shard_map/finish/pallas_call | solution.py:414
  (36 shorter events, 0.7 us)
Async XLA Ops:
  0.0 1.2 copy-start
  1.8 20.3 %collective-permute-start = (f32[8,128,128]{2,1,0:T(8,128)S(1)}, f32[8,128,128]{2,1,0:T(8,128)S(1)}, u32[]{:S(2)}, u32[]{:S(2)}) collective-permute-start(f32[8,128,128]{2,1,0:T(8,128)S(1)} %get-tuple-element.9.own_ref.rest_0_), channel_id=1, source_target_pairs={{120,0},{0,8},{8,16},{16,24},{24,32},{32,40},{40,48},{48,56},{56,6... | collective-permute-start | bytes 1572872 | tf_op jit(solution)/shard_map/ppermute | solution.py:451
  3.9 18.2 %collective-permute-start.1 = (f32[8,128,128]{2,1,0:T(8,128)S(1)}, f32[8,128,128]{2,1,0:T(8,128)S(1)}, u32[]{:S(2)}, u32[]{:S(2)}) collective-permute-start(f32[8,128,128]{2,1,0:T(8,128)S(1)} %get-tuple-element.9.own_ref.rest_0_), channel_id=1, source_target_pairs={{8,0},{16,8},{24,16},{32,24},{40,32},{48,40},{56,48},{64,56},{72,6... | collective-permute-start | bytes 1572872 | tf_op jit(solution)/shard_map/ppermute | solution.py:451
  8.7 23.8 %collective-permute-start.4 = (f32[8,128,128]{2,1,0:T(8,128)S(1)}, f32[8,128,128]{2,1,0:T(8,128)S(1)}, u32[]{:S(2)}, u32[]{:S(2)}) collective-permute-start(f32[8,128,128]{2,1,0:T(8,128)S(1)} %get-tuple-element.10.own_ref.rest_0_), channel_id=1, source_target_pairs={{120,0},{0,8},{8,16},{16,24},{24,32},{32,40},{40,48},{48,56},{56,6... | collective-permute-start | bytes 1572872 | tf_op jit(solution)/shard_map/ppermute | solution.py:451
  8.7 23.8 %collective-permute-start.5 = (f32[8,128,128]{2,1,0:T(8,128)S(1)}, f32[8,128,128]{2,1,0:T(8,128)S(1)}, u32[]{:S(2)}, u32[]{:S(2)}) collective-permute-start(f32[8,128,128]{2,1,0:T(8,128)S(1)} %get-tuple-element.10.own_ref.rest_0_), channel_id=1, source_target_pairs={{8,0},{16,8},{24,16},{32,24},{40,32},{48,40},{56,48},{64,56},{72,6... | collective-permute-start | bytes 1572872 | tf_op jit(solution)/shard_map/ppermute | solution.py:451
  27.6 15.4 %collective-permute-start.2 = (f32[8,128,128]{2,1,0:T(8,128)S(1)}, f32[8,128,128]{2,1,0:T(8,128)S(1)}, u32[]{:S(2)}, u32[]{:S(2)}) collective-permute-start(f32[8,128,128]{2,1,0:T(8,128)S(1)} %field.4.own_ref), channel_id=1, source_target_pairs={{120,0},{0,8},{8,16},{16,24},{24,32},{32,40},{40,48},{48,56},{56,6... | collective-permute-start | bytes 1572872 | tf_op jit(solution)/shard_map/ppermute | solution.py:451
  27.7 15.3 %collective-permute-start.3 = (f32[8,128,128]{2,1,0:T(8,128)S(1)}, f32[8,128,128]{2,1,0:T(8,128)S(1)}, u32[]{:S(2)}, u32[]{:S(2)}) collective-permute-start(f32[8,128,128]{2,1,0:T(8,128)S(1)} %field.4.own_ref), channel_id=1, source_target_pairs={{8,0},{16,8},{24,16},{32,24},{40,32},{48,40},{56,48},{64,56},{72,6... | collective-permute-start | bytes 1572872 | tf_op jit(solution)/shard_map/ppermute | solution.py:451
  38.1 16.4 %collective-permute-start.6 = (f32[8,128,128]{2,1,0:T(8,128)S(1)}, f32[8,128,128]{2,1,0:T(8,128)S(1)}, u32[]{:S(2)}, u32[]{:S(2)}) collective-permute-start(f32[8,128,128]{2,1,0:T(8,128)S(1)} %field.6.own_ref), channel_id=1, source_target_pairs={{120,0},{0,8},{8,16},{16,24},{24,32},{32,40},{40,48},{48,56},{56,6... | collective-permute-start | bytes 1572872 | tf_op jit(solution)/shard_map/ppermute | solution.py:451
  38.2 16.3 %collective-permute-start.7 = (f32[8,128,128]{2,1,0:T(8,128)S(1)}, f32[8,128,128]{2,1,0:T(8,128)S(1)}, u32[]{:S(2)}, u32[]{:S(2)}) collective-permute-start(f32[8,128,128]{2,1,0:T(8,128)S(1)} %field.6.own_ref), channel_id=1, source_target_pairs={{8,0},{16,8},{24,16},{32,24},{40,32},{48,40},{56,48},{64,56},{72,6... | collective-permute-start | bytes 1572872 | tf_op jit(solution)/shard_map/ppermute | solution.py:451
  48.6 18.1 %collective-permute-start.8 = (f32[1024,128]{1,0:T(8,128)S(1)}, f32[1024,128]{1,0:T(8,128)S(1)}, u32[]{:S(2)}, u32[]{:S(2)}) collective-permute-start(f32[1024,128]{1,0:T(8,128)S(1)} %bitcast.6), channel_id=1, source_target_pairs={{0,1},{1,0},{2,3},{3,2},{4,5},{5,4},{6,7},{7,6},{8,9},{9,8},{10,11... | collective-permute-start | bytes 1572872 | tf_op jit(solution)/shard_map/ppermute | solution.py:464
  60.1 6.6 %collective-permute-start.9 = (f32[1024,128]{1,0:T(8,128)S(1)}, f32[1024,128]{1,0:T(8,128)S(1)}, u32[]{:S(2)}, u32[]{:S(2)}) collective-permute-start(f32[1024,128]{1,0:T(8,128)S(1)} %bitcast.12), channel_id=1, source_target_pairs={{0,1},{1,0},{2,3},{3,2},{4,5},{5,4},{6,7},{7,6},{8,9},{9,8},{10,11... | collective-permute-start | bytes 1572872 | tf_op jit(solution)/shard_map/ppermute | solution.py:464
  62.5 13.9 %collective-permute-start.10 = (f32[1024,128]{1,0:T(8,128)S(1)}, f32[1024,128]{1,0:T(8,128)S(1)}, u32[]{:S(2)}, u32[]{:S(2)}) collective-permute-start(f32[1024,128]{1,0:T(8,128)S(1)} %bitcast.7), channel_id=1, source_target_pairs={{2,0},{3,1},{4,2},{5,3},{6,4},{7,5},{0,6},{1,7},{10,8},{11,9},{12,... | collective-permute-start | bytes 1572872 | tf_op jit(solution)/shard_map/ppermute | solution.py:454
  65.2 22.4 %collective-permute-start.11 = (f32[1024,128]{1,0:T(8,128)S(1)}, f32[1024,128]{1,0:T(8,128)S(1)}, u32[]{:S(2)}, u32[]{:S(2)}) collective-permute-start(f32[1024,128]{1,0:T(8,128)S(1)} %bitcast.13), channel_id=1, source_target_pairs={{2,0},{3,1},{4,2},{5,3},{6,4},{7,5},{0,6},{1,7},{10,8},{11,9},{12,... | collective-permute-start | bytes 1572872 | tf_op jit(solution)/shard_map/ppermute | solution.py:454
  65.7 22.0 %collective-permute-start.12 = (f32[1024,128]{1,0:T(8,128)S(1)}, f32[1024,128]{1,0:T(8,128)S(1)}, u32[]{:S(2)}, u32[]{:S(2)}) collective-permute-start(f32[1024,128]{1,0:T(8,128)S(1)} %bitcast.8), channel_id=1, source_target_pairs={{6,0},{7,1},{0,2},{1,3},{3,4},{2,5},{5,6},{4,7},{14,8},{15,9},{8,1... | collective-permute-start | bytes 1572872 | tf_op jit(solution)/shard_map/ppermute | solution.py:459
  66.7 24.3 %collective-permute-start.13 = (f32[1024,128]{1,0:T(8,128)S(1)}, f32[1024,128]{1,0:T(8,128)S(1)}, u32[]{:S(2)}, u32[]{:S(2)}) collective-permute-start(f32[1024,128]{1,0:T(8,128)S(1)} %bitcast.14), channel_id=1, source_target_pairs={{6,0},{7,1},{0,2},{1,3},{3,4},{2,5},{5,6},{4,7},{14,8},{15,9},{8,1... | collective-permute-start | bytes 1572872 | tf_op jit(solution)/shard_map/ppermute | solution.py:459
  87.6 5.3 %copy-start.1 = (f32[1024,128]{1,0:T(8,128)}, f32[1024,128]{1,0:T(8,128)S(1)}, u32[]{:S(2)}) copy-start(f32[1024,128]{1,0:T(8,128)S(1)} %collective-permute-done.12.rest_2_.rest_8_) | copy-start | bytes 1572868
  90.9 2.0 %copy-start.3 = (f32[1024,128]{1,0:T(8,128)}, f32[1024,128]{1,0:T(8,128)S(1)}, u32[]{:S(2)}) copy-start(f32[1024,128]{1,0:T(8,128)S(1)} %collective-permute-done.13.rest_3_.rest_9_) | copy-start | bytes 1572868
  108.1 25.1 %all-to-all-start.1 = ((f32[64,8,640]{2,1,0:T(8,128)}), f32[64,8,640]{2,1,0:T(8,128)S(1)}, u32[]{:S(2)}, u32[]{:S(2)}) async-start(f32[64,8,640]{2,1,0:T(8,128)} %total.1), calls=%async_computation.1 | async-start | bytes 2621440 | tf_op jit(solution)/shard_map/all_to_all | solution.py:503
  113.9 22.9 %collective-permute-start.15 = (f32[1024,128]{1,0:T(8,128)S(1)}, f32[1024,128]{1,0:T(8,128)}, u32[]{:S(2)}, u32[]{:S(2)}) collective-permute-start(f32[1024,128]{1,0:T(8,128)S(1)} %bitcast.10), channel_id=1, source_target_pairs={{0,1},{1,0},{2,3},{3,2},{4,5},{5,4},{6,7},{7,6},{8,9},{9,8},{10,11... | collective-permute-start | bytes 1572872 | tf_op jit(solution)/shard_map/ppermute | solution.py:464
  115.7 21.5 %collective-permute-start.16 = (f32[1024,128]{1,0:T(8,128)S(1)}, f32[1024,128]{1,0:T(8,128)}, u32[]{:S(2)}, u32[]{:S(2)}) collective-permute-start(f32[1024,128]{1,0:T(8,128)S(1)} %bitcast.16), channel_id=1, source_target_pairs={{0,1},{1,0},{2,3},{3,2},{4,5},{5,4},{6,7},{7,6},{8,9},{9,8},{10,11... | collective-permute-start | bytes 1572872 | tf_op jit(solution)/shard_map/ppermute | solution.py:464
  133.2 21.7 %collective-permute-start.14 = (f32[16,4,8,640]{3,2,1,0:T(8,128)S(1)}, f32[16,4,8,640]{3,2,1,0:T(8,128)}, u32[]{:S(2)}, u32[]{:S(2)}) collective-permute-start(f32[16,4,8,640]{3,2,1,0:T(8,128)S(1)} %bitcast.19), channel_id=1, source_target_pairs={{0,1},{1,0},{2,3},{3,2},{4,5},{5,4},{6,7},{7,6},{8,9},{9,8},{10,11... | collective-permute-start | bytes 3932168 | tf_op jit(solution)/shard_map/ppermute | solution.py:464
  136.3 3.4 %collective-permute-start.17 = (f32[1024,128]{1,0:T(8,128)S(1)}, f32[1024,128]{1,0:T(8,128)S(1)}, u32[]{:S(2)}, u32[]{:S(2)}) collective-permute-start(f32[1024,128]{1,0:T(8,128)S(1)} %collective-permute-done.10.rest_0_.rest_4_), channel_id=1, source_target_pairs={{0,1},{1,0},{2,3},{3,2},{4,5},{5,4},{6,7},{7,6},{8,9},{9,8},{10,11... | collective-permute-start | bytes 1572872 | tf_op jit(solution)/shard_map/ppermute | solution.py:464
  136.3 4.6 %collective-permute-start.18 = (f32[1024,128]{1,0:T(8,128)S(1)}, f32[1024,128]{1,0:T(8,128)S(1)}, u32[]{:S(2)}, u32[]{:S(2)}) collective-permute-start(f32[1024,128]{1,0:T(8,128)S(1)} %collective-permute-done.11.rest_1_.rest_5_), channel_id=1, source_target_pairs={{0,1},{1,0},{2,3},{3,2},{4,5},{5,4},{6,7},{7,6},{8,9},{9,8},{10,11... | collective-permute-start | bytes 1572872 | tf_op jit(solution)/shard_map/ppermute | solution.py:464
  136.8 13.6 %collective-permute-start.21 = (f32[1024,128]{1,0:T(8,128)S(1)}, f32[1024,128]{1,0:T(8,128)}, u32[]{:S(2)}, u32[]{:S(2)}) collective-permute-start(f32[1024,128]{1,0:T(8,128)S(1)} %collective-permute-done.10.rest_0_.rest_4_), channel_id=1, source_target_pairs={{2,0},{3,1},{4,2},{5,3},{6,4},{7,5},{0,6},{1,7},{10,8},{11,9},{12,... | collective-permute-start | bytes 1572872 | tf_op jit(solution)/shard_map/ppermute | solution.py:454
  137.2 15.3 %collective-permute-start.22 = (f32[1024,128]{1,0:T(8,128)}, f32[1024,128]{1,0:T(8,128)}, u32[]{:S(2)}, u32[]{:S(2)}) collective-permute-start(f32[1024,128]{1,0:T(8,128)} %copy-done.3), channel_id=1, source_target_pairs={{7,0},{6,1},{0,2},{1,3},{2,4},{3,5},{5,6},{4,7},{15,8},{14,9},{8,1... | collective-permute-start | bytes 1572872 | tf_op jit(solution)/shard_map/ppermute | solution.py:468
  139.7 0.8 copy-start.5
  140.5 12.3 %collective-permute-start.19 = (f32[1024,128]{1,0:T(8,128)}, f32[1024,128]{1,0:T(8,128)}, u32[]{:S(2)}, u32[]{:S(2)}) collective-permute-start(f32[1024,128]{1,0:T(8,128)} %copy-done.1), channel_id=1, source_target_pairs={{0,1},{1,0},{2,3},{3,2},{4,5},{5,4},{6,7},{7,6},{8,9},{9,8},{10,11... | collective-permute-start | bytes 1572872 | tf_op jit(solution)/shard_map/ppermute | solution.py:464
  140.9 0.8 copy-start.7
  141.7 11.2 %collective-permute-start.20 = (f32[1024,128]{1,0:T(8,128)}, f32[1024,128]{1,0:T(8,128)}, u32[]{:S(2)}, u32[]{:S(2)}) collective-permute-start(f32[1024,128]{1,0:T(8,128)} %copy-done.3), channel_id=1, source_target_pairs={{0,1},{1,0},{2,3},{3,2},{4,5},{5,4},{6,7},{7,6},{8,9},{9,8},{10,11... | collective-permute-start | bytes 1572872 | tf_op jit(solution)/shard_map/ppermute | solution.py:464
  150.4 2.7 %collective-permute-start.23 = (f32[1024,128]{1,0:T(8,128)}, f32[1024,128]{1,0:T(8,128)}, u32[]{:S(2)}, u32[]{:S(2)}) collective-permute-start(f32[1024,128]{1,0:T(8,128)} %collective-permute-done.21.rest_12_), channel_id=1, source_target_pairs={{0,1},{1,0},{2,3},{3,2},{4,5},{5,4},{6,7},{7,6},{8,9},{9,8},{10,11... | collective-permute-start | bytes 1572872 | tf_op jit(solution)/shard_map/ppermute | solution.py:464
  152.6 2.3 %collective-permute-start.24 = (f32[1024,128]{1,0:T(8,128)}, f32[1024,128]{1,0:T(8,128)}, u32[]{:S(2)}, u32[]{:S(2)}) collective-permute-start(f32[1024,128]{1,0:T(8,128)} %collective-permute-done.22.rest_13_), channel_id=1, source_target_pairs={{0,1},{1,0},{2,3},{3,2},{4,5},{5,4},{6,7},{7,6},{8,9},{9,8},{10,11... | collective-permute-start | bytes 1572872 | tf_op jit(solution)/shard_map/ppermute | solution.py:464
  154.8 1.0 copy-start.2
  155.9 1.0 copy-start.4
  156.9 1.0 copy-start.6
  158.0 1.0 copy-start.8
